TPU v7x, 32 devices: a whole 2x2x4 slice. The times are simulated.
32 devices in a mesh: comp: 2 (over x), gy: 4 (over y, core), gx: 4 (over z).
Axes of the slice: x: 2, y: 2, z: 4, core: 2. Of those that a mesh axis runs over, the one named last changes fastest.
Arguments:
- state: float32 [2, 8, 512, 512], P('comp', None, 'gy', 'gx'), may hold values from -6 to 6
- target: float32 [2, 8, 512, 512], P('comp', None, 'gy', 'gx'), may hold values from -2.5 to 0.5
- land_mask: int32 [2, 512, 512], P('comp', 'gy', 'gx'), may hold values 0 or 1
- diffusivity: float32 [2, 8], replicated, may hold values from 0.03 to 0.24
- coupling: float32 [2, 8, 4], replicated, may hold values from -3 to 3
- w_in: bfloat16 [16, 256], replicated, may hold values from -1.5 to 1.5
- b_in: float32 [256], replicated, may hold values from -3 to 3
- w_mid: bfloat16 [256, 256], replicated, may hold values from -0.375 to 0.375
- b_mid: float32 [256], replicated, may hold values from -3 to 3
- w_out: bfloat16 [256, 4], replicated, may hold values from -0.375 to 0.375
- b_out: float32 [4], replicated, may hold values from -3 to 3
- remap_weight: bfloat16 [2, 4, 4, 16, 4, 128, 128], P('comp', 'gy', 'gx'), may hold values from -0.5 to 0.5
- remap_source: int32 [2, 4, 4, 16, 4], P('comp', 'gy', 'gx'), may hold values from 0 to 127
- remap_target: int32 [2, 4, 4, 16, 4], P('comp', 'gy', 'gx'), may hold values from 0 to 127
- remap_count: int32 [2, 4, 4, 16], P('comp', 'gy', 'gx'), may hold values from 0 to 4, as said below
Outputs:
- new_state: float32 [2, 8, 512, 512], P('comp', None, 'gy', 'gx')
- state_adjoint: float32 [2, 8, 512, 512], P('comp', None, 'gy', 'gx')
- grad_w_in: float32 [16, 256], replicated
- grad_b_in: float32 [256], replicated
- grad_w_mid: float32 [256, 256], replicated
- grad_b_mid: float32 [256], replicated
- grad_w_out: float32 [256, 4], replicated
- grad_b_out: float32 [4], replicated
Inputs may be any that keep to these rules, and one draw needn't show every extreme that they name: remap_count[c, i, j, q] leading slots of the pair are in use, the rest are padding. A pair has slots in use exactly where receiving tile q lies within 2 tile rows of i and in a tile column within 2 of j (periodic), or, for a sender in the top tile row, where q lies in the top tile row within 1 column (periodic) of column 3 - j; such pairs use 1 slot or more; for each component one receiving tile has all 4 slots in use from every such sending tile.
All inputs are finite; a program needn't handle non-finite values. No bound on the sum of `land_mask` on one device may be relied on, other than what follows from the above.
Results may differ from a plain program's by a relative error of at most 0.0037.
Values may be sent and summed in bfloat16 or wider, within the bound.
No kernel may reach another device: no remote copies, remote signals or barrier semaphores. Data moves between devices by JAX's collectives and lax.ppermute only.
A program may use at most 64 MiB of HBM per device.

v0:
```python
import math

import jax
import jax.numpy as jnp
from jax import lax
from jax.sharding import PartitionSpec as P

PRECISE = lax.Precision.HIGHEST


def extended(cells, sides, width, closed):
    for axis, dim in sides:
        count = lax.axis_size(axis)
        ends = count if closed else count - 1
        head = lax.slice_in_dim(cells, 0, width, axis=dim)
        tail = lax.slice_in_dim(cells, cells.shape[dim] - width, cells.shape[dim], axis=dim)
        cells = jnp.concatenate(
            [
                lax.ppermute(tail, axis, [(i, (i + 1) % count) for i in range(ends)]),
                cells,
                lax.ppermute(head, axis, [((i + 1) % count, i) for i in range(ends)]),
            ],
            axis=dim,
        )
    return cells


def partner(block, axis, stride):
    count = lax.axis_size(axis)
    route = []
    for low in range(count):
        high = low | 1 << stride
        if high != low and high < count:
            route += [(low, high), (high, low)]
    return lax.ppermute(block, axis, route)


def silu_slope(preact):
    sigmoid_value = jax.nn.sigmoid(preact)
    return sigmoid_value * (1.0 + preact * (1.0 - sigmoid_value))


def laplace(surface, on_fold):
    wide_field = extended(surface, (("gx", 2),), 1, True)
    tall_field = extended(surface, (("gy", 1),), 1, False)
    top_row = surface[:, -1, :]
    mirrored = top_row[:, ::-1]
    for bit_index in range(lax.axis_size("gx").bit_length() - 1):
        mirrored = partner(mirrored, "gx", bit_index)
    north_rows = tall_field[:, 2:, :]
    north_rows = north_rows.at[:, -1, :].add(jnp.where(on_fold, mirrored, 0.0))
    return (
        wide_field[:, :, 2:]
        + wide_field[:, :, :-2]
        + tall_field[:, :-2, :]
        + north_rows
        - 4.0 * surface
    )


def forward_route(outgoing):
    relayed = lax.all_to_all(outgoing, ("gy", "gx"), split_axis=0, concat_axis=0, tiled=True)
    arrived = partner(relayed, "comp", 0)
    return arrived


def return_route(outgoing):
    relayed = lax.all_to_all(outgoing, ("gy", "gx"), split_axis=0, concat_axis=0, tiled=True)
    arrived = partner(relayed, "comp", 0)
    return arrived


def shards(
    state,
    target,
    land_mask,
    diffusivity,
    coupling,
    w_in,
    b_in,
    w_mid,
    b_mid,
    w_out,
    b_out,
    remap_weight,
    remap_source,
    remap_target,
    remap_count,
):
    comp_index = lax.axis_index("comp")
    is_ocean = comp_index == 1
    on_fold = jnp.logical_and(is_ocean, lax.axis_index("gy") == lax.axis_size("gy") - 1)
    surface = state[0]
    channels, tile_rows, tile_width = surface.shape
    cell_count = tile_rows * tile_width
    peer_count = remap_source.shape[3]
    slot_count = remap_source.shape[4]
    pair_count = peer_count * slot_count
    wet_mask = land_mask[0].astype(jnp.float32).reshape(1, cell_count)
    diff_mask = jnp.where(is_ocean, wet_mask, 1.0)
    diffuse_rate = diffusivity[comp_index]
    couple = coupling[comp_index]
    rounded = surface.astype(jnp.bfloat16)
    source = remap_source[0, 0, 0].reshape(pair_count)
    kernels = remap_weight[0, 0, 0].reshape(pair_count, tile_width, tile_width)
    slot_index = lax.broadcasted_iota(jnp.int32, (peer_count, slot_count), 1)
    live_mask = (
        (slot_index < remap_count[0, 0, 0][:, None]).astype(jnp.float32).reshape(pair_count, 1, 1)
    )
    picked = rounded[:, source, :]
    outgoing = (
        jnp.einsum("cki,kij->kcj", picked, kernels, preferred_element_type=jnp.float32) * live_mask
    )
    arrived = forward_route(outgoing.reshape(peer_count, slot_count, channels, tile_width))
    laplacian = laplace(surface, on_fold).reshape(channels, cell_count)
    row_index = lax.broadcasted_iota(jnp.int32, (tile_rows, pair_count), 0)
    landing = (row_index == remap_target[0, 0, 0].reshape(1, pair_count)).astype(jnp.float32)
    remapped = jnp.einsum(
        "tk,kcj->ctj", landing, arrived.reshape(pair_count, channels, tile_width), precision=PRECISE
    )
    own_fields = rounded.reshape(channels, cell_count)
    other_fields = remapped.astype(jnp.bfloat16).reshape(channels, cell_count)
    features = jnp.concatenate(
        [
            jnp.where(is_ocean, other_fields, own_fields),
            jnp.where(is_ocean, own_fields, other_fields),
        ],
        axis=0,
    )
    current = surface.reshape(channels, cell_count)
    goal = target[0].reshape(channels, cell_count)
    block_size = math.gcd(cell_count, 2048)

    def advance(block_index, loop_state):
        new_fields, misfits, feature_cots, gradients = loop_state
        offset = block_index * block_size

        def take_block(array):
            return lax.dynamic_slice_in_dim(array, offset, block_size, 1)

        feature_block = take_block(features)
        wet_block = take_block(wet_mask)
        diff_block = take_block(diff_mask)
        pre_first = (
            jnp.einsum("fh,fn->hn", w_in, feature_block, preferred_element_type=jnp.float32)
            + b_in[:, None]
        )
        hidden_first = jax.nn.silu(pre_first).astype(jnp.bfloat16)
        pre_second = (
            jnp.einsum("hk,hn->kn", w_mid, hidden_first, preferred_element_type=jnp.float32)
            + b_mid[:, None]
        )
        hidden_second = jax.nn.silu(pre_second).astype(jnp.bfloat16)
        fluxes = (
            jnp.einsum("ho,hn->on", w_out, hidden_second, preferred_element_type=jnp.float32)
            + b_out[:, None]
        ) * wet_block
        updated = (
            take_block(current)
            + diffuse_rate[:, None] * diff_block * take_block(laplacian)
            + jnp.dot(couple, fluxes, precision=PRECISE)
        )
        misfit = updated - take_block(goal)
        flux_cot = (wet_block * jnp.dot(couple.T, misfit, precision=PRECISE)).astype(jnp.bfloat16)
        second_cot = (
            jnp.einsum("ho,on->hn", w_out, flux_cot, preferred_element_type=jnp.float32)
            * silu_slope(pre_second)
        ).astype(jnp.bfloat16)
        first_cot = (
            jnp.einsum("hk,kn->hn", w_mid, second_cot, preferred_element_type=jnp.float32)
            * silu_slope(pre_first)
        ).astype(jnp.bfloat16)
        feature_cot = jnp.einsum("fh,hn->fn", w_in, first_cot, preferred_element_type=jnp.float32)
        additions = (
            jnp.einsum("fn,hn->fh", feature_block, first_cot, preferred_element_type=jnp.float32),
            jnp.sum(first_cot.astype(jnp.float32), axis=1),
            jnp.einsum("hn,kn->hk", hidden_first, second_cot, preferred_element_type=jnp.float32),
            jnp.sum(second_cot.astype(jnp.float32), axis=1),
            jnp.einsum("hn,on->ho", hidden_second, flux_cot, preferred_element_type=jnp.float32),
            jnp.sum(flux_cot.astype(jnp.float32), axis=1),
        )
        new_fields = lax.dynamic_update_slice_in_dim(new_fields, updated, offset, 1)
        misfits = lax.dynamic_update_slice_in_dim(misfits, misfit, offset, 1)
        feature_cots = lax.dynamic_update_slice_in_dim(feature_cots, feature_cot, offset, 1)
        return (new_fields, misfits, feature_cots, jax.tree.map(jnp.add, gradients, additions))

    initial = (
        jnp.zeros((channels, cell_count), jnp.float32),
        jnp.zeros((channels, cell_count), jnp.float32),
        jnp.zeros((2 * channels, cell_count), jnp.float32),
        (
            jnp.zeros(w_in.shape, jnp.float32),
            jnp.zeros(b_in.shape, jnp.float32),
            jnp.zeros(w_mid.shape, jnp.float32),
            jnp.zeros(b_mid.shape, jnp.float32),
            jnp.zeros(w_out.shape, jnp.float32),
            jnp.zeros(b_out.shape, jnp.float32),
        ),
    )
    new_fields, misfits, feature_cots, gradients = lax.fori_loop(
        0, cell_count // block_size, advance, initial
    )
    back_lap = laplace((diff_mask * misfits).reshape(channels, tile_rows, tile_width), on_fold)
    own_cot = jnp.where(is_ocean, feature_cots[channels:], feature_cots[:channels]).reshape(
        channels, tile_rows, tile_width
    )
    other_cot = jnp.where(is_ocean, feature_cots[:channels], feature_cots[channels:]).reshape(
        channels, tile_rows, tile_width
    )
    going_back = jnp.einsum("tk,ctj->kcj", landing, other_cot, precision=PRECISE).astype(
        jnp.bfloat16
    )
    returned = return_route(going_back.reshape(peer_count, slot_count, channels, tile_width))
    spread = (
        jnp.einsum(
            "kcj,kij->kci",
            returned.reshape(pair_count, channels, tile_width),
            kernels,
            preferred_element_type=jnp.float32,
        )
        * live_mask
    )
    anchor = (row_index == source.reshape(1, pair_count)).astype(jnp.float32)
    remap_back = jnp.einsum("tk,kci->cti", anchor, spread, precision=PRECISE)
    adjoint_field = (
        misfits.reshape(channels, tile_rows, tile_width)
        + diffuse_rate[:, None, None] * back_lap
        + own_cot
        + remap_back
    )
    grad_first, bias_first, grad_second, bias_second, grad_third, bias_third = gradients
    grad_first, bias_first, grad_second, bias_second, grad_third, bias_third = lax.psum(
        (grad_first, bias_first, grad_second, bias_second, grad_third, bias_third),
        ("comp", "gy", "gx"),
    )
    scale = 1.0 / (cell_count * lax.axis_size("gy") * lax.axis_size("gx"))
    return (
        new_fields.reshape(1, channels, tile_rows, tile_width),
        adjoint_field.reshape(1, channels, tile_rows, tile_width),
        grad_first * scale,
        bias_first * scale,
        grad_second * scale,
        bias_second * scale,
        grad_third * scale,
        bias_third * scale,
    )


def solution(mesh):
    placed = (
        P("comp", None, "gy", "gx"),
        P("comp", None, "gy", "gx"),
        P("comp", "gy", "gx"),
        P(),
        P(),
        P(),
        P(),
        P(),
        P(),
        P(),
        P(),
        P("comp", "gy", "gx", None, None, None, None),
        P("comp", "gy", "gx", None, None),
        P("comp", "gy", "gx", None, None),
        P("comp", "gy", "gx", None),
    )
    return jax.shard_map(
        shards,
        mesh=mesh,
        in_specs=placed,
        out_specs=(
            P("comp", None, "gy", "gx"),
            P("comp", None, "gy", "gx"),
            P(),
            P(),
            P(),
            P(),
            P(),
            P(),
        ),
        check_vma=False,
    )
```

profile of v0, /device:TPU:0, one launch (start us, length us, event | category | flops | bytes accessed | tf_op | source)
XLA Modules:
  0.0 382.0 jit_solution(18036116100139440150)
XLA Ops:
  7.2 1.4 copy.120
  8.6 1.3 fusion.47
  10.0 3.1 collective-permute-start.4
  13.0 1.3 collective-permute-start.3
  14.3 3.8 %collective-permute-start.2 = (f32[8,1,128]{1,2,0:T(8,128)}, f32[8,1,128]{1,2,0:T(8,128)}, u32[]{:S(2)}, u32[]{:S(2)}) collective-permute-start(f32[8,1,128]{1,2,0:T(8,128)} %get-tuple-element.628), channel_id=1, source_target_pairs={{0,4},{4,8},{8,12},{1,5},{5,9},{9,13},{2,6},{6,10},{10,14},{3,7},{... | collective-permute-start | bytes 12296 | tf_op jit(solution)/shard_map/ppermute | solution.py:19
  18.1 2.5 collective-permute-start
  22.0 1.6 gather_fusion
  23.6 1.4 convolution_multiply_fusion.2
  25.0 6.2 %all-to-all-start = ((f32[16,4,8,128]{3,2,1,0:T(8,128)}), f32[16,4,8,128]{3,2,1,0:T(8,128)}, u32[]{:S(2)}, u32[]{:S(2)}) async-start(f32[16,4,8,128]{3,2,1,0:T(8,128)} %bitcast.7), calls=%async_computation | async-start | bytes 524288 | tf_op jit(solution)/shard_map/all_to_all | solution.py:62
  32.8 2.8 collective-permute-start.5
  35.6 2.2 pad_maximum_fusion.4
  37.8 3.1 collective-permute-done.5
  42.0 2.0 add.258
  44.0 2.7 scatter-add.6
  46.7 2.3 fusion.29
  49.0 1.2 copy.122
  50.3 1.6 collective-permute-start.6
  51.9 2.6 copy_bitcast_fusion.4
  54.5 3.9 %collective-permute-done.6 = f32[16,4,8,128]{3,2,1,0:T(8,128)S(1)} collective-permute-done((f32[16,4,8,128]{3,2,1,0:T(8,128)}, f32[16,4,8,128]{3,2,1,0:T(8,128)S(1)}, u32[]{:S(2)}, u32[]{:S(2)}) %collective-permute-start.6) | collective-permute-done | bytes 262176 | tf_op jit(solution)/shard_map/ppermute | solution.py:35
  62.6 104.6 %while.32 = (s32[]{:T(128)}, f32[8,16384]{1,0:T(8,128)}, f32[8,16384]{1,0:T(8,128)}, f32[16,16384]{1,0:T(8,128)}, f32[16,256]{1,0:T(8,128)S(1)}, /*index=5*/f32[...) while((s32[]{:T(128)}, f32[8,16384]{1,0:T(8,128)}, ...), condition=%wide.region_4.5_spmd.clone, body=%wide.region_0.4_spmd.clone.sunk | while | flops 890530304 | bytes 47954832 | solution.py:200
  63.7 2.4 multiply_convert_fusion.7
  66.5 1.8 fusion.115
  69.7 2.7 convert_reduce_fusion.7
  76.8 2.4 multiply_convert_fusion.7
  79.5 1.8 fusion.115
  82.8 2.7 convert_reduce_fusion.7
  89.9 2.4 multiply_convert_fusion.7
  92.6 1.8 fusion.115
  95.9 2.7 convert_reduce_fusion.7
  103.0 2.4 multiply_convert_fusion.7
  105.7 1.8 fusion.115
  108.9 2.7 convert_reduce_fusion.7
  116.0 2.4 multiply_convert_fusion.7
  118.8 1.8 fusion.115
  122.0 2.7 convert_reduce_fusion.7
  129.1 2.4 multiply_convert_fusion.7
  131.8 1.8 fusion.115
  135.1 2.7 convert_reduce_fusion.7
  142.2 2.4 multiply_convert_fusion.7
  144.9 1.8 fusion.115
  148.2 2.7 convert_reduce_fusion.7
  155.3 2.4 multiply_convert_fusion.7
  158.0 1.8 fusion.115
  161.3 2.7 convert_reduce_fusion.7
  168.7 1.4 fusion.45
  170.0 38.8 %all-reduce = (f32[16,256]{1,0:T(8,128)S(1)}, f32[256]{0:T(256)S(1)}, f32[256]{0:T(256)S(1)}, f32[256,4]{0,1:T(4,128)S(1)}, f32[4]{0:T(128)S(1)}) all-reduce(f32[16,256]{1,0:T(8,128)S(1)} %get-tuple-element.422, f32[256]{0:T(256)S(1)} %get-tuple-element.423, ...), channel_id=1, replica_groups=mesh['comp'=2,'gy'=4,'gx'=4] {'comp','gy','gx'}, use_global_device_ids=true, to_apply=%region_5.6 | all-reduce | flops 5636 | bytes 45088 | tf_op jit(solution)/shard_map/psum | solution.py:232
  211.8 1.8 collective-permute-start.11
  213.6 1.3 collective-permute-start.10
  214.9 3.8 %collective-permute-start.9 = (f32[8,1,128]{1,2,0:T(8,128)}, f32[8,1,128]{1,2,0:T(8,128)}, u32[]{:S(2)}, u32[]{:S(2)}) collective-permute-start(f32[8,1,128]{1,2,0:T(8,128)} %get-tuple-element.623), channel_id=1, source_target_pairs={{0,4},{4,8},{8,12},{1,5},{5,9},{9,13},{2,6},{6,10},{10,14},{3,7},{... | collective-permute-start | bytes 12296 | tf_op jit(solution)/shard_map/ppermute | solution.py:19
  218.7 2.3 collective-permute-start.7
  221.0 2.1 select_bitcast_fusion
  224.2 7.0 %all-to-all-start.1 = ((bf16[16,4,8,128]{3,1,2,0:T(4,128)(2,1)}), bf16[16,4,8,128]{3,1,2,0:T(4,128)(2,1)S(1)}, u32[]{:S(2)}, u32[]{:S(2)}) async-start(bf16[16,4,8,128]{3,1,2,0:T(4,128)(2,1)} %copy.141), calls=%async_computation.1 | async-start | bytes 262144 | tf_op jit(solution)/shard_map/all_to_all | solution.py:68
  231.4 1.9 copy.171
  233.3 2.0 copy.139
  236.3 2.0 copy.138
  238.3 1.9 copy.174
  240.3 2.9 collective-permute-start.12
  243.2 1.4 pad_maximum_fusion
  245.9 2.1 add.264
  247.9 2.2 scatter-add.9
  250.8 116.6 %all-reduce.3.cloned.1.call-done = f32[256,256]{1,0:T(8,128)} async-done(((f32[256,256]{1,0:T(8,128)}), f32[256,256]{1,0:T(8,128)}) %all-reduce.3.cloned.1.call-update) | async-done | bytes 262160 | tf_op jit(solution)/shard_map/psum | solution.py:232
  367.4 1.8 broadcast_multiply_fusion
  370.4 2.7 fusion.18
  373.1 2.0 copy.145
  (328 shorter events, 66.1 us)
Async XLA Ops:
  7.2 16.4 %copy-start = (bf16[1,1,1,16,4,128,128]{6,5,4,3,2,1,0:T(8,128)(2,1)S(1)}, bf16[1,1,1,16,4,128,128]{6,5,4,3,2,1,0:T(8,128)(2,1)}, u32[]{:S(2)}) copy-start(bf16[1,1,1,16,4,128,128]{6,5,4,3,2,1,0:T(8,128)(2,1)} %param.32) | copy-start | bytes 6291460
  7.2 14.5 %copy-start.16 = (s32[1,1,1,16,4]{3,4,2,1,0:T(4,128)S(1)}, s32[1,1,1,16,4]{3,4,2,1,0:T(4,128)}, u32[]{:S(2)}) copy-start(s32[1,1,1,16,4]{3,4,2,1,0:T(4,128)} %param.33) | copy-start | bytes 772
  7.2 14.6 %copy-start.19 = (s32[1,1,1,16]{3,2,1,0:T(1,128)S(1)}, s32[1,1,1,16]{3,2,1,0:T(1,128)}, u32[]{:S(2)}) copy-start(s32[1,1,1,16]{3,2,1,0:T(1,128)} %param.35) | copy-start | bytes 196
  10.0 22.8 %collective-permute-start.4 = (f32[8,128]{1,0:T(8,128)S(1)}, f32[8,128]{1,0:T(8,128)S(1)}, u32[]{:S(2)}, u32[]{:S(2)}) collective-permute-start(f32[8,128]{1,0:T(8,128)S(1)} %rev.6), channel_id=1, source_target_pairs={{0,1},{1,0},{2,3},{3,2},{4,5},{5,4},{6,7},{7,6},{8,9},{9,8},{10,11... | collective-permute-start | bytes 12296 | tf_op jit(solution)/shard_map/ppermute | solution.py:35
  13.0 22.6 %collective-permute-start.3 = (f32[8,1,128]{1,2,0:T(8,128)}, f32[8,1,128]{1,2,0:T(8,128)}, u32[]{:S(2)}, u32[]{:S(2)}) collective-permute-start(f32[8,1,128]{1,2,0:T(8,128)} %get-tuple-element.630), channel_id=1, source_target_pairs={{4,0},{8,4},{12,8},{5,1},{9,5},{13,9},{6,2},{10,6},{14,10},{7,3},{... | collective-permute-start | bytes 12296 | tf_op jit(solution)/shard_map/ppermute | solution.py:21
  14.3 32.4 %collective-permute-start.2 = (f32[8,1,128]{1,2,0:T(8,128)}, f32[8,1,128]{1,2,0:T(8,128)}, u32[]{:S(2)}, u32[]{:S(2)}) collective-permute-start(f32[8,1,128]{1,2,0:T(8,128)} %get-tuple-element.628), channel_id=1, source_target_pairs={{0,4},{4,8},{8,12},{1,5},{5,9},{9,13},{2,6},{6,10},{10,14},{3,7},{... | collective-permute-start | bytes 12296 | tf_op jit(solution)/shard_map/ppermute | solution.py:19
  18.1 28.6 %collective-permute-start = (f32[8,128,1]{1,2,0:T(1,128)S(1)}, f32[8,128,1]{1,2,0:T(1,128)S(1)}, u32[]{:S(2)}, u32[]{:S(2)}) collective-permute-start(f32[8,128,1]{1,2,0:T(1,128)S(1)} %get-tuple-element.626), channel_id=1, source_target_pairs={{1,0},{2,1},{3,2},{0,3},{5,4},{6,5},{7,6},{4,7},{9,8},{10,9},{11,1... | collective-permute-start | bytes 12296 | tf_op jit(solution)/shard_map/ppermute | solution.py:21
  20.7 26.1 %collective-permute-start.1 = (f32[8,128,1]{1,2,0:T(1,128)S(1)}, f32[8,128,1]{1,2,0:T(1,128)S(1)}, u32[]{:S(2)}, u32[]{:S(2)}) collective-permute-start(f32[8,128,1]{1,2,0:T(1,128)S(1)} %get-tuple-element.627), channel_id=1, source_target_pairs={{0,1},{1,2},{2,3},{3,0},{4,5},{5,6},{6,7},{7,4},{8,9},{9,10},{10,1... | collective-permute-start | bytes 12296 | tf_op jit(solution)/shard_map/ppermute | solution.py:19
  20.7 10.5 %copy-start.18 = (f32[2,8,4]{1,2,0:T(4,128)S(1)}, f32[2,8,4]{1,2,0:T(4,128)}, u32[]{:S(2)}) copy-start(f32[2,8,4]{1,2,0:T(4,128)} %param.25) | copy-start | bytes 772
  20.7 10.5 %copy-start.22 = (f32[2,8]{1,0:T(2,128)S(1)}, f32[2,8]{1,0:T(2,128)}, u32[]{:S(2)}) copy-start(f32[2,8]{1,0:T(2,128)} %param.24) | copy-start | bytes 196
  20.7 10.6 %copy-start.12 = (s32[1,128,128]{2,1,0:T(8,128)S(1)}, s32[1,128,128]{2,1,0:T(8,128)}, u32[]{:S(2)}) copy-start(s32[1,128,128]{2,1,0:T(8,128)} %param.23) | copy-start | bytes 196612
  20.7 10.7 %copy-start.3 = (f32[1,8,128,128]{3,2,1,0:T(8,128)S(1)}, f32[1,8,128,128]{3,2,1,0:T(8,128)}, u32[]{:S(2)}) copy-start(f32[1,8,128,128]{3,2,1,0:T(8,128)} %param.21) | copy-start | bytes 1572868
  23.6 9.0 %copy-start.17 = (s32[1,1,1,16,4]{3,4,2,1,0:T(4,128)S(1)}, s32[1,1,1,16,4]{3,4,2,1,0:T(4,128)}, u32[]{:S(2)}) copy-start(s32[1,1,1,16,4]{3,4,2,1,0:T(4,128)} %param.34) | copy-start | bytes 772
  25.0 25.3 %all-to-all-start = ((f32[16,4,8,128]{3,2,1,0:T(8,128)}), f32[16,4,8,128]{3,2,1,0:T(8,128)}, u32[]{:S(2)}, u32[]{:S(2)}) async-start(f32[16,4,8,128]{3,2,1,0:T(8,128)} %bitcast.7), calls=%async_computation | async-start | bytes 524288 | tf_op jit(solution)/shard_map/all_to_all | solution.py:62
  32.8 8.1 %collective-permute-start.5 = (f32[8,128]{1,0:T(8,128)S(1)}, f32[8,128]{1,0:T(8,128)S(1)}, u32[]{:S(2)}, u32[]{:S(2)}) collective-permute-start(f32[8,128]{1,0:T(8,128)S(1)} %collective-permute-done.4), channel_id=1, source_target_pairs={{0,2},{2,0},{1,3},{3,1},{4,6},{6,4},{5,7},{7,5},{8,10},{10,8},{9,1... | collective-permute-start | bytes 12296 | tf_op jit(solution)/shard_map/ppermute | solution.py:35
  50.3 8.1 %collective-permute-start.6 = (f32[16,4,8,128]{3,2,1,0:T(8,128)}, f32[16,4,8,128]{3,2,1,0:T(8,128)S(1)}, u32[]{:S(2)}, u32[]{:S(2)}) collective-permute-start(f32[16,4,8,128]{3,2,1,0:T(8,128)} %all-to-all-done), channel_id=1, source_target_pairs={{0,16},{16,0},{1,17},{17,1},{2,18},{18,2},{3,19},{19,3},{4,20},{20... | collective-permute-start | bytes 786440 | tf_op jit(solution)/shard_map/ppermute | solution.py:35
  59.3 3.3 copy-start.9
  59.3 3.3 copy-start.13
  59.3 3.3 copy-start.14
  59.3 3.3 copy-start.15
  59.4 3.2 copy-start.23
  63.1 2.9 copy-start.1
  69.7 2.7 copy-start.2
  69.7 2.7 copy-start.10
  73.4 2.0 copy-start.6
  76.2 2.9 copy-start.1
  82.8 2.7 copy-start.2
  82.8 2.7 copy-start.10
  86.5 2.0 copy-start.6
  89.3 2.9 copy-start.1
  95.9 2.7 copy-start.2
  95.9 2.7 copy-start.10
  99.5 2.0 copy-start.6
  102.4 2.9 copy-start.1
  108.9 2.7 copy-start.2
  108.9 2.7 copy-start.10
  112.6 2.0 copy-start.6
  115.5 2.9 copy-start.1
  122.0 2.7 copy-start.2
  122.0 2.7 copy-start.10
  125.7 2.0 copy-start.6
  128.5 2.9 copy-start.1
  135.1 2.7 copy-start.2
  135.1 2.7 copy-start.10
  138.8 2.0 copy-start.6
  141.6 2.9 copy-start.1
  148.2 2.7 copy-start.2
  148.2 2.7 copy-start.10
  151.8 2.0 copy-start.6
  154.7 2.9 copy-start.1
  161.2 2.7 copy-start.2
  161.2 2.7 copy-start.10
  211.8 28.5 %collective-permute-start.11 = (f32[8,128]{1,0:T(8,128)S(1)}, f32[8,128]{1,0:T(8,128)S(1)}, u32[]{:S(2)}, u32[]{:S(2)}) collective-permute-start(f32[8,128]{1,0:T(8,128)S(1)} %rev.7), channel_id=1, source_target_pairs={{0,1},{1,0},{2,3},{3,2},{4,5},{5,4},{6,7},{7,6},{8,9},{9,8},{10,11... | collective-permute-start | bytes 12296 | tf_op jit(solution)/shard_map/ppermute | solution.py:35
  213.6 29.6 %collective-permute-start.10 = (f32[8,1,128]{1,2,0:T(8,128)}, f32[8,1,128]{1,2,0:T(8,128)}, u32[]{:S(2)}, u32[]{:S(2)}) collective-permute-start(f32[8,1,128]{1,2,0:T(8,128)} %get-tuple-element.625), channel_id=1, source_target_pairs={{4,0},{8,4},{12,8},{5,1},{9,5},{13,9},{6,2},{10,6},{14,10},{7,3},{... | collective-permute-start | bytes 12296 | tf_op jit(solution)/shard_map/ppermute | solution.py:21
  214.9 155.4 %collective-permute-start.9 = (f32[8,1,128]{1,2,0:T(8,128)}, f32[8,1,128]{1,2,0:T(8,128)}, u32[]{:S(2)}, u32[]{:S(2)}) collective-permute-start(f32[8,1,128]{1,2,0:T(8,128)} %get-tuple-element.623), channel_id=1, source_target_pairs={{0,4},{4,8},{8,12},{1,5},{5,9},{9,13},{2,6},{6,10},{10,14},{3,7},{... | collective-permute-start | bytes 12296 | tf_op jit(solution)/shard_map/ppermute | solution.py:19
  218.7 151.6 %collective-permute-start.7 = (f32[8,128,1]{1,2,0:T(1,128)S(1)}, f32[8,128,1]{1,2,0:T(1,128)S(1)}, u32[]{:S(2)}, u32[]{:S(2)}) collective-permute-start(f32[8,128,1]{1,2,0:T(1,128)S(1)} %get-tuple-element.621), channel_id=1, source_target_pairs={{1,0},{2,1},{3,2},{0,3},{5,4},{6,5},{7,6},{4,7},{9,8},{10,9},{11,1... | collective-permute-start | bytes 12296 | tf_op jit(solution)/shard_map/ppermute | solution.py:21
  221.0 149.4 %collective-permute-start.8 = (f32[8,128,1]{1,2,0:T(1,128)S(1)}, f32[8,128,1]{1,2,0:T(1,128)S(1)}, u32[]{:S(2)}, u32[]{:S(2)}) collective-permute-start(f32[8,128,1]{1,2,0:T(1,128)S(1)} %get-tuple-element.622), channel_id=1, source_target_pairs={{0,1},{1,2},{2,3},{3,0},{4,5},{5,6},{6,7},{7,4},{8,9},{9,10},{10,1... | collective-permute-start | bytes 12296 | tf_op jit(solution)/shard_map/ppermute | solution.py:19
  223.1 12.3 %copy-start.4 = (f32[8,16384]{1,0:T(8,128)S(1)}, f32[8,16384]{1,0:T(8,128)}, u32[]{:S(2)}) copy-start(f32[8,16384]{1,0:T(8,128)} %get-tuple-element.420) | copy-start | bytes 1572868
  224.2 26.0 %all-to-all-start.1 = ((bf16[16,4,8,128]{3,1,2,0:T(4,128)(2,1)}), bf16[16,4,8,128]{3,1,2,0:T(4,128)(2,1)S(1)}, u32[]{:S(2)}, u32[]{:S(2)}) async-start(bf16[16,4,8,128]{3,1,2,0:T(4,128)(2,1)} %copy.141), calls=%async_computation.1 | async-start | bytes 262144 | tf_op jit(solution)/shard_map/all_to_all | solution.py:68
  231.2 136.2 %all-reduce.3.cloned.1.call-start = ((), (), s32[]{:S(2)}) async-start(), calls=%async_computation.2 | async-start | bytes 524288 | tf_op jit(solution)/shard_map/psum | solution.py:232
  240.3 4.6 %collective-permute-start.12 = (f32[8,128]{1,0:T(8,128)S(1)}, f32[8,128]{1,0:T(8,128)S(1)}, u32[]{:S(2)}, u32[]{:S(2)}) collective-permute-start(f32[8,128]{1,0:T(8,128)S(1)} %collective-permute-done.11), channel_id=1, source_target_pairs={{0,2},{2,0},{1,3},{3,1},{4,6},{6,4},{5,7},{7,5},{8,10},{10,8},{9,1... | collective-permute-start | bytes 12296 | tf_op jit(solution)/shard_map/ppermute | solution.py:35
  250.2 118.9 %collective-permute-start.13 = (bf16[16,4,8,128]{3,1,2,0:T(4,128)(2,1)S(1)}, bf16[16,4,8,128]{3,1,2,0:T(4,128)(2,1)S(1)}, u32[]{:S(2)}, u32[]{:S(2)}) collective-permute-start(bf16[16,4,8,128]{3,1,2,0:T(4,128)(2,1)S(1)} %all-to-all-done.1), channel_id=1, source_target_pairs={{0,16},{16,0},{1,17},{17,1},{2,18},{18,2},{3,19},{19,3},{4,20},{20... | collective-permute-start | bytes 393224 | tf_op jit(solution)/shard_map/ppermute | solution.py:35
  367.4 3.0 copy-start.7
  367.4 3.0 copy-start.8
  (33 other events, 32.2 us)
Sparse Core Ops, SparseCore 0:
  240.4 126.9 all-reduce.2
where the time goes:
time: 384 us; the launch traced here: 382 us
  waiting for transfers between devices  124 us (32%)
  matrix products  105 us (27%)
  starting transfers between devices  41.2 us (11%)
  local copies, waits for them, and re-layouts  38.9 us (10%)
  blocking collectives  38.8 us (10%)
  other arithmetic  18.7 us (5%)
  between operations  14.5 us (4%)
    psum x1, waiting for transfers between devices, shards(): lax.psum((grad_first, bias_first, grad_second, bias_second, grad_third, b...  117 us
    psum x1, blocking collectives, shards(): lax.psum((grad_first, bias_first, grad_second, bias_second, grad_third, b...  38.8 us
    dot_general x8, matrix products, advance(): jnp.einsum('ho,on->hn', w_out, flux_cot, preferred_element_type=jnp.float32)  21.6 us
    dot_general x8, matrix products, advance(): jnp.einsum('hk,hn->kn', w_mid, hidden_first, preferred_element_type=jnp.f...  18.9 us
    dot_general x8, matrix products, advance(): jnp.dot(couple, fluxes, precision=PRECISE)  14.6 us
    ppermute x6, starting transfers between devices, partner(): return lax.ppermute(block, axis, route)  12.7 us
    unnamed x41, local copies, waits for them, and re-layouts  9.63 us
    dot_general x8, matrix products, advance(): jnp.dot(couple.T, misfit, precision=PRECISE)  9.23 us
  transfers between devices with their start and end apart: 17, of which 4 were waited for; matrix products, arithmetic and copies ran while one was open for 11% of the time, Pallas kernels for 0%

commit v1 on v0

--- a/solution.py
+++ b/solution.py
@@ -229,10 +229,37 @@
         + remap_back
     )
     grad_first, bias_first, grad_second, bias_second, grad_third, bias_third = gradients
-    grad_first, bias_first, grad_second, bias_second, grad_third, bias_third = lax.psum(
-        (grad_first, bias_first, grad_second, bias_second, grad_third, bias_third),
-        ("comp", "gy", "gx"),
-    )
+    everywhere = ("comp", "gy", "gx")
+    device_count = math.prod(lax.axis_size(axis) for axis in everywhere)
+    packed = jnp.concatenate(
+        [
+            grad_first,
+            bias_first[None],
+            grad_second,
+            bias_second[None],
+            grad_third.T,
+            jnp.pad(bias_third, (0, w_in.shape[1] - bias_third.shape[0]))[None],
+        ],
+        axis=0,
+    )
+    total_rows = packed.shape[0]
+    share = -(-total_rows // device_count)
+    packed = jnp.pad(packed, ((0, share * device_count - total_rows), (0, 0)))
+    pieces = lax.all_to_all(
+        packed.reshape(device_count, share, -1), everywhere, 0, 0, tiled=True
+    )
+    summed = jnp.sum(pieces, axis=0, keepdims=True)
+    packed = lax.all_to_all(
+        jnp.broadcast_to(summed, pieces.shape), everywhere, 0, 0, tiled=True
+    ).reshape(share * device_count, -1)
+    inputs, hidden = w_in.shape
+    outputs = w_out.shape[1]
+    grad_first = packed[:inputs]
+    bias_first = packed[inputs]
+    grad_second = packed[inputs + 1 : inputs + 1 + hidden]
+    bias_second = packed[inputs + 1 + hidden]
+    grad_third = packed[inputs + 2 + hidden : inputs + 2 + hidden + outputs].T
+    bias_third = packed[inputs + 2 + hidden + outputs, :outputs]
     scale = 1.0 / (cell_count * lax.axis_size("gy") * lax.axis_size("gx"))
     return (
         new_fields.reshape(1, channels, tile_rows, tile_width),

time: 384 us -> 233 us (0.61)
  waiting for transfers between devices: 124 us -> 15.1 us
  blocking collectives: 38.8 us -> 0 us
  between operations: 14.5 us -> 1.2 us
  local copies, waits for them, and re-layouts: 38.9 us -> 44.7 us
  starting transfers between devices: 41.2 us -> 45.5 us
    psum x1 -> x0, waiting for transfers between devices: 117 us -> none  [shards(): lax.psum((grad_first, bias_first, grad_second, bias_second, grad_third, b...]
    psum x1 -> x0, blocking collectives: 38.8 us -> none  [shards(): lax.psum((grad_first, bias_first, grad_second, bias_second, grad_third, b...]
    all_to_all x0 -> x2, starting transfers between devices: none -> 7.12 us  [the longest x1 3.78 us: shards(): lax.all_to_all(jnp.broadcast_to(summed, pieces.shape), everywhere, 0, 0,...]
    all_to_all x1, waiting for transfers between devices: 0.01 us -> 5.16 us  [return_route(): lax.all_to_all(outgoing, ('gy', 'gx'), split_axis=0, concat_axis=0, tiled...]
  transfers between devices with their start and end apart: 17 -> 18, of which waited for: 4 -> 4; matrix products, arithmetic and copies ran while one was open for 11% -> 20% of each run, Pallas kernels for 0% -> 0%
where the time goes in v1:
time: 233 us; the launch traced here: 230 us
  matrix products  105 us (45%)
  starting transfers between devices  45.5 us (20%)
  local copies, waits for them, and re-layouts  44.7 us (19%)
  other arithmetic  17.2 us (7%)
  waiting for transfers between devices  15.1 us (6%)
    dot_general x8, matrix products, advance(): jnp.einsum('ho,on->hn', w_out, flux_cot, preferred_element_type=jnp.float32)  21.6 us
    dot_general x8, matrix products, advance(): jnp.einsum('hk,hn->kn', w_mid, hidden_first, preferred_element_type=jnp.f...  18.9 us
    dot_general x8, matrix products, advance(): jnp.dot(couple, fluxes, precision=PRECISE)  14.6 us
    ppermute x6, starting transfers between devices, partner(): return lax.ppermute(block, axis, route)  12.7 us
    unnamed x41, local copies, waits for them, and re-layouts  10.4 us
    dot_general x8, matrix products, advance(): jnp.dot(couple.T, misfit, precision=PRECISE)  9.23 us
    dot_general x8, matrix products, advance(): jnp.einsum('fh,hn->fn', w_in, first_cot, preferred_element_type=jnp.float32)  8.36 us
    ppermute x4, starting transfers between devices, extended(): lax.ppermute(tail, axis, [(i, (i + 1) % count) for i in range(ends)])  7.65 us
  transfers between devices with their start and end apart: 18, of which 4 were waited for; matrix products, arithmetic and copies ran while one was open for 20% of the time, Pallas kernels for 0%

profile of v1, /device:TPU:0, one launch (start us, length us, event | category | flops | bytes accessed | tf_op | source)
XLA Modules:
  0.0 229.5 jit_solution(4973544228846165503)
XLA Ops:
  0.7 1.4 copy.120
  2.1 1.3 fusion.49
  3.4 3.1 %collective-permute-start.4 = (f32[8,128]{1,0:T(8,128)S(1)}, f32[8,128]{1,0:T(8,128)S(1)}, u32[]{:S(2)}, u32[]{:S(2)}) collective-permute-start(f32[8,128]{1,0:T(8,128)S(1)} %rev.6), channel_id=1, source_target_pairs={{0,1},{1,0},{2,3},{3,2},{4,5},{5,4},{6,7},{7,6},{8,9},{9,8},{10,11... | collective-permute-start | bytes 12296 | tf_op jit(solution)/shard_map/ppermute | solution.py:35
  6.5 1.3 collective-permute-start.3
  7.8 3.8 %collective-permute-start.2 = (f32[8,1,128]{1,2,0:T(8,128)}, f32[8,1,128]{1,2,0:T(8,128)}, u32[]{:S(2)}, u32[]{:S(2)}) collective-permute-start(f32[8,1,128]{1,2,0:T(8,128)} %get-tuple-element.623), channel_id=1, source_target_pairs={{0,4},{4,8},{8,12},{1,5},{5,9},{9,13},{2,6},{6,10},{10,14},{3,7},{... | collective-permute-start | bytes 12296 | tf_op jit(solution)/shard_map/ppermute | solution.py:19
  11.6 2.5 %collective-permute-start = (f32[8,128,1]{1,2,0:T(1,128)S(1)}, f32[8,128,1]{1,2,0:T(1,128)S(1)}, u32[]{:S(2)}, u32[]{:S(2)}) collective-permute-start(f32[8,128,1]{1,2,0:T(1,128)S(1)} %get-tuple-element.621), channel_id=1, source_target_pairs={{1,0},{2,1},{3,2},{0,3},{5,4},{6,5},{7,6},{4,7},{9,8},{10,9},{11,1... | collective-permute-start | bytes 12296 | tf_op jit(solution)/shard_map/ppermute | solution.py:21
  15.5 1.6 gather_fusion
  17.1 1.3 convolution_multiply_fusion.2
  18.4 6.2 %all-to-all-start = ((f32[16,4,8,128]{3,2,1,0:T(8,128)}), f32[16,4,8,128]{3,2,1,0:T(8,128)}, u32[]{:S(2)}, u32[]{:S(2)}) async-start(f32[16,4,8,128]{3,2,1,0:T(8,128)} %bitcast.7), calls=%async_computation | async-start | bytes 524288 | tf_op jit(solution)/shard_map/all_to_all | solution.py:62
  26.3 2.8 %collective-permute-start.5 = (f32[8,128]{1,0:T(8,128)S(1)}, f32[8,128]{1,0:T(8,128)S(1)}, u32[]{:S(2)}, u32[]{:S(2)}) collective-permute-start(f32[8,128]{1,0:T(8,128)S(1)} %collective-permute-done.4), channel_id=1, source_target_pairs={{0,2},{2,0},{1,3},{3,1},{4,6},{6,4},{5,7},{7,5},{8,10},{10,8},{9,1... | collective-permute-start | bytes 12296 | tf_op jit(solution)/shard_map/ppermute | solution.py:35
  29.1 2.2 pad_maximum_fusion.4
  31.3 3.1 %collective-permute-done.5 = f32[8,128]{1,0:T(8,128)S(1)} collective-permute-done((f32[8,128]{1,0:T(8,128)S(1)}, f32[8,128]{1,0:T(8,128)S(1)}, u32[]{:S(2)}, u32[]{:S(2)}) %collective-permute-start.5) | collective-permute-done | bytes 4128 | tf_op jit(solution)/shard_map/ppermute | solution.py:35
  35.5 2.0 add.250
  37.5 2.7 %scatter-add.6 = f32[8,128,128]{1,2,0:T(8,128)} dynamic-update-slice(f32[8,128,128]{1,2,0:T(8,128)} %pad_maximum_fusion.4, f32[8,1,128]{1,2,0:T(8,128)} %add.250, s32[]{:T(128)} %constant.119.clone.1, s32[]{:T(128)} %constant.130.clone.1, s32[]{:T(128)} %constant.119.clone.1) | dynamic-update-slice | bytes 8196 | tf_op jit(solution)/shard_map/scatter-add | solution.py:51
  40.2 2.3 %fusion.29 = f32[8,128,128]{1,2,0:T(8,128)} fusion(f32[8,128,128]{1,2,0:T(8,128)} %scatter-add.6, f32[8,128,128]{1,2,0:T(8,128)S(1)} %bitcast.195, f32[8,1,128]{1,2,0:T(8,128)} %collective-permute-done.2, f32[8,128,1]{1,2,0:T(1,128)S(1)} %collective-permute-done.1, f32[8,128,1]{1,2,0:T(1,128)S(1)} %collective-permute-done), kind=kLoop, calls=%fused_computation.73 | loop fusion | flops 1048576 | bytes 1585152 | tf_op jit(solution)/shard_map/sub | solution.py:53
  43.8 1.6 collective-permute-start.6
  45.3 2.6 %copy_bitcast_fusion.4 = (f32[8,16384]{1,0:T(8,128)}, f32[8,16384]{1,0:T(8,128)}) fusion(f32[1,8,128,128]{3,2,1,0:T(8,128)} %param.22, f32[1,8,128,128]{3,2,1,0:T(8,128)S(1)} %bitcast.201), kind=kLoop, calls=%fused_computation.55 | loop fusion | bytes 2097152 | tf_op jit(solution)/shard_map/reshape;squeeze | solution.py:131
  48.0 3.9 %collective-permute-done.6 = f32[16,4,8,128]{3,2,1,0:T(8,128)S(1)} collective-permute-done((f32[16,4,8,128]{3,2,1,0:T(8,128)}, f32[16,4,8,128]{3,2,1,0:T(8,128)S(1)}, u32[]{:S(2)}, u32[]{:S(2)}) %collective-permute-start.6) | collective-permute-done | bytes 262176 | tf_op jit(solution)/shard_map/ppermute | solution.py:35
  56.0 104.6 %while.32 = (s32[]{:T(128)}, f32[8,16384]{1,0:T(8,128)}, f32[8,16384]{1,0:T(8,128)}, f32[16,16384]{1,0:T(8,128)}, f32[16,256]{1,0:T(8,128)S(1)}, /*index=5*/f32[...) while((s32[]{:T(128)}, f32[8,16384]{1,0:T(8,128)}, ...), condition=%wide.region_4.5_spmd.clone, body=%wide.region_0.4_spmd.clone.sunk | while | flops 890530304 | bytes 47954832 | solution.py:200
  57.2 2.4 %multiply_convert_fusion.7 = (bf16[256,2048]{0,1:T(8,128)(2,1)S(1)}, f32[256,2048]{0,1:T(8,128)}) fusion(f32[256]{0:T(256)S(1)} %get-tuple-element.875, bf16[256,256]{1,0:T(8,128)(2,1)S(1)} %copy-done.20, f32[256,2048]{0,1:T(8,128)S(1)} %fusion.115), kind=kOutput, calls=%fused_computation.21.clone.1 | convolution fusion | flops 274202624 | bytes 5374976 | tf_op jit(solution)/shard_map/while/body/eval_jaxpr/hk,hn->kn/dot_general | solution.py:150
  59.9 1.8 fusion.117
  63.1 2.7 %convert_reduce_fusion.7 = (f32[256]{0:T(256)S(1)}, bf16[256,2048]{0,1:T(8,128)(2,1)S(1)}) fusion(f32[256,2048]{0,1:T(8,128)} %get-tuple-element.793, bf16[2048,4]{0,1:T(4,128)(2,1)S(1)} %get-tuple-element.795, bf16[256,4]{0,1:T(4,128)(2,1)S(1)} %get-tuple-element.876), kind=kOutput, calls=%fused_computation.19.clone.1 | convolution fusion | flops 9961216 | bytes 3165184 | tf_op jit(solution)/shard_map/while/body/eval_jaxpr/ho,on->hn/dot_general | solution.py:166
  70.2 2.4 %multiply_convert_fusion.7 = (bf16[256,2048]{0,1:T(8,128)(2,1)S(1)}, f32[256,2048]{0,1:T(8,128)}) fusion(f32[256]{0:T(256)S(1)} %get-tuple-element.875, bf16[256,256]{1,0:T(8,128)(2,1)S(1)} %copy-done.20, f32[256,2048]{0,1:T(8,128)S(1)} %fusion.115), kind=kOutput, calls=%fused_computation.21.clone.1 | convolution fusion | flops 274202624 | bytes 5374976 | tf_op jit(solution)/shard_map/while/body/eval_jaxpr/hk,hn->kn/dot_general | solution.py:150
  73.0 1.8 fusion.117
  76.2 2.7 %convert_reduce_fusion.7 = (f32[256]{0:T(256)S(1)}, bf16[256,2048]{0,1:T(8,128)(2,1)S(1)}) fusion(f32[256,2048]{0,1:T(8,128)} %get-tuple-element.793, bf16[2048,4]{0,1:T(4,128)(2,1)S(1)} %get-tuple-element.795, bf16[256,4]{0,1:T(4,128)(2,1)S(1)} %get-tuple-element.876), kind=kOutput, calls=%fused_computation.19.clone.1 | convolution fusion | flops 9961216 | bytes 3165184 | tf_op jit(solution)/shard_map/while/body/eval_jaxpr/ho,on->hn/dot_general | solution.py:166
  83.3 2.4 %multiply_convert_fusion.7 = (bf16[256,2048]{0,1:T(8,128)(2,1)S(1)}, f32[256,2048]{0,1:T(8,128)}) fusion(f32[256]{0:T(256)S(1)} %get-tuple-element.875, bf16[256,256]{1,0:T(8,128)(2,1)S(1)} %copy-done.20, f32[256,2048]{0,1:T(8,128)S(1)} %fusion.115), kind=kOutput, calls=%fused_computation.21.clone.1 | convolution fusion | flops 274202624 | bytes 5374976 | tf_op jit(solution)/shard_map/while/body/eval_jaxpr/hk,hn->kn/dot_general | solution.py:150
  86.0 1.8 fusion.117
  89.3 2.7 %convert_reduce_fusion.7 = (f32[256]{0:T(256)S(1)}, bf16[256,2048]{0,1:T(8,128)(2,1)S(1)}) fusion(f32[256,2048]{0,1:T(8,128)} %get-tuple-element.793, bf16[2048,4]{0,1:T(4,128)(2,1)S(1)} %get-tuple-element.795, bf16[256,4]{0,1:T(4,128)(2,1)S(1)} %get-tuple-element.876), kind=kOutput, calls=%fused_computation.19.clone.1 | convolution fusion | flops 9961216 | bytes 3165184 | tf_op jit(solution)/shard_map/while/body/eval_jaxpr/ho,on->hn/dot_general | solution.py:166
  96.4 2.4 %multiply_convert_fusion.7 = (bf16[256,2048]{0,1:T(8,128)(2,1)S(1)}, f32[256,2048]{0,1:T(8,128)}) fusion(f32[256]{0:T(256)S(1)} %get-tuple-element.875, bf16[256,256]{1,0:T(8,128)(2,1)S(1)} %copy-done.20, f32[256,2048]{0,1:T(8,128)S(1)} %fusion.115), kind=kOutput, calls=%fused_computation.21.clone.1 | convolution fusion | flops 274202624 | bytes 5374976 | tf_op jit(solution)/shard_map/while/body/eval_jaxpr/hk,hn->kn/dot_general | solution.py:150
  99.1 1.8 fusion.117
  102.4 2.7 %convert_reduce_fusion.7 = (f32[256]{0:T(256)S(1)}, bf16[256,2048]{0,1:T(8,128)(2,1)S(1)}) fusion(f32[256,2048]{0,1:T(8,128)} %get-tuple-element.793, bf16[2048,4]{0,1:T(4,128)(2,1)S(1)} %get-tuple-element.795, bf16[256,4]{0,1:T(4,128)(2,1)S(1)} %get-tuple-element.876), kind=kOutput, calls=%fused_computation.19.clone.1 | convolution fusion | flops 9961216 | bytes 3165184 | tf_op jit(solution)/shard_map/while/body/eval_jaxpr/ho,on->hn/dot_general | solution.py:166
  109.5 2.4 %multiply_convert_fusion.7 = (bf16[256,2048]{0,1:T(8,128)(2,1)S(1)}, f32[256,2048]{0,1:T(8,128)}) fusion(f32[256]{0:T(256)S(1)} %get-tuple-element.875, bf16[256,256]{1,0:T(8,128)(2,1)S(1)} %copy-done.20, f32[256,2048]{0,1:T(8,128)S(1)} %fusion.115), kind=kOutput, calls=%fused_computation.21.clone.1 | convolution fusion | flops 274202624 | bytes 5374976 | tf_op jit(solution)/shard_map/while/body/eval_jaxpr/hk,hn->kn/dot_general | solution.py:150
  112.2 1.8 fusion.117
  115.4 2.7 %convert_reduce_fusion.7 = (f32[256]{0:T(256)S(1)}, bf16[256,2048]{0,1:T(8,128)(2,1)S(1)}) fusion(f32[256,2048]{0,1:T(8,128)} %get-tuple-element.793, bf16[2048,4]{0,1:T(4,128)(2,1)S(1)} %get-tuple-element.795, bf16[256,4]{0,1:T(4,128)(2,1)S(1)} %get-tuple-element.876), kind=kOutput, calls=%fused_computation.19.clone.1 | convolution fusion | flops 9961216 | bytes 3165184 | tf_op jit(solution)/shard_map/while/body/eval_jaxpr/ho,on->hn/dot_general | solution.py:166
  122.5 2.4 %multiply_convert_fusion.7 = (bf16[256,2048]{0,1:T(8,128)(2,1)S(1)}, f32[256,2048]{0,1:T(8,128)}) fusion(f32[256]{0:T(256)S(1)} %get-tuple-element.875, bf16[256,256]{1,0:T(8,128)(2,1)S(1)} %copy-done.20, f32[256,2048]{0,1:T(8,128)S(1)} %fusion.115), kind=kOutput, calls=%fused_computation.21.clone.1 | convolution fusion | flops 274202624 | bytes 5374976 | tf_op jit(solution)/shard_map/while/body/eval_jaxpr/hk,hn->kn/dot_general | solution.py:150
  125.3 1.8 fusion.117
  128.5 2.7 %convert_reduce_fusion.7 = (f32[256]{0:T(256)S(1)}, bf16[256,2048]{0,1:T(8,128)(2,1)S(1)}) fusion(f32[256,2048]{0,1:T(8,128)} %get-tuple-element.793, bf16[2048,4]{0,1:T(4,128)(2,1)S(1)} %get-tuple-element.795, bf16[256,4]{0,1:T(4,128)(2,1)S(1)} %get-tuple-element.876), kind=kOutput, calls=%fused_computation.19.clone.1 | convolution fusion | flops 9961216 | bytes 3165184 | tf_op jit(solution)/shard_map/while/body/eval_jaxpr/ho,on->hn/dot_general | solution.py:166
  135.6 2.4 %multiply_convert_fusion.7 = (bf16[256,2048]{0,1:T(8,128)(2,1)S(1)}, f32[256,2048]{0,1:T(8,128)}) fusion(f32[256]{0:T(256)S(1)} %get-tuple-element.875, bf16[256,256]{1,0:T(8,128)(2,1)S(1)} %copy-done.20, f32[256,2048]{0,1:T(8,128)S(1)} %fusion.115), kind=kOutput, calls=%fused_computation.21.clone.1 | convolution fusion | flops 274202624 | bytes 5374976 | tf_op jit(solution)/shard_map/while/body/eval_jaxpr/hk,hn->kn/dot_general | solution.py:150
  138.4 1.8 fusion.117
  141.6 2.7 %convert_reduce_fusion.7 = (f32[256]{0:T(256)S(1)}, bf16[256,2048]{0,1:T(8,128)(2,1)S(1)}) fusion(f32[256,2048]{0,1:T(8,128)} %get-tuple-element.793, bf16[2048,4]{0,1:T(4,128)(2,1)S(1)} %get-tuple-element.795, bf16[256,4]{0,1:T(4,128)(2,1)S(1)} %get-tuple-element.876), kind=kOutput, calls=%fused_computation.19.clone.1 | convolution fusion | flops 9961216 | bytes 3165184 | tf_op jit(solution)/shard_map/while/body/eval_jaxpr/ho,on->hn/dot_general | solution.py:166
  148.7 2.4 %multiply_convert_fusion.7 = (bf16[256,2048]{0,1:T(8,128)(2,1)S(1)}, f32[256,2048]{0,1:T(8,128)}) fusion(f32[256]{0:T(256)S(1)} %get-tuple-element.875, bf16[256,256]{1,0:T(8,128)(2,1)S(1)} %copy-done.20, f32[256,2048]{0,1:T(8,128)S(1)} %fusion.115), kind=kOutput, calls=%fused_computation.21.clone.1 | convolution fusion | flops 274202624 | bytes 5374976 | tf_op jit(solution)/shard_map/while/body/eval_jaxpr/hk,hn->kn/dot_general | solution.py:150
  151.4 1.8 fusion.117
  154.7 2.7 %convert_reduce_fusion.7 = (f32[256]{0:T(256)S(1)}, bf16[256,2048]{0,1:T(8,128)(2,1)S(1)}) fusion(f32[256,2048]{0,1:T(8,128)} %get-tuple-element.793, bf16[2048,4]{0,1:T(4,128)(2,1)S(1)} %get-tuple-element.795, bf16[256,4]{0,1:T(4,128)(2,1)S(1)} %get-tuple-element.876), kind=kOutput, calls=%fused_computation.19.clone.1 | convolution fusion | flops 9961216 | bytes 3165184 | tf_op jit(solution)/shard_map/while/body/eval_jaxpr/ho,on->hn/dot_general | solution.py:166
  162.7 2.1 select_bitcast_fusion
  165.9 4.3 %all-to-all-start.1 = ((bf16[16,4,8,128]{3,1,2,0:T(4,128)(2,1)}), bf16[16,4,8,128]{3,1,2,0:T(4,128)(2,1)S(1)}, u32[]{:S(2)}, u32[]{:S(2)}) async-start(bf16[16,4,8,128]{3,1,2,0:T(4,128)(2,1)} %copy.141), calls=%async_computation.1 | async-start | bytes 262144 | tf_op jit(solution)/shard_map/all_to_all | solution.py:68
  172.4 5.2 %all-to-all-done.1 = bf16[16,4,8,128]{3,1,2,0:T(4,128)(2,1)S(1)} async-done(((bf16[16,4,8,128]{3,1,2,0:T(4,128)(2,1)}), bf16[16,4,8,128]{3,1,2,0:T(4,128)(2,1)S(1)}, u32[]{:S(2)}, u32[]{:S(2)}) %all-to-all-start.1) | async-done | bytes 131104 | tf_op jit(solution)/shard_map/all_to_all | solution.py:68
  177.6 3.3 %all-to-all-start.2 = ((f32[32,9,256]{2,1,0:T(8,128)}), f32[32,9,256]{2,1,0:T(8,128)}, u32[]{:S(2)}, u32[]{:S(2)}) async-start(f32[32,9,256]{2,1,0:T(8,128)} %reshape.223), calls=%async_computation.2 | async-start | bytes 1048576 | tf_op jit(solution)/shard_map/all_to_all | solution.py:248
  180.9 1.4 fusion.47
  182.4 1.6 collective-permute-start.11
  185.3 3.8 %collective-permute-start.9 = (f32[8,1,128]{1,2,0:T(8,128)}, f32[8,1,128]{1,2,0:T(8,128)}, u32[]{:S(2)}, u32[]{:S(2)}) collective-permute-start(f32[8,1,128]{1,2,0:T(8,128)} %get-tuple-element.618), channel_id=1, source_target_pairs={{0,4},{4,8},{8,12},{1,5},{5,9},{9,13},{2,6},{6,10},{10,14},{3,7},{... | collective-permute-start | bytes 12296 | tf_op jit(solution)/shard_map/ppermute | solution.py:19
  189.1 2.4 %collective-permute-start.7 = (f32[8,128,1]{1,2,0:T(1,128)S(1)}, f32[8,128,1]{1,2,0:T(1,128)S(1)}, u32[]{:S(2)}, u32[]{:S(2)}) collective-permute-start(f32[8,128,1]{1,2,0:T(1,128)S(1)} %get-tuple-element.616), channel_id=1, source_target_pairs={{1,0},{2,1},{3,2},{0,3},{5,4},{6,5},{7,6},{4,7},{9,8},{10,9},{11,1... | collective-permute-start | bytes 12296 | tf_op jit(solution)/shard_map/ppermute | solution.py:21
  191.5 1.9 copy.171
  193.5 2.1 copy.139
  196.4 2.0 copy.138
  198.5 1.9 copy.174
  200.4 2.1 collective-permute-start.12
  202.5 1.4 pad_maximum_fusion
  203.9 1.5 collective-permute-start.13
  207.4 3.8 %all-to-all-start.3 = ((f32[32,9,256]{2,1,0:T(8,128)}), f32[32,9,256]{2,1,0:T(8,128)}, u32[]{:S(2)}, u32[]{:S(2)}) async-start(f32[32,9,256]{2,1,0:T(8,128)} %broadcast_in_dim.58), calls=%async_computation.3 | async-start | bytes 1048576 | tf_op jit(solution)/shard_map/all_to_all | solution.py:252
  212.2 2.0 add.256
  214.3 2.2 scatter-add.9
  217.8 2.7 %fusion.18 = f32[1,8,128,128]{2,3,1,0:T(8,128)} fusion(f32[8,128,128]{1,2,0:T(8,128)S(1)} %copy-done.7, f32[8,128,128]{1,2,0:T(8,128)S(1)} %copy-done.8, f32[8,128,128]{1,2,0:T(8,128)S(1)} %scatter-add.9, f32[8,128,128]{1,2,0:T(8,128)S(1)} %copy.129, f32[8,1,128]{1,2,0:T(8,128)} %collective-permute-done.9, f32[8,128,1]{1,2,0:T(1,128)S(1)} %collective-permute-done.8, ...), kind=kOutput, calls=%fused_computation.45 | convolution fusion | flops 102244352 | bytes 2896160 | tf_op jit(solution)/shard_map/tk,kci->cti/dot_general | solution.py:224
  220.5 2.0 copy.145
  222.6 2.9 %all-to-all-done.3 = f32[32,9,256]{2,1,0:T(8,128)} async-done(((f32[32,9,256]{2,1,0:T(8,128)}), f32[32,9,256]{2,1,0:T(8,128)}, u32[]{:S(2)}, u32[]{:S(2)}) %all-to-all-start.3) | async-done | bytes 294944 | tf_op jit(solution)/shard_map/all_to_all | solution.py:252
  (334 shorter events, 73.5 us)
Async XLA Ops:
  0.6 16.4 %copy-start = (bf16[1,1,1,16,4,128,128]{6,5,4,3,2,1,0:T(8,128)(2,1)S(1)}, bf16[1,1,1,16,4,128,128]{6,5,4,3,2,1,0:T(8,128)(2,1)}, u32[]{:S(2)}) copy-start(bf16[1,1,1,16,4,128,128]{6,5,4,3,2,1,0:T(8,128)(2,1)} %param.32) | copy-start | bytes 6291460
  0.6 14.4 %copy-start.16 = (s32[1,1,1,16,4]{3,4,2,1,0:T(4,128)S(1)}, s32[1,1,1,16,4]{3,4,2,1,0:T(4,128)}, u32[]{:S(2)}) copy-start(s32[1,1,1,16,4]{3,4,2,1,0:T(4,128)} %param.33) | copy-start | bytes 772
  0.7 14.6 %copy-start.19 = (s32[1,1,1,16]{3,2,1,0:T(1,128)S(1)}, s32[1,1,1,16]{3,2,1,0:T(1,128)}, u32[]{:S(2)}) copy-start(s32[1,1,1,16]{3,2,1,0:T(1,128)} %param.35) | copy-start | bytes 196
  3.4 22.8 %collective-permute-start.4 = (f32[8,128]{1,0:T(8,128)S(1)}, f32[8,128]{1,0:T(8,128)S(1)}, u32[]{:S(2)}, u32[]{:S(2)}) collective-permute-start(f32[8,128]{1,0:T(8,128)S(1)} %rev.6), channel_id=1, source_target_pairs={{0,1},{1,0},{2,3},{3,2},{4,5},{5,4},{6,7},{7,6},{8,9},{9,8},{10,11... | collective-permute-start | bytes 12296 | tf_op jit(solution)/shard_map/ppermute | solution.py:35
  6.5 22.6 %collective-permute-start.3 = (f32[8,1,128]{1,2,0:T(8,128)}, f32[8,1,128]{1,2,0:T(8,128)}, u32[]{:S(2)}, u32[]{:S(2)}) collective-permute-start(f32[8,1,128]{1,2,0:T(8,128)} %get-tuple-element.625), channel_id=1, source_target_pairs={{4,0},{8,4},{12,8},{5,1},{9,5},{13,9},{6,2},{10,6},{14,10},{7,3},{... | collective-permute-start | bytes 12296 | tf_op jit(solution)/shard_map/ppermute | solution.py:21
  7.8 32.4 %collective-permute-start.2 = (f32[8,1,128]{1,2,0:T(8,128)}, f32[8,1,128]{1,2,0:T(8,128)}, u32[]{:S(2)}, u32[]{:S(2)}) collective-permute-start(f32[8,1,128]{1,2,0:T(8,128)} %get-tuple-element.623), channel_id=1, source_target_pairs={{0,4},{4,8},{8,12},{1,5},{5,9},{9,13},{2,6},{6,10},{10,14},{3,7},{... | collective-permute-start | bytes 12296 | tf_op jit(solution)/shard_map/ppermute | solution.py:19
  11.6 28.6 %collective-permute-start = (f32[8,128,1]{1,2,0:T(1,128)S(1)}, f32[8,128,1]{1,2,0:T(1,128)S(1)}, u32[]{:S(2)}, u32[]{:S(2)}) collective-permute-start(f32[8,128,1]{1,2,0:T(1,128)S(1)} %get-tuple-element.621), channel_id=1, source_target_pairs={{1,0},{2,1},{3,2},{0,3},{5,4},{6,5},{7,6},{4,7},{9,8},{10,9},{11,1... | collective-permute-start | bytes 12296 | tf_op jit(solution)/shard_map/ppermute | solution.py:21
  14.1 26.1 %collective-permute-start.1 = (f32[8,128,1]{1,2,0:T(1,128)S(1)}, f32[8,128,1]{1,2,0:T(1,128)S(1)}, u32[]{:S(2)}, u32[]{:S(2)}) collective-permute-start(f32[8,128,1]{1,2,0:T(1,128)S(1)} %get-tuple-element.622), channel_id=1, source_target_pairs={{0,1},{1,2},{2,3},{3,0},{4,5},{5,6},{6,7},{7,4},{8,9},{9,10},{10,1... | collective-permute-start | bytes 12296 | tf_op jit(solution)/shard_map/ppermute | solution.py:19
  14.2 10.5 %copy-start.18 = (f32[2,8,4]{1,2,0:T(4,128)S(1)}, f32[2,8,4]{1,2,0:T(4,128)}, u32[]{:S(2)}) copy-start(f32[2,8,4]{1,2,0:T(4,128)} %param.25) | copy-start | bytes 772
  14.2 10.5 %copy-start.22 = (f32[2,8]{1,0:T(2,128)S(1)}, f32[2,8]{1,0:T(2,128)}, u32[]{:S(2)}) copy-start(f32[2,8]{1,0:T(2,128)} %param.24) | copy-start | bytes 196
  14.2 10.6 %copy-start.12 = (s32[1,128,128]{2,1,0:T(8,128)S(1)}, s32[1,128,128]{2,1,0:T(8,128)}, u32[]{:S(2)}) copy-start(s32[1,128,128]{2,1,0:T(8,128)} %param.23) | copy-start | bytes 196612
  14.2 10.7 %copy-start.3 = (f32[1,8,128,128]{3,2,1,0:T(8,128)S(1)}, f32[1,8,128,128]{3,2,1,0:T(8,128)}, u32[]{:S(2)}) copy-start(f32[1,8,128,128]{3,2,1,0:T(8,128)} %param.21) | copy-start | bytes 1572868
  17.1 9.0 %copy-start.17 = (s32[1,1,1,16,4]{3,4,2,1,0:T(4,128)S(1)}, s32[1,1,1,16,4]{3,4,2,1,0:T(4,128)}, u32[]{:S(2)}) copy-start(s32[1,1,1,16,4]{3,4,2,1,0:T(4,128)} %param.34) | copy-start | bytes 772
  18.4 25.3 %all-to-all-start = ((f32[16,4,8,128]{3,2,1,0:T(8,128)}), f32[16,4,8,128]{3,2,1,0:T(8,128)}, u32[]{:S(2)}, u32[]{:S(2)}) async-start(f32[16,4,8,128]{3,2,1,0:T(8,128)} %bitcast.7), calls=%async_computation | async-start | bytes 524288 | tf_op jit(solution)/shard_map/all_to_all | solution.py:62
  26.3 8.2 %collective-permute-start.5 = (f32[8,128]{1,0:T(8,128)S(1)}, f32[8,128]{1,0:T(8,128)S(1)}, u32[]{:S(2)}, u32[]{:S(2)}) collective-permute-start(f32[8,128]{1,0:T(8,128)S(1)} %collective-permute-done.4), channel_id=1, source_target_pairs={{0,2},{2,0},{1,3},{3,1},{4,6},{6,4},{5,7},{7,5},{8,10},{10,8},{9,1... | collective-permute-start | bytes 12296 | tf_op jit(solution)/shard_map/ppermute | solution.py:35
  43.8 8.1 %collective-permute-start.6 = (f32[16,4,8,128]{3,2,1,0:T(8,128)}, f32[16,4,8,128]{3,2,1,0:T(8,128)S(1)}, u32[]{:S(2)}, u32[]{:S(2)}) collective-permute-start(f32[16,4,8,128]{3,2,1,0:T(8,128)} %all-to-all-done), channel_id=1, source_target_pairs={{0,16},{16,0},{1,17},{17,1},{2,18},{18,2},{3,19},{19,3},{4,20},{20... | collective-permute-start | bytes 786440 | tf_op jit(solution)/shard_map/ppermute | solution.py:35
  52.8 3.3 %copy-start.9 = (bf16[16,256]{1,0:T(8,128)(2,1)S(1)}, bf16[16,256]{1,0:T(8,128)(2,1)}, u32[]{:S(2)}) copy-start(bf16[16,256]{1,0:T(8,128)(2,1)} %param.26) | copy-start | bytes 24580
  52.8 3.3 %copy-start.13 = (bf16[256,4]{0,1:T(4,128)(2,1)S(1)}, bf16[256,4]{0,1:T(4,128)(2,1)}, u32[]{:S(2)}) copy-start(bf16[256,4]{0,1:T(4,128)(2,1)} %param.30) | copy-start | bytes 6148
  52.8 3.2 %copy-start.14 = (f32[256]{0:T(256)S(1)}, f32[256]{0:T(256)}, u32[]{:S(2)}) copy-start(f32[256]{0:T(256)} %param.27) | copy-start | bytes 3076
  52.8 3.2 %copy-start.15 = (f32[4]{0:T(128)S(1)}, f32[4]{0:T(128)}, u32[]{:S(2)}) copy-start(f32[4]{0:T(128)} %param.31) | copy-start | bytes 52
  52.8 3.2 %copy-start.23 = (f32[256]{0:T(256)S(1)}, f32[256]{0:T(256)}, u32[]{:S(2)}) copy-start(f32[256]{0:T(256)} %param.29) | copy-start | bytes 3076
  56.6 2.9 %copy-start.1 = (f32[256,2048]{0,1:T(8,128)}, f32[256,2048]{0,1:T(8,128)S(1)}, u32[]{:S(2)}) copy-start(f32[256,2048]{0,1:T(8,128)S(1)} %fusion.115) | copy-start | bytes 6291460 | tf_op jit(solution)/shard_map/while
  63.1 2.7 %copy-start.2 = (f32[256,2048]{0,1:T(8,128)S(1)}, f32[256,2048]{0,1:T(8,128)}, u32[]{:S(2)}) copy-start(f32[256,2048]{0,1:T(8,128)} %copy-done.1) | copy-start | bytes 6291460 | tf_op jit(solution)/shard_map/while
  63.1 2.7 %copy-start.10 = (f32[256,256]{1,0:T(8,128)S(1)}, f32[256,256]{1,0:T(8,128)}, u32[]{:S(2)}) copy-start(f32[256,256]{1,0:T(8,128)} %get-tuple-element.835) | copy-start | bytes 786436 | tf_op jit(solution)/shard_map/while
  66.8 2.0 copy-start.6
  69.7 2.9 %copy-start.1 = (f32[256,2048]{0,1:T(8,128)}, f32[256,2048]{0,1:T(8,128)S(1)}, u32[]{:S(2)}) copy-start(f32[256,2048]{0,1:T(8,128)S(1)} %fusion.115) | copy-start | bytes 6291460 | tf_op jit(solution)/shard_map/while
  76.2 2.7 %copy-start.2 = (f32[256,2048]{0,1:T(8,128)S(1)}, f32[256,2048]{0,1:T(8,128)}, u32[]{:S(2)}) copy-start(f32[256,2048]{0,1:T(8,128)} %copy-done.1) | copy-start | bytes 6291460 | tf_op jit(solution)/shard_map/while
  76.2 2.7 %copy-start.10 = (f32[256,256]{1,0:T(8,128)S(1)}, f32[256,256]{1,0:T(8,128)}, u32[]{:S(2)}) copy-start(f32[256,256]{1,0:T(8,128)} %get-tuple-element.835) | copy-start | bytes 786436 | tf_op jit(solution)/shard_map/while
  79.9 2.0 copy-start.6
  82.7 2.9 %copy-start.1 = (f32[256,2048]{0,1:T(8,128)}, f32[256,2048]{0,1:T(8,128)S(1)}, u32[]{:S(2)}) copy-start(f32[256,2048]{0,1:T(8,128)S(1)} %fusion.115) | copy-start | bytes 6291460 | tf_op jit(solution)/shard_map/while
  89.3 2.7 %copy-start.2 = (f32[256,2048]{0,1:T(8,128)S(1)}, f32[256,2048]{0,1:T(8,128)}, u32[]{:S(2)}) copy-start(f32[256,2048]{0,1:T(8,128)} %copy-done.1) | copy-start | bytes 6291460 | tf_op jit(solution)/shard_map/while
  89.3 2.7 %copy-start.10 = (f32[256,256]{1,0:T(8,128)S(1)}, f32[256,256]{1,0:T(8,128)}, u32[]{:S(2)}) copy-start(f32[256,256]{1,0:T(8,128)} %get-tuple-element.835) | copy-start | bytes 786436 | tf_op jit(solution)/shard_map/while
  93.0 2.0 copy-start.6
  95.8 2.9 %copy-start.1 = (f32[256,2048]{0,1:T(8,128)}, f32[256,2048]{0,1:T(8,128)S(1)}, u32[]{:S(2)}) copy-start(f32[256,2048]{0,1:T(8,128)S(1)} %fusion.115) | copy-start | bytes 6291460 | tf_op jit(solution)/shard_map/while
  102.4 2.7 %copy-start.2 = (f32[256,2048]{0,1:T(8,128)S(1)}, f32[256,2048]{0,1:T(8,128)}, u32[]{:S(2)}) copy-start(f32[256,2048]{0,1:T(8,128)} %copy-done.1) | copy-start | bytes 6291460 | tf_op jit(solution)/shard_map/while
  102.4 2.7 %copy-start.10 = (f32[256,256]{1,0:T(8,128)S(1)}, f32[256,256]{1,0:T(8,128)}, u32[]{:S(2)}) copy-start(f32[256,256]{1,0:T(8,128)} %get-tuple-element.835) | copy-start | bytes 786436 | tf_op jit(solution)/shard_map/while
  106.0 2.0 copy-start.6
  108.9 2.9 %copy-start.1 = (f32[256,2048]{0,1:T(8,128)}, f32[256,2048]{0,1:T(8,128)S(1)}, u32[]{:S(2)}) copy-start(f32[256,2048]{0,1:T(8,128)S(1)} %fusion.115) | copy-start | bytes 6291460 | tf_op jit(solution)/shard_map/while
  115.4 2.7 %copy-start.2 = (f32[256,2048]{0,1:T(8,128)S(1)}, f32[256,2048]{0,1:T(8,128)}, u32[]{:S(2)}) copy-start(f32[256,2048]{0,1:T(8,128)} %copy-done.1) | copy-start | bytes 6291460 | tf_op jit(solution)/shard_map/while
  115.4 2.7 %copy-start.10 = (f32[256,256]{1,0:T(8,128)S(1)}, f32[256,256]{1,0:T(8,128)}, u32[]{:S(2)}) copy-start(f32[256,256]{1,0:T(8,128)} %get-tuple-element.835) | copy-start | bytes 786436 | tf_op jit(solution)/shard_map/while
  119.1 2.0 copy-start.6
  122.0 2.9 %copy-start.1 = (f32[256,2048]{0,1:T(8,128)}, f32[256,2048]{0,1:T(8,128)S(1)}, u32[]{:S(2)}) copy-start(f32[256,2048]{0,1:T(8,128)S(1)} %fusion.115) | copy-start | bytes 6291460 | tf_op jit(solution)/shard_map/while
  128.5 2.7 %copy-start.2 = (f32[256,2048]{0,1:T(8,128)S(1)}, f32[256,2048]{0,1:T(8,128)}, u32[]{:S(2)}) copy-start(f32[256,2048]{0,1:T(8,128)} %copy-done.1) | copy-start | bytes 6291460 | tf_op jit(solution)/shard_map/while
  128.5 2.7 %copy-start.10 = (f32[256,256]{1,0:T(8,128)S(1)}, f32[256,256]{1,0:T(8,128)}, u32[]{:S(2)}) copy-start(f32[256,256]{1,0:T(8,128)} %get-tuple-element.835) | copy-start | bytes 786436 | tf_op jit(solution)/shard_map/while
  132.2 2.0 copy-start.6
  135.0 2.9 %copy-start.1 = (f32[256,2048]{0,1:T(8,128)}, f32[256,2048]{0,1:T(8,128)S(1)}, u32[]{:S(2)}) copy-start(f32[256,2048]{0,1:T(8,128)S(1)} %fusion.115) | copy-start | bytes 6291460 | tf_op jit(solution)/shard_map/while
  141.6 2.7 %copy-start.2 = (f32[256,2048]{0,1:T(8,128)S(1)}, f32[256,2048]{0,1:T(8,128)}, u32[]{:S(2)}) copy-start(f32[256,2048]{0,1:T(8,128)} %copy-done.1) | copy-start | bytes 6291460 | tf_op jit(solution)/shard_map/while
  141.6 2.7 %copy-start.10 = (f32[256,256]{1,0:T(8,128)S(1)}, f32[256,256]{1,0:T(8,128)}, u32[]{:S(2)}) copy-start(f32[256,256]{1,0:T(8,128)} %get-tuple-element.835) | copy-start | bytes 786436 | tf_op jit(solution)/shard_map/while
  145.3 2.0 copy-start.6
  148.1 2.9 %copy-start.1 = (f32[256,2048]{0,1:T(8,128)}, f32[256,2048]{0,1:T(8,128)S(1)}, u32[]{:S(2)}) copy-start(f32[256,2048]{0,1:T(8,128)S(1)} %fusion.115) | copy-start | bytes 6291460 | tf_op jit(solution)/shard_map/while
  154.7 2.7 %copy-start.2 = (f32[256,2048]{0,1:T(8,128)S(1)}, f32[256,2048]{0,1:T(8,128)}, u32[]{:S(2)}) copy-start(f32[256,2048]{0,1:T(8,128)} %copy-done.1) | copy-start | bytes 6291460 | tf_op jit(solution)/shard_map/while
  154.7 2.7 %copy-start.10 = (f32[256,256]{1,0:T(8,128)S(1)}, f32[256,256]{1,0:T(8,128)}, u32[]{:S(2)}) copy-start(f32[256,256]{1,0:T(8,128)} %get-tuple-element.835) | copy-start | bytes 786436 | tf_op jit(solution)/shard_map/while
  158.3 2.0 copy-start.6
  161.9 8.3 %copy-start.4 = (f32[8,16384]{1,0:T(8,128)S(1)}, f32[8,16384]{1,0:T(8,128)}, u32[]{:S(2)}) copy-start(f32[8,16384]{1,0:T(8,128)} %get-tuple-element.420) | copy-start | bytes 1572868
  165.9 11.7 %all-to-all-start.1 = ((bf16[16,4,8,128]{3,1,2,0:T(4,128)(2,1)}), bf16[16,4,8,128]{3,1,2,0:T(4,128)(2,1)S(1)}, u32[]{:S(2)}, u32[]{:S(2)}) async-start(bf16[16,4,8,128]{3,1,2,0:T(4,128)(2,1)} %copy.141), calls=%async_computation.1 | async-start | bytes 262144 | tf_op jit(solution)/shard_map/all_to_all | solution.py:68
  177.6 27.8 %all-to-all-start.2 = ((f32[32,9,256]{2,1,0:T(8,128)}), f32[32,9,256]{2,1,0:T(8,128)}, u32[]{:S(2)}, u32[]{:S(2)}) async-start(f32[32,9,256]{2,1,0:T(8,128)} %reshape.223), calls=%async_computation.2 | async-start | bytes 1048576 | tf_op jit(solution)/shard_map/all_to_all | solution.py:248
  182.4 18.0 %collective-permute-start.11 = (f32[8,128]{1,0:T(8,128)S(1)}, f32[8,128]{1,0:T(8,128)S(1)}, u32[]{:S(2)}, u32[]{:S(2)}) collective-permute-start(f32[8,128]{1,0:T(8,128)S(1)} %rev.7), channel_id=1, source_target_pairs={{0,1},{1,0},{2,3},{3,2},{4,5},{5,4},{6,7},{7,6},{8,9},{9,8},{10,11... | collective-permute-start | bytes 12296 | tf_op jit(solution)/shard_map/ppermute | solution.py:35
  184.0 18.5 %collective-permute-start.10 = (f32[8,1,128]{1,2,0:T(8,128)}, f32[8,1,128]{1,2,0:T(8,128)}, u32[]{:S(2)}, u32[]{:S(2)}) collective-permute-start(f32[8,1,128]{1,2,0:T(8,128)} %get-tuple-element.620), channel_id=1, source_target_pairs={{4,0},{8,4},{12,8},{5,1},{9,5},{13,9},{6,2},{10,6},{14,10},{7,3},{... | collective-permute-start | bytes 12296 | tf_op jit(solution)/shard_map/ppermute | solution.py:21
  185.3 32.5 %collective-permute-start.9 = (f32[8,1,128]{1,2,0:T(8,128)}, f32[8,1,128]{1,2,0:T(8,128)}, u32[]{:S(2)}, u32[]{:S(2)}) collective-permute-start(f32[8,1,128]{1,2,0:T(8,128)} %get-tuple-element.618), channel_id=1, source_target_pairs={{0,4},{4,8},{8,12},{1,5},{5,9},{9,13},{2,6},{6,10},{10,14},{3,7},{... | collective-permute-start | bytes 12296 | tf_op jit(solution)/shard_map/ppermute | solution.py:19
  189.1 28.7 %collective-permute-start.7 = (f32[8,128,1]{1,2,0:T(1,128)S(1)}, f32[8,128,1]{1,2,0:T(1,128)S(1)}, u32[]{:S(2)}, u32[]{:S(2)}) collective-permute-start(f32[8,128,1]{1,2,0:T(1,128)S(1)} %get-tuple-element.616), channel_id=1, source_target_pairs={{1,0},{2,1},{3,2},{0,3},{5,4},{6,5},{7,6},{4,7},{9,8},{10,9},{11,1... | collective-permute-start | bytes 12296 | tf_op jit(solution)/shard_map/ppermute | solution.py:21
  191.5 26.2 %collective-permute-start.8 = (f32[8,128,1]{1,2,0:T(1,128)S(1)}, f32[8,128,1]{1,2,0:T(1,128)S(1)}, u32[]{:S(2)}, u32[]{:S(2)}) collective-permute-start(f32[8,128,1]{1,2,0:T(1,128)S(1)} %get-tuple-element.617), channel_id=1, source_target_pairs={{0,1},{1,2},{2,3},{3,0},{4,5},{5,6},{6,7},{7,4},{8,9},{9,10},{10,1... | collective-permute-start | bytes 12296 | tf_op jit(solution)/shard_map/ppermute | solution.py:19
  200.4 10.8 %collective-permute-start.12 = (f32[8,128]{1,0:T(8,128)S(1)}, f32[8,128]{1,0:T(8,128)S(1)}, u32[]{:S(2)}, u32[]{:S(2)}) collective-permute-start(f32[8,128]{1,0:T(8,128)S(1)} %collective-permute-done.11), channel_id=1, source_target_pairs={{0,2},{2,0},{1,3},{3,1},{4,6},{6,4},{5,7},{7,5},{8,10},{10,8},{9,1... | collective-permute-start | bytes 12296 | tf_op jit(solution)/shard_map/ppermute | solution.py:35
  203.9 12.7 %collective-permute-start.13 = (bf16[16,4,8,128]{3,1,2,0:T(4,128)(2,1)S(1)}, bf16[16,4,8,128]{3,1,2,0:T(4,128)(2,1)S(1)}, u32[]{:S(2)}, u32[]{:S(2)}) collective-permute-start(bf16[16,4,8,128]{3,1,2,0:T(4,128)(2,1)S(1)} %all-to-all-done.1), channel_id=1, source_target_pairs={{0,16},{16,0},{1,17},{17,1},{2,18},{18,2},{3,19},{19,3},{4,20},{20... | collective-permute-start | bytes 393224 | tf_op jit(solution)/shard_map/ppermute | solution.py:35
  207.4 18.0 %all-to-all-start.3 = ((f32[32,9,256]{2,1,0:T(8,128)}), f32[32,9,256]{2,1,0:T(8,128)}, u32[]{:S(2)}, u32[]{:S(2)}) async-start(f32[32,9,256]{2,1,0:T(8,128)} %broadcast_in_dim.58), calls=%async_computation.3 | async-start | bytes 1048576 | tf_op jit(solution)/shard_map/all_to_all | solution.py:252
  (34 other events, 32.8 us)

commit v2 on v0

v2 whole, which is shorter than its diff:
```python
import functools
import math

import jax
import jax.numpy as jnp
from jax import lax
from jax.experimental import pallas as pl
from jax.experimental.pallas import tpu as pltpu
from jax.sharding import PartitionSpec as P

EVERYWHERE = ("comp", "gy", "gx")
BLOCK_ROWS = 8
CHUNK = 256
SUBLANES = 8

OWN, OTHER, WEST, EAST, SOUTH, NORTH, COMP, HAS_SOUTH, HAS_NORTH, ON_FOLD = range(10)

f32 = jnp.float32
bf16 = jnp.bfloat16


def dot(a, b):
    return jnp.dot(a, b, preferred_element_type=f32)


def dot_nt(a, b):
    return lax.dot_general(a, b, (((1,), (1,)), ((), ())), preferred_element_type=f32)


def mirror(tile):
    width = tile.shape[1]
    row = lax.broadcasted_iota(jnp.int32, (width, width), 0)
    col = lax.broadcasted_iota(jnp.int32, (width, width), 1)
    flip = (row + col == width - 1).astype(f32).astype(bf16)
    return dot(tile.astype(bf16), flip)


def edge_columns(read_row, rows, shape):
    lane = lax.broadcasted_iota(jnp.int32, shape, 1)
    width = shape[1]

    def step(r, sides):
        first, last = sides
        tile = read_row(r)
        here = lane == r
        first = jnp.where(here, pltpu.roll(tile, r, 1), first)
        last = jnp.where(here, pltpu.roll(tile, lax.rem(r + 1, width), 1), last)
        return first, last

    zero = jnp.zeros(shape, f32)
    return lax.fori_loop(0, rows, step, (zero, zero), unroll=8)


def put_edges(meta, read_row, rows, shape, stage):
    first, last = edge_columns(read_row, rows, shape)
    stage[meta[EAST], 0:SUBLANES, :] = last
    stage[meta[WEST], SUBLANES : 2 * SUBLANES, :] = first
    top = read_row(rows - 1)
    top = jnp.where(meta[ON_FOLD] == 1, mirror(top), top)
    stage[meta[NORTH], 2 * SUBLANES : 3 * SUBLANES, :] = top
    stage[meta[SOUTH], 3 * SUBLANES : 4 * SUBLANES, :] = read_row(0)


def get_edges(meta, recv):
    west = recv[meta[WEST], 0:32, :].astype(f32)[0:SUBLANES]
    east = recv[meta[EAST], 0:32, :].astype(f32)[SUBLANES : 2 * SUBLANES]
    south = recv[meta[SOUTH], 0:32, :].astype(f32)[2 * SUBLANES : 3 * SUBLANES]
    above = recv[meta[NORTH], 0:32, :].astype(f32)
    north = jnp.where(
        meta[ON_FOLD] == 1,
        above[2 * SUBLANES : 3 * SUBLANES],
        above[3 * SUBLANES : 4 * SUBLANES],
    )
    south = jnp.where(meta[HAS_SOUTH] == 1, south, 0.0)
    north = jnp.where(meta[HAS_NORTH] == 1, north, 0.0)
    return west, east, south, north


def laplace_row(here, below, above, west, east, r, lane):
    width = here.shape[1]
    left = jnp.where(
        lane == 0, pltpu.roll(west, lax.rem(width - r, width), 1), pltpu.roll(here, 1, 1)
    )
    right = jnp.where(
        lane == width - 1, pltpu.roll(east, width - 1 - r, 1), pltpu.roll(here, width - 1, 1)
    )
    return left + right + below + above - 4.0 * here


def send_kernel(rows, peers, slots, meta, source, count, state, kernels, out, stage):
    shape = (SUBLANES, state.shape[1])

    def read_row(r):
        return state[pl.ds(r, SUBLANES, stride=rows), :]

    stage[pl.ds(meta[OWN], peers)] = jnp.zeros((peers,) + stage.shape[1:], f32)

    def peer_step(q, unused):
        for s in range(slots):
            k = q * slots + s
            picked = read_row(source[k]).astype(bf16)
            live = (s < count[q]).astype(f32)
            stage[meta[OTHER] + q, s * SUBLANES : (s + 1) * SUBLANES, :] = (
                dot(picked, kernels[k]) * live
            )
        return unused

    lax.fori_loop(0, peers, peer_step, 0, unroll=4)
    put_edges(meta, read_row, rows, shape, stage)
    out[...] = stage[...].astype(bf16)


def main_kernel(
    rows,
    peers,
    slots,
    share,
    small_share,
    meta,
    landing,
    b_out,
    state,
    goal,
    mask,
    recv,
    rate_ref,
    couple_ref,
    w_first,
    w_second,
    b_second,
    w_third,
    w_third_back,
    w_second_back,
    w_first_back,
    new_out,
    base_out,
    diffuse_out,
    send_out,
    stage,
    other,
    feat,
    hid_first,
    hid_second,
    slope_first,
    slope_second,
    cot_second,
    cot_first,
    flux,
    flux_cot,
    feat_cot,
    g_first,
    g_second,
    g_third,
    g_bias,
    small,
):
    width = state.shape[1]
    hidden = w_second.shape[0]
    shape = (SUBLANES, width)
    cells = BLOCK_ROWS * width
    lane = lax.broadcasted_iota(jnp.int32, shape, 1)
    sub = lax.broadcasted_iota(jnp.int32, shape, 0)
    fluxes = couple_ref.shape[2]

    def read_row(r):
        return state[pl.ds(r, SUBLANES, stride=rows), :]

    other[...] = jnp.zeros(other.shape, f32)

    def land(p, unused):
        block = recv[meta[OTHER] + p, 0:32, :].astype(f32)
        for s in range(slots):
            row = landing[p * slots + s]
            other[row] = other[row] + block[s * SUBLANES : (s + 1) * SUBLANES]
        return unused

    lax.fori_loop(0, peers, land, 0, unroll=2)
    west, east, south, north = get_edges(meta, recv)
    comp = meta[COMP]
    eye = (
        lax.broadcasted_iota(jnp.int32, (SUBLANES, SUBLANES), 0)
        == lax.broadcasted_iota(jnp.int32, (SUBLANES, SUBLANES), 1)
    ).astype(f32)
    rate = jnp.sum(
        jnp.broadcast_to(rate_ref[pl.ds(comp, 1), :], (SUBLANES, SUBLANES)) * eye,
        axis=1,
        keepdims=True,
    )
    rate = jnp.broadcast_to(rate, shape)
    pairs = couple_ref[comp]
    couple = [jnp.broadcast_to(pairs[:, f : f + 1], shape) for f in range(fluxes)]
    ones = (lax.broadcasted_iota(jnp.int32, (16, cells), 0) < 3).astype(f32).astype(bf16)
    feat[16:32, :] = ones
    hid_first[hidden : hidden + 16, :] = ones
    flux_cot[...] = jnp.zeros(flux_cot.shape, bf16)
    g_first[...] = jnp.zeros(g_first.shape, f32)
    g_second[...] = jnp.zeros(g_second.shape, f32)
    g_third[...] = jnp.zeros(g_third.shape, f32)
    g_bias[...] = jnp.zeros(g_bias.shape, f32)
    bias = jnp.broadcast_to(b_second[...], (hidden, CHUNK))
    b_third = jnp.zeros(shape, f32)
    for f in range(fluxes):
        b_third = jnp.where(sub == f, b_out[f], b_third)

    def block_step(block, unused):
        start = block * BLOCK_ROWS
        for i in range(BLOCK_ROWS):
            at = pl.ds(i * width, width)
            r = start + i
            feat[0:16, at] = jnp.concatenate([read_row(r), other[r]], axis=0).astype(bf16)
        for j in range(cells // CHUNK):
            at = pl.ds(j * CHUNK, CHUNK)
            half = dot(w_first[...], feat[:, at])
            turn = jnp.tanh(half)
            up = 1.0 + turn
            hid = half * up
            hid_first[0:hidden, at] = hid.astype(bf16)
            slope_first[:, at] = (up + hid) - hid * turn
        for j in range(cells // CHUNK):
            at = pl.ds(j * CHUNK, CHUNK)
            half = dot(w_second[...], hid_first[0:hidden, at]) + bias
            turn = jnp.tanh(half)
            up = 1.0 + turn
            hid = half * up
            hid_second[:, at] = hid.astype(bf16)
            slope_second[:, at] = (up + hid) - hid * turn
        for j in range(cells // CHUNK):
            at = pl.ds(j * CHUNK, CHUNK)
            flux[:, at] = dot(w_third[...], hid_second[:, at])[0:SUBLANES]
        for i in range(BLOCK_ROWS):
            at = pl.ds(i * width, width)
            r = start + i
            here = read_row(r)
            below = jnp.where(r > 0, read_row(jnp.maximum(r - 1, 0)), south)
            above = jnp.where(r < rows - 1, read_row(jnp.minimum(r + 1, rows - 1)), north)
            lap = laplace_row(here, below, above, west, east, r, lane)
            wet = jnp.broadcast_to(mask[pl.ds(r, 1), :].astype(f32), shape)
            spread_mask = jnp.where(comp == 1, wet, 1.0)
            wet_flux = (flux[:, at] + b_third) * wet
            updated = here + rate * spread_mask * lap
            for f in range(fluxes):
                updated = updated + couple[f] * jnp.broadcast_to(wet_flux[f : f + 1], shape)
            new_out[pl.ds(r, SUBLANES, stride=rows), :] = updated
            misfit = updated - goal[pl.ds(r, SUBLANES, stride=rows), :]
            diffuse_out[r] = spread_mask * misfit
            base_out[r] = misfit
            pulled = jnp.zeros(shape, f32)
            for f in range(fluxes):
                total = jnp.sum(couple[f] * misfit, axis=0, keepdims=True)
                pulled = jnp.where(sub == f, jnp.broadcast_to(total, shape), pulled)
            pulled = (pulled * wet).astype(bf16)
            flux_cot[0:SUBLANES, at] = pulled
            g_bias[...] = g_bias[...] + pulled.astype(f32)
        for j in range(cells // CHUNK):
            at = pl.ds(j * CHUNK, CHUNK)
            cot_second[:, at] = (
                dot(w_third_back[...], flux_cot[:, at]) * slope_second[:, at]
            ).astype(bf16)
        for j in range(cells // CHUNK):
            at = pl.ds(j * CHUNK, CHUNK)
            cot_first[:, at] = (
                dot(w_second_back[...], cot_second[:, at]) * slope_first[:, at]
            ).astype(bf16)
        for j in range(cells // CHUNK):
            at = pl.ds(j * CHUNK, CHUNK)
            feat_cot[:, at] = dot(w_first_back[...], cot_first[:, at])
        for i in range(BLOCK_ROWS):
            at = pl.ds(i * width, width)
            r = start + i
            base_out[r] = base_out[r] + feat_cot[0:SUBLANES, at]
            other[r] = feat_cot[SUBLANES : 2 * SUBLANES, at]
        g_second[...] += dot_nt(hid_first[...], cot_second[...])
        g_first[...] += dot_nt(feat[...], cot_first[...])
        g_third[...] += dot_nt(flux_cot[...], hid_second[...])
        return unused

    lax.fori_loop(0, rows // BLOCK_ROWS, block_step, 0)

    stage[pl.ds(meta[OWN], peers), 0:32, :] = jnp.zeros((peers, 32, width), f32)

    def leave(p, unused):
        for s in range(slots):
            row = landing[p * slots + s]
            stage[meta[OTHER] + p, s * SUBLANES : (s + 1) * SUBLANES, :] = other[row]
        return unused

    lax.fori_loop(0, peers, leave, 0, unroll=2)
    put_edges(meta, lambda r: diffuse_out[r], rows, shape, stage)

    devices = stage.shape[0]
    halves = hidden // width
    inputs = 2 * SUBLANES
    small[...] = jnp.zeros(small.shape, f32)
    low, high = g_first[0:SUBLANES, :], g_first[SUBLANES:inputs, :]
    low, high = jnp.where(comp == 1, high, low), jnp.where(comp == 1, low, high)
    bias_sum = jnp.sum(g_bias[...], axis=1, keepdims=True)
    bias_row = jnp.sum(jnp.where(sub == lane, jnp.broadcast_to(bias_sum, shape), 0.0), axis=0,
                       keepdims=True)
    for h in range(halves):
        cols = slice(h * width, (h + 1) * width)
        top = h * 24
        small[top : top + 8, :] = low[:, cols]
        small[top + 8 : top + 16, :] = high[:, cols]
        small[top + 16 : top + 17, :] = g_first[inputs : inputs + 1, cols]
        small[top + 17 : top + 18, :] = g_second[hidden : hidden + 1, cols]
        if h == 0:
            small[top + 18 : top + 19, :] = bias_row
        small[top + 19 : top + 19 + fluxes, :] = g_third[0:fluxes, cols]
    for d in range(devices):
        done = 0
        while done < share:
            at = d * share + done
            h, row = divmod(at, hidden)
            step = min(share - done, hidden - row)
            if h < halves:
                stage[d, 32 + done : 32 + done + step, :] = g_second[
                    row : row + step, h * width : (h + 1) * width
                ]
            done += step
        stage[d, 32 + share : 32 + share + small_share, :] = small[
            d * small_share : (d + 1) * small_share, :
        ]
    send_out[...] = stage[...].astype(bf16)


def sum_kernel(scale, recv, out):
    devices = recv.shape[0]
    total = recv[0, 32:, :].astype(f32)
    for d in range(1, devices):
        total = total + recv[d, 32:, :].astype(f32)
    total = (total * scale).astype(bf16)
    for d in range(devices):
        out[d] = total


def back_kernel(
    rows, peers, slots, meta, source, count, recv, kernels, base, diffuse, rate_ref, out, total
):
    width = diffuse.shape[2]
    shape = (SUBLANES, width)
    lane = lax.broadcasted_iota(jnp.int32, shape, 1)
    west, east, south, north = get_edges(meta, recv)
    comp = meta[COMP]
    eye = (
        lax.broadcasted_iota(jnp.int32, (SUBLANES, SUBLANES), 0)
        == lax.broadcasted_iota(jnp.int32, (SUBLANES, SUBLANES), 1)
    ).astype(f32)
    rate = jnp.sum(
        jnp.broadcast_to(rate_ref[pl.ds(comp, 1), :], (SUBLANES, SUBLANES)) * eye,
        axis=1,
        keepdims=True,
    )
    rate = jnp.broadcast_to(rate, shape)

    def lap_step(r, unused):
        here = diffuse[r]
        below = jnp.where(r > 0, diffuse[jnp.maximum(r - 1, 0)], south)
        above = jnp.where(r < rows - 1, diffuse[jnp.minimum(r + 1, rows - 1)], north)
        total[r] = base[r] + rate * laplace_row(here, below, above, west, east, r, lane)
        return unused

    lax.fori_loop(0, rows, lap_step, 0, unroll=8)

    def peer_step(q, unused):
        block = recv[meta[OTHER] + q, 0:32, :].astype(f32)
        for s in range(slots):
            k = q * slots + s
            sent = block[s * SUBLANES : (s + 1) * SUBLANES].astype(bf16)
            live = (s < count[q]).astype(f32)
            row = source[k]
            total[row] = total[row] + dot_nt(sent, kernels[k]) * live
        return unused

    lax.fori_loop(0, peers, peer_step, 0, unroll=4)

    def out_step(r, unused):
        out[pl.ds(r, SUBLANES, stride=rows), :] = total[r]
        return unused

    lax.fori_loop(0, rows, out_step, 0, unroll=8)


def unpack_kernel(share, small_share, fluxes, recv, first, bias_one, second, bias_two, third,
                  bias_three, small):
    devices = recv.shape[0]
    width = recv.shape[2]
    hidden = second.shape[0]
    halves = hidden // width
    for d in range(devices):
        block = recv[d].astype(f32)
        done = 0
        while done < share:
            at = d * share + done
            h, row = divmod(at, hidden)
            step = min(share - done, hidden - row)
            if h < halves:
                second[row : row + step, h * width : (h + 1) * width] = block[done : done + step]
            done += step
        small[d * small_share : (d + 1) * small_share, :] = block[share : share + small_share]
    for h in range(halves):
        cols = slice(h * width, (h + 1) * width)
        top = h * 24
        first[:, cols] = small[top : top + 16, :]
        bias_one[:, cols] = small[top + 16 : top + 17, :]
        bias_two[:, cols] = small[top + 17 : top + 18, :]
        third[:, cols] = small[top + 19 : top + 19 + fluxes, :]
    bias_three[...] = small[18:19, :]


def shards(
    state,
    target,
    land_mask,
    diffusivity,
    coupling,
    w_in,
    b_in,
    w_mid,
    b_mid,
    w_out,
    b_out,
    remap_weight,
    remap_source,
    remap_target,
    remap_count,
):
    n_gy, n_gx = lax.axis_size("gy"), lax.axis_size("gx")
    tiles = n_gy * n_gx
    devices = 2 * tiles
    comp, row, col = (lax.axis_index(axis) for axis in EVERYWHERE)
    own, other = comp * tiles, (1 - comp) * tiles
    is_top = row == n_gy - 1
    on_fold = jnp.logical_and(comp == 1, is_top)
    line = own + row * n_gx
    here = line + col
    meta = jnp.stack(
        [
            own,
            other,
            line + (col + n_gx - 1) % n_gx,
            line + (col + 1) % n_gx,
            jnp.where(row > 0, here - n_gx, here),
            jnp.where(on_fold, line + n_gx - 1 - col, jnp.where(is_top, here, here + n_gx)),
            comp,
            (row > 0).astype(jnp.int32),
            jnp.logical_or(on_fold, jnp.logical_not(is_top)).astype(jnp.int32),
            on_fold.astype(jnp.int32),
        ]
    ).astype(jnp.int32)
    channels, rows, width = state.shape[1:]
    hidden = w_mid.shape[0]
    inputs = w_in.shape[0]
    fluxes = w_out.shape[1]
    peers, slots = remap_source.shape[3:]
    surface = state.reshape(channels * rows, width)
    goal = target.reshape(channels * rows, width)
    mask = land_mask[0]
    source = remap_source.reshape(peers * slots)
    landing = remap_target.reshape(peers * slots)
    count = remap_count.reshape(peers)
    kernels = remap_weight.reshape(peers * slots, width, width)
    slot_rows = slots * channels

    smem = pl.BlockSpec(memory_space=pltpu.SMEM)
    vmem = pl.BlockSpec(memory_space=pltpu.VMEM)

    outgoing = pl.pallas_call(
        functools.partial(send_kernel, rows, peers, slots),
        name="send",
        out_shape=jax.ShapeDtypeStruct((devices, slot_rows, width), bf16),
        in_specs=[smem, smem, smem, vmem, vmem],
        out_specs=vmem,
        scratch_shapes=[pltpu.VMEM((devices, slot_rows, width), f32)],
    )(meta, source, count, surface, kernels)
    arrived = lax.all_to_all(outgoing, EVERYWHERE, 0, 0, tiled=True)

    def parts(bias):
        high = bias.astype(bf16)
        rest = bias - high.astype(f32)
        middle = rest.astype(bf16)
        low = (rest - middle.astype(f32)).astype(bf16)
        return jnp.stack([high, middle, low], axis=0)

    local_in = jnp.where(comp == 1, jnp.roll(w_in, channels, axis=0), w_in)
    half = jnp.asarray(0.5, bf16)
    w_first = jnp.concatenate(
        [local_in, parts(b_in), jnp.zeros((13, hidden), bf16)], axis=0
    ).T * half
    w_second = w_mid.T * half
    b_second = (b_mid * 0.5)[:, None]
    w_third = jnp.pad(w_out.T, ((0, 16 - fluxes), (0, 0)))
    w_third_back = jnp.pad(w_out * half, ((0, 0), (0, 16 - fluxes)))
    w_second_back = w_mid * half
    w_first_back = local_in

    share = -(-hidden * hidden // (width * devices))
    small_share = -(-24 * hidden // (width * devices))
    packed = -(-(share + small_share) // 8) * 8
    cells = BLOCK_ROWS * width

    new_state, base, diffuse, leaving = pl.pallas_call(
        functools.partial(main_kernel, rows, peers, slots, share, small_share),
        name="main",
        out_shape=(
            jax.ShapeDtypeStruct((channels * rows, width), f32),
            jax.ShapeDtypeStruct((rows, channels, width), f32),
            jax.ShapeDtypeStruct((rows, channels, width), f32),
            jax.ShapeDtypeStruct((devices, slot_rows + packed, width), bf16),
        ),
        in_specs=[smem, smem, smem] + [vmem] * 13,
        out_specs=(vmem,) * 4,
        scratch_shapes=[
            pltpu.VMEM((devices, slot_rows + packed, width), f32),
            pltpu.VMEM((rows, channels, width), f32),
            pltpu.VMEM((32, cells), bf16),
            pltpu.VMEM((hidden + 16, cells), bf16),
            pltpu.VMEM((hidden, cells), bf16),
            pltpu.VMEM((hidden, cells), f32),
            pltpu.VMEM((hidden, cells), f32),
            pltpu.VMEM((hidden, cells), bf16),
            pltpu.VMEM((hidden, cells), bf16),
            pltpu.VMEM((8, cells), f32),
            pltpu.VMEM((16, cells), bf16),
            pltpu.VMEM((16, cells), f32),
            pltpu.VMEM((32, hidden), f32),
            pltpu.VMEM((hidden + 16, hidden), f32),
            pltpu.VMEM((16, hidden), f32),
            pltpu.VMEM((8, width), f32),
            pltpu.VMEM((max(48, small_share * devices), width), f32),
        ],
    )(
        meta,
        landing,
        b_out,
        surface,
        goal,
        mask,
        arrived,
        diffusivity,
        coupling,
        w_first,
        w_second,
        b_second,
        w_third,
        w_third_back,
        w_second_back,
        w_first_back,
    )
    returned = lax.all_to_all(leaving, EVERYWHERE, 0, 0, tiled=True)
    scale = 1.0 / (rows * width * tiles)
    summed = pl.pallas_call(
        functools.partial(sum_kernel, scale),
        name="sum",
        out_shape=jax.ShapeDtypeStruct((devices, packed, width), bf16),
        in_specs=[vmem],
        out_specs=vmem,
    )(returned)
    gathered = lax.all_to_all(summed, EVERYWHERE, 0, 0, tiled=True)
    adjoint = pl.pallas_call(
        functools.partial(back_kernel, rows, peers, slots),
        name="back",
        out_shape=jax.ShapeDtypeStruct((channels * rows, width), f32),
        in_specs=[smem, smem, smem] + [vmem] * 5,
        out_specs=vmem,
        scratch_shapes=[pltpu.VMEM((rows, channels, width), f32)],
    )(meta, source, count, returned, kernels, base, diffuse, diffusivity)
    first, bias_one, second, bias_two, third, bias_three = pl.pallas_call(
        functools.partial(unpack_kernel, share, small_share, fluxes),
        name="unpack",
        out_shape=(
            jax.ShapeDtypeStruct((inputs, hidden), f32),
            jax.ShapeDtypeStruct((1, hidden), f32),
            jax.ShapeDtypeStruct((hidden, hidden), f32),
            jax.ShapeDtypeStruct((1, hidden), f32),
            jax.ShapeDtypeStruct((fluxes, hidden), f32),
            jax.ShapeDtypeStruct((1, width), f32),
        ),
        in_specs=[vmem],
        out_specs=(vmem,) * 6,
        scratch_shapes=[pltpu.VMEM((max(48, small_share * devices), width), f32)],
    )(gathered)
    return (
        new_state.reshape(state.shape),
        adjoint.reshape(state.shape),
        first,
        bias_one[0],
        second,
        bias_two[0],
        third.T,
        bias_three[0, :fluxes],
    )


def solution(mesh):
    tiles = P("comp", None, "gy", "gx")
    placed = (
        tiles,
        tiles,
        P("comp", "gy", "gx"),
        *(P() for _ in range(8)),
        P("comp", "gy", "gx", None, None, None, None),
        P("comp", "gy", "gx", None, None),
        P("comp", "gy", "gx", None, None),
        P("comp", "gy", "gx", None),
    )
    return jax.shard_map(
        shards,
        mesh=mesh,
        in_specs=placed,
        out_specs=(tiles, tiles, *(P() for _ in range(6))),
        check_vma=False,
    )
```

time: 384 us -> 96 us (0.25)
  waiting for transfers between devices: 124 us -> 6.98 us
  matrix products: 105 us -> 0 us
  Pallas kernels: 0 us -> 49.6 us
  starting transfers between devices: 41.2 us -> 11.3 us
  local copies, waits for them, and re-layouts: 38.9 us -> 9.75 us
  blocking collectives: 38.8 us -> 16.3 us
  other arithmetic: 18.7 us -> 0.71 us
  between operations: 14.5 us -> 0.88 us
    psum x1 -> x0, waiting for transfers between devices: 117 us -> none  [shards(): lax.psum((grad_first, bias_first, grad_second, bias_second, grad_third, b...]
    dot_general x93 -> x0, matrix products: 105 us -> none  [the longest x8 21.6 us: advance(): jnp.einsum('ho,on->hn', w_out, flux_cot, preferred_element_type=jnp.float32)]
    pallas_call x0 -> x5, Pallas kernels: none -> 49.6 us  [the longest x1 34.4 us: shards(): pl.pallas_call(functools.partial(main_kernel, rows, peers, slots, share,...]
    psum x1 -> x0, blocking collectives: 38.8 us -> none  [shards(): lax.psum((grad_first, bias_first, grad_second, bias_second, grad_third, b...]
    ppermute x14 -> x0, starting transfers between devices: 27.7 us -> none  [the longest x6 12.7 us: partner(): return lax.ppermute(block, axis, route)]
    all_to_all x0 -> x1, blocking collectives: none -> 16.3 us  [shards(): returned = lax.all_to_all(leaving, EVERYWHERE, 0, 0, tiled=True)]
    ppermute x14 -> x0, waiting for transfers between devices: 7.41 us -> none  [the longest x6 7.38 us: partner(): return lax.ppermute(block, axis, route)]
    all_to_all x2, waiting for transfers between devices: 0.01 us -> 6.98 us  [the longest x1 4.22 us: shards(): arrived = lax.all_to_all(outgoing, EVERYWHERE, 0, 0, tiled=True)]
  transfers between devices with their start and end apart: 17 -> 2, of which waited for: 4 -> 2; matrix products, arithmetic and copies ran while one was open for 11% -> 6% of each run, Pallas kernels for 0% -> 7%
where the time goes in v2:
time: 96 us; the launch traced here: 95.6 us
  Pallas kernels  49.6 us (52%)
  blocking collectives  16.3 us (17%)
  starting transfers between devices  11.3 us (12%)
  local copies, waits for them, and re-layouts  9.75 us (10%)
  waiting for transfers between devices  6.98 us (7%)
    pallas_call x1, Pallas kernels, shards(): pl.pallas_call(functools.partial(main_kernel, rows, peers, slots, share,...  34.4 us
    all_to_all x1, blocking collectives, shards(): returned = lax.all_to_all(leaving, EVERYWHERE, 0, 0, tiled=True)  16.3 us
    all_to_all x1, starting transfers between devices, shards(): arrived = lax.all_to_all(outgoing, EVERYWHERE, 0, 0, tiled=True)  7.33 us
    pallas_call x1, Pallas kernels, shards(): pl.pallas_call(functools.partial(back_kernel, rows, peers, slots), name='...  6.54 us
    pallas_call x1, Pallas kernels, shards(): pl.pallas_call(functools.partial(send_kernel, rows, peers, slots), name='...  5.26 us
    all_to_all x1, waiting for transfers between devices, shards(): arrived = lax.all_to_all(outgoing, EVERYWHERE, 0, 0, tiled=True)  4.22 us
    all_to_all x1, starting transfers between devices, shards(): gathered = lax.all_to_all(summed, EVERYWHERE, 0, 0, tiled=True)  4.01 us
    unnamed x24, local copies, waits for them, and re-layouts  3.13 us
  transfers between devices with their start and end apart: 2, of which 2 were waited for; matrix products, arithmetic and copies ran while one was open for 6% of the time, Pallas kernels for 7%

profile of v2, /device:TPU:0, one launch (start us, length us, event | category | flops | bytes accessed | tf_op | source)
XLA Modules:
  0.0 95.6 jit_solution(7847004034448838563)
XLA Ops:
  0.6 0.0 copy-start.8
  0.6 0.0 copy-start.4
  0.7 0.0 copy-start.5
  0.7 0.0 copy-start.6
  0.7 0.0 copy-start.7
  0.7 0.0 copy-start.9
  0.7 0.0 copy-start.2
  0.8 0.8 copy.37
  1.5 0.6 reshape.43.source
  2.2 0.6 stack.64.meta
  2.7 5.3 %send.1 = bf16[32,32,128]{2,1,0:T(8,128)(2,1)} custom-call(s32[10]{0:T(128)} %stack.64.meta, s32[64]{0:T(128)} %reshape.43.source, s32[16]{0:T(128)} %bitcast.41, f32[1024,128]{1,0:T(8,128)} %bitcast.34, bf16[64,128,128]{2,1,0:T(8,128)(2,1)} %bitcast.32), custom_call_target="tpu_custom_call" | custom-call | tf_op jit(solution)/shard_map/send/pallas_call | solution.py:467
  8.0 7.3 %all-to-all-start = ((bf16[32,32,128]{2,1,0:T(8,128)(2,1)}), bf16[32,32,128]{2,1,0:T(8,128)(2,1)S(1)}, u32[]{:S(2)}, u32[]{:S(2)}) async-start(bf16[32,32,128]{2,1,0:T(8,128)(2,1)} %send.1), calls=%async_computation | async-start | bytes 524288 | tf_op jit(solution)/shard_map/all_to_all | solution.py:475
  15.3 0.0 copy-done.8
  15.4 0.0 copy-done.4
  15.4 0.0 copy-done.5
  15.4 0.1 copy.38
  15.6 0.0 copy-start.3
  15.6 0.1 concatenate.8
  15.8 0.0 copy-done.6
  15.8 0.7 copy.40.couple_ref
  16.5 0.0 copy-done.7
  16.5 0.1 copy.36
  16.6 0.6 reshape.40.landing
  17.2 0.6 pad.8.w_third
  17.8 0.7 copy.41.w_first
  18.5 0.6 pad.9.w_third_back
  19.1 0.0 copy-done.9
  19.1 0.8 copy.43.b_second
  19.9 0.0 copy-done.2
  20.0 0.7 broadcast_multiply_fusion
  20.6 0.7 copy.42.w_second
  21.4 4.2 %all-to-all-done.recv = bf16[32,32,128]{2,1,0:T(8,128)(2,1)S(1)} async-done(((bf16[32,32,128]{2,1,0:T(8,128)(2,1)}), bf16[32,32,128]{2,1,0:T(8,128)(2,1)S(1)}, u32[]{:S(2)}, u32[]{:S(2)}) %all-to-all-start) | async-done | bytes 262176 | tf_op jit(solution)/shard_map/all_to_all | solution.py:475
  25.6 0.0 copy-start
  25.6 0.0 copy-done.3
  25.6 0.7 copy-done
  26.3 34.4 %main.1 = (f32[1024,128]{1,0:T(8,128)}, f32[128,8,128]{2,1,0:T(8,128)}, f32[128,8,128]{2,1,0:T(8,128)}, bf16[32,56,128]{2,1,0:T(8,128)(2,1)}) custom-call(s32[10]{0:T(128)} %stack.64.meta, s32[64]{0:T(128)} %reshape.40.landing, f32[4]{0:T(128)} %b_out.1, f32[1024,128]{1,0:T(8,128)} %bitcast.35, f32[1024,128]{1,0:T(8,128)} %bitcast.36, s32[128,128]{1,0:T(8,128)} %bitcast.38, ...), custom_call_target="tpu_custom_call" | custom-call | tf_op jit(solution)/shard_map/main/pallas_call | solution.py:501
  60.7 16.3 %all_to_all.15.recv = bf16[32,56,128]{2,1,0:T(8,128)(2,1)} all-to-all(bf16[32,56,128]{2,1,0:T(8,128)(2,1)} %get-tuple-element.19), channel_id=1, replica_groups=mesh['comp'=2,'gy'=4,'gx'=4] {'comp','gy','gx'}, dimensions={0} | all-to-all | bytes 917504 | tf_op jit(solution)/shard_map/all_to_all | solution.py:549
  77.0 1.7 %sum.1 = bf16[32,24,128]{2,1,0:T(8,128)(2,1)} custom-call(bf16[32,56,128]{2,1,0:T(8,128)(2,1)} %all_to_all.15.recv), custom_call_target="tpu_custom_call" | custom-call | tf_op jit(solution)/shard_map/sum/pallas_call | solution.py:551
  78.7 4.0 %all-to-all-start.2 = ((bf16[32,24,128]{2,1,0:T(8,128)(2,1)}), bf16[32,24,128]{2,1,0:T(8,128)(2,1)S(1)}, u32[]{:S(2)}, u32[]{:S(2)}) async-start(bf16[32,24,128]{2,1,0:T(8,128)(2,1)} %sum.1), calls=%async_computation.2 | async-start | bytes 393216 | tf_op jit(solution)/shard_map/all_to_all | solution.py:558
  82.8 6.5 %back.1 = f32[1024,128]{1,0:T(8,128)} custom-call(s32[10]{0:T(128)} %stack.64.meta, s32[64]{0:T(128)} %reshape.43.source, s32[16]{0:T(128)} %bitcast.42, bf16[32,56,128]{2,1,0:T(8,128)(2,1)} %all_to_all.15.recv, bf16[64,128,128]{2,1,0:T(8,128)(2,1)} %bitcast.33, f32[128,8,128]{2,1,0:T(8,128)} %get-tuple-element.20.base, ...), custom_call_target="tpu_custom_call" | custom-call | tf_op jit(solution)/shard_map/back/pallas_call | solution.py:559
  89.3 2.8 %all-to-all-done.2.recv = bf16[32,24,128]{2,1,0:T(8,128)(2,1)S(1)} async-done(((bf16[32,24,128]{2,1,0:T(8,128)(2,1)}), bf16[32,24,128]{2,1,0:T(8,128)(2,1)S(1)}, u32[]{:S(2)}, u32[]{:S(2)}) %all-to-all-start.2) | async-done | bytes 196640 | tf_op jit(solution)/shard_map/all_to_all | solution.py:558
  92.1 0.0 copy-start.1
  92.1 0.7 copy-done.1
  92.8 1.7 %unpack.1 = (f32[16,256]{1,0:T(8,128)}, f32[1,256]{1,0:T(1,128)}, f32[256,256]{1,0:T(8,128)}, f32[1,256]{1,0:T(1,128)}, f32[4,256]{1,0:T(4,128)}, /*index=5*/f32[1,128]{1,0:T(1,128)}) custom-call(bf16[32,24,128]{2,1,0:T(8,128)(2,1)} %copy-done.1), custom_call_target="tpu_custom_call" | custom-call | tf_op jit(solution)/shard_map/unpack/pallas_call | solution.py:567
  94.4 1.1 %slice_bitcast_fusion = f32[4]{0:T(128)} fusion(f32[1,128]{1,0:T(1,128)} %get-tuple-element.27), kind=kLoop, calls=%fused_computation.7 | loop fusion | bytes 32 | tf_op jit(solution)/shard_map/squeeze | solution.py:590
  (10 shorter events, 0.1 us)
Async XLA Ops:
  0.6 14.7 %copy-start.8 = (f32[256]{0:T(256)S(1)}, f32[256]{0:T(256)}, u32[]{:S(2)}) copy-start(f32[256]{0:T(256)} %param.21) | copy-start | bytes 3076
  0.6 14.7 %copy-start.4 = (bf16[16,256]{1,0:T(8,128)(2,1)S(1)}, bf16[16,256]{1,0:T(8,128)(2,1)}, u32[]{:S(2)}) copy-start(bf16[16,256]{1,0:T(8,128)(2,1)} %param.20) | copy-start | bytes 24580
  0.7 14.8 %copy-start.5 = (bf16[256,4]{0,1:T(4,128)(2,1)S(1)}, bf16[256,4]{0,1:T(4,128)(2,1)}, u32[]{:S(2)}) copy-start(bf16[256,4]{0,1:T(4,128)(2,1)} %param.24) | copy-start | bytes 6148
  0.7 15.1 %copy-start.6 = (f32[2,8,4]{1,2,0:T(4,128)S(1)}, f32[2,8,4]{1,2,0:T(4,128)}, u32[]{:S(2)}) copy-start(f32[2,8,4]{1,2,0:T(4,128)} %param.19) | copy-start | bytes 772
  0.7 15.8 %copy-start.7 = (s32[1,1,1,16,4]{3,4,2,1,0:T(4,128)S(1)}, s32[1,1,1,16,4]{3,4,2,1,0:T(4,128)}, u32[]{:S(2)}) copy-start(s32[1,1,1,16,4]{3,4,2,1,0:T(4,128)} %param.28) | copy-start | bytes 772
  0.7 18.5 %copy-start.9 = (f32[256]{0:T(256)S(1)}, f32[256]{0:T(256)}, u32[]{:S(2)}) copy-start(f32[256]{0:T(256)} %param.23) | copy-start | bytes 3076
  0.7 19.2 %copy-start.2 = (bf16[256,256]{1,0:T(8,128)(2,1)S(1)}, bf16[256,256]{1,0:T(8,128)(2,1)}, u32[]{:S(2)}) copy-start(bf16[256,256]{1,0:T(8,128)(2,1)} %param.22) | copy-start | bytes 393220
  8.0 17.6 %all-to-all-start = ((bf16[32,32,128]{2,1,0:T(8,128)(2,1)}), bf16[32,32,128]{2,1,0:T(8,128)(2,1)S(1)}, u32[]{:S(2)}, u32[]{:S(2)}) async-start(bf16[32,32,128]{2,1,0:T(8,128)(2,1)} %send.1), calls=%async_computation | async-start | bytes 524288 | tf_op jit(solution)/shard_map/all_to_all | solution.py:475
  15.6 10.0 %copy-start.3 = (bf16[16,256]{1,0:T(8,128)(2,1)}, bf16[16,256]{1,0:T(8,128)(2,1)S(1)}, u32[]{:S(2)}) copy-start(bf16[16,256]{1,0:T(8,128)(2,1)S(1)} %maximum_select_fusion.w_first_back) | copy-start | bytes 24580
  25.6 0.7 copy-start
  78.7 13.3 %all-to-all-start.2 = ((bf16[32,24,128]{2,1,0:T(8,128)(2,1)}), bf16[32,24,128]{2,1,0:T(8,128)(2,1)S(1)}, u32[]{:S(2)}, u32[]{:S(2)}) async-start(bf16[32,24,128]{2,1,0:T(8,128)(2,1)} %sum.1), calls=%async_computation.2 | async-start | bytes 393216 | tf_op jit(solution)/shard_map/all_to_all | solution.py:558
  92.1 0.7 copy-start.1

commit v3 on v2

v3 whole, which is shorter than its diff:
```python
import functools
import math

import jax
import jax.numpy as jnp
from jax import lax
from jax.experimental import pallas as pl
from jax.experimental.pallas import tpu as pltpu
from jax.sharding import PartitionSpec as P

EVERYWHERE = ("comp", "gy", "gx")
BLOCK_ROWS = 8
CHUNK = 256
SUBLANES = 8

OWN, OTHER, WEST, EAST, SOUTH, NORTH, COMP, HAS_SOUTH, HAS_NORTH, ON_FOLD = range(10)

f32 = jnp.float32
bf16 = jnp.bfloat16


def dot(a, b):
    return jnp.dot(a, b, preferred_element_type=f32)


def dot_nt(a, b):
    return lax.dot_general(a, b, (((1,), (1,)), ((), ())), preferred_element_type=f32)


def mirror(tile):
    width = tile.shape[1]
    row = lax.broadcasted_iota(jnp.int32, (width, width), 0)
    col = lax.broadcasted_iota(jnp.int32, (width, width), 1)
    flip = (row + col == width - 1).astype(f32).astype(bf16)
    return dot(tile.astype(bf16), flip)


def put_edges(meta, first, last, bottom, top, stage):
    stage[meta[EAST], 0:SUBLANES, :] = last
    stage[meta[WEST], SUBLANES : 2 * SUBLANES, :] = first
    top = jnp.where(meta[ON_FOLD] == 1, mirror(top), top)
    stage[meta[NORTH], 2 * SUBLANES : 3 * SUBLANES, :] = top
    stage[meta[SOUTH], 3 * SUBLANES : 4 * SUBLANES, :] = bottom


def take_edges(tile, r, lane, sides):
    width = tile.shape[1]
    here = lane == r
    first, last = sides
    first = jnp.where(here, pltpu.roll(tile, r, 1), first)
    last = jnp.where(here, pltpu.roll(tile, lax.rem(r + 1, width), 1), last)
    return first, last


def get_edges(meta, recv):
    west = recv[meta[WEST], 0:32, :].astype(f32)[0:SUBLANES]
    east = recv[meta[EAST], 0:32, :].astype(f32)[SUBLANES : 2 * SUBLANES]
    south = recv[meta[SOUTH], 0:32, :].astype(f32)[2 * SUBLANES : 3 * SUBLANES]
    above = recv[meta[NORTH], 0:32, :].astype(f32)
    north = jnp.where(
        meta[ON_FOLD] == 1,
        above[2 * SUBLANES : 3 * SUBLANES],
        above[3 * SUBLANES : 4 * SUBLANES],
    )
    south = jnp.where(meta[HAS_SOUTH] == 1, south, 0.0)
    north = jnp.where(meta[HAS_NORTH] == 1, north, 0.0)
    return west, east, south, north


def laplace_row(here, below, above, west, east, r, lane):
    width = here.shape[1]
    left = jnp.where(
        lane == 0, pltpu.roll(west, lax.rem(width - r, width), 1), pltpu.roll(here, 1, 1)
    )
    right = jnp.where(
        lane == width - 1, pltpu.roll(east, width - 1 - r, 1), pltpu.roll(here, width - 1, 1)
    )
    return left + right + below + above - 4.0 * here


def column_of(row, comp):
    eye = (
        lax.broadcasted_iota(jnp.int32, (SUBLANES, SUBLANES), 0)
        == lax.broadcasted_iota(jnp.int32, (SUBLANES, SUBLANES), 1)
    ).astype(f32)
    return jnp.sum(
        jnp.broadcast_to(row[pl.ds(comp, 1), :], (SUBLANES, SUBLANES)) * eye,
        axis=1,
        keepdims=True,
    )


def send_kernel(
    rows, peers, slots, meta, source, count, state, kernels, out, by_row, stage, blocks, sems
):
    width = state.shape[1]
    shape = (SUBLANES, width)
    lane = lax.broadcasted_iota(jnp.int32, shape, 1)
    parts = sems.shape[0]
    part = peers // parts
    copies = [
        pltpu.make_async_copy(
            kernels.at[pl.ds(i * part * slots, part * slots)],
            blocks.at[pl.ds(i * part * slots, part * slots)],
            sems.at[i],
        )
        for i in range(parts)
    ]
    for copy in copies:
        copy.start()
    stage[pl.ds(meta[OWN], peers)] = jnp.zeros((peers,) + stage.shape[1:], f32)

    def row_step(r, sides):
        tile = state[pl.ds(r, SUBLANES, stride=rows), :]
        by_row[r] = tile
        return take_edges(tile, r, lane, sides)

    zero = jnp.zeros(shape, f32)
    first, last = lax.fori_loop(0, rows, row_step, (zero, zero), unroll=8)
    put_edges(meta, first, last, by_row[0], by_row[rows - 1], stage)

    def peer_step(q, unused):
        for s in range(slots):
            k = q * slots + s
            picked = by_row[source[s, q]].astype(bf16)
            live = (s < count[q]).astype(f32)
            stage[meta[OTHER] + q, s * SUBLANES : (s + 1) * SUBLANES, :] = (
                dot(picked, blocks[k]) * live
            )
        return unused

    for i in range(parts):
        copies[i].wait()
        lax.fori_loop(i * part, (i + 1) * part, peer_step, 0, unroll=math.gcd(part, 4))
    out[...] = stage[...].astype(bf16)


def weave(*lists):
    keyed = []
    for order, steps in enumerate(lists):
        for i, step in enumerate(steps):
            keyed.append(((i + 0.5) / len(steps), order, i, step))
    for entry in sorted(keyed, key=lambda e: e[:3]):
        entry[3]()


def main_kernel(
    rows,
    peers,
    slots,
    share,
    small_share,
    meta,
    landing,
    b_out,
    state,
    goal,
    mask,
    recv,
    rate_ref,
    couple_ref,
    w_first,
    w_second,
    b_second,
    w_third,
    w_third_back,
    w_second_back,
    w_first_back,
    new_out,
    base_out,
    diffuse_out,
    send_out,
    grad_out,
    stage,
    grad_stage,
    other,
    misfits,
    feats,
    hid_firsts,
    hid_seconds,
    slope_firsts,
    slope_seconds,
    flux_cots,
    cot_second,
    cot_first,
    flux,
    feat_cot,
    g_first,
    g_second,
    g_third,
    g_bias,
    edges,
    small,
):
    width = state.shape[2]
    hidden = w_second.shape[0]
    shape = (SUBLANES, width)
    cells = BLOCK_ROWS * width
    chunks = cells // CHUNK
    lane = lax.broadcasted_iota(jnp.int32, shape, 1)
    sub = lax.broadcasted_iota(jnp.int32, shape, 0)
    fluxes = couple_ref.shape[2]
    pad = BLOCK_ROWS

    other[...] = jnp.zeros(other.shape, f32)

    def land(p, unused):
        block = recv[meta[OTHER] + p, 0:32, :].astype(f32)
        for s in range(slots):
            row = landing[s, p] + pad
            other[row] = other[row] + block[s * SUBLANES : (s + 1) * SUBLANES]
        return unused

    lax.fori_loop(0, peers, land, 0, unroll=2)
    west, east, south, north = get_edges(meta, recv)
    comp = meta[COMP]
    rate = jnp.broadcast_to(column_of(rate_ref, comp), shape)
    pairs = couple_ref[comp]
    couple = [jnp.broadcast_to(pairs[:, f : f + 1], shape) for f in range(fluxes)]
    ones = (lax.broadcasted_iota(jnp.int32, (16, cells), 0) < 3).astype(f32).astype(bf16)
    for ref in (*hid_firsts, *hid_seconds, *flux_cots, *feats):
        ref[...] = jnp.zeros(ref.shape, bf16)
    for ref in (*slope_firsts, *slope_seconds):
        ref[...] = jnp.zeros(ref.shape, f32)
    for ref in feats:
        ref[16:32, :] = ones
    for ref in hid_firsts:
        ref[hidden : hidden + 16, :] = ones
    for ref in (g_first, g_second, g_third, g_bias, edges):
        ref[...] = jnp.zeros(ref.shape, f32)
    bias = jnp.broadcast_to(b_second[...], (hidden, CHUNK))
    b_third = jnp.zeros(shape, f32)
    for f in range(fluxes):
        b_third = jnp.where(sub == f, b_out[f], b_third)

    def forward(block, feat, hid_first, hid_second, slope_first, slope_second, flux_cot):
        start = block * BLOCK_ROWS

        def take(i):
            at = pl.ds(i * width, width)
            r = start + i
            feat[0:16, at] = jnp.concatenate([state[r], other[r + pad]], axis=0).astype(bf16)

        def layer(net, hid_ref, slope_ref, at):
            turn = jnp.tanh(net)
            up = 1.0 + turn
            hid = net * up
            hid_ref[0:hidden, at] = hid.astype(bf16)
            slope_ref[:, at] = (up + hid) - hid * turn

        def first(j):
            at = pl.ds(j * CHUNK, CHUNK)
            layer(dot(w_first[...], feat[:, at]), hid_first, slope_first, at)

        def second(j):
            at = pl.ds(j * CHUNK, CHUNK)
            net = dot(w_second[...], hid_first[0:hidden, at]) + bias
            layer(net, hid_second, slope_second, at)

        def third(j):
            at = pl.ds(j * CHUNK, CHUNK)
            flux[:, at] = dot(w_third[...], hid_second[:, at])[0:SUBLANES]

        def fields(i):
            at = pl.ds(i * width, width)
            r = start + i
            here = state[r]
            below = jnp.where(r > 0, state[jnp.maximum(r - 1, 0)], south)
            above = jnp.where(r < rows - 1, state[jnp.minimum(r + 1, rows - 1)], north)
            lap = laplace_row(here, below, above, west, east, r, lane)
            wet = jnp.broadcast_to(mask[pl.ds(r, 1), :].astype(f32), shape)
            spread_mask = jnp.where(comp == 1, wet, 1.0)
            wet_flux = (flux[:, at] + b_third) * wet
            updated = here + rate * spread_mask * lap
            for f in range(fluxes):
                updated = updated + couple[f] * jnp.broadcast_to(wet_flux[f : f + 1], shape)
            new_out[pl.ds(r, SUBLANES, stride=rows), :] = updated
            misfit = updated - goal[pl.ds(r, SUBLANES, stride=rows), :]
            diffuse = spread_mask * misfit
            diffuse_out[r] = diffuse
            edges[0], edges[1] = take_edges(diffuse, r, lane, (edges[0], edges[1]))
            misfits[r + pad] = misfit
            pulled = jnp.zeros(shape, f32)
            for f in range(fluxes):
                total = jnp.sum(couple[f] * misfit, axis=0, keepdims=True)
                pulled = jnp.where(sub == f, jnp.broadcast_to(total, shape), pulled)
            pulled = (pulled * wet).astype(bf16)
            flux_cot[0:SUBLANES, at] = pulled
            g_bias[...] = g_bias[...] + pulled.astype(f32)

        steps = [functools.partial(take, i) for i in range(BLOCK_ROWS)]
        for stage_step in (first, second, third):
            steps += [functools.partial(stage_step, j) for j in range(chunks)]
        return steps + [functools.partial(fields, i) for i in range(BLOCK_ROWS)]

    def backward(block, feat, hid_first, hid_second, slope_first, slope_second, flux_cot):
        start = block * BLOCK_ROWS

        def second(j):
            at = pl.ds(j * CHUNK, CHUNK)
            net = dot(w_third_back[...], flux_cot[:, at])
            cot_second[:, at] = (net * slope_second[:, at]).astype(bf16)

        def first(j):
            at = pl.ds(j * CHUNK, CHUNK)
            net = dot(w_second_back[...], cot_second[:, at])
            cot_first[:, at] = (net * slope_first[:, at]).astype(bf16)

        def inputs(j):
            at = pl.ds(j * CHUNK, CHUNK)
            feat_cot[:, at] = dot(w_first_back[...], cot_first[:, at])

        def leave(i):
            at = pl.ds(i * width, width)
            r = start + i + pad
            base_out[r] = misfits[r] + feat_cot[0:SUBLANES, at]
            other[r] = feat_cot[SUBLANES : 2 * SUBLANES, at]

        def grad_second():
            g_second[...] += dot_nt(hid_first[...], cot_second[...])

        def grad_third():
            g_third[...] += dot_nt(flux_cot[...], hid_second[...])

        def grad_first():
            g_first[...] += dot_nt(feat[...], cot_first[...])

        steps = [functools.partial(second, j) for j in range(chunks)]
        steps += [functools.partial(first, j) for j in range(chunks)]
        steps += [grad_third, grad_second]
        steps += [functools.partial(inputs, j) for j in range(chunks)]
        steps += [grad_first]
        return steps + [functools.partial(leave, i) for i in range(BLOCK_ROWS)]

    sets = list(
        zip(feats, hid_firsts, hid_seconds, slope_firsts, slope_seconds, flux_cots, strict=True)
    )
    blocks = rows // BLOCK_ROWS

    def pair_step(pair, unused):
        even = pair * 2
        weave(backward(even - 1, *sets[1]), forward(even, *sets[0]))
        weave(backward(even, *sets[0]), forward(even + 1, *sets[1]))
        return unused

    lax.fori_loop(0, blocks // 2, pair_step, 0)
    weave(backward(blocks - 1, *sets[1]))

    stage[pl.ds(meta[OWN], peers)] = jnp.zeros((peers,) + stage.shape[1:], f32)

    def leave(p, unused):
        for s in range(slots):
            row = landing[s, p] + pad
            stage[meta[OTHER] + p, s * SUBLANES : (s + 1) * SUBLANES, :] = other[row]
        return unused

    lax.fori_loop(0, peers, leave, 0, unroll=2)
    put_edges(meta, edges[0], edges[1], diffuse_out[0], diffuse_out[rows - 1], stage)
    send_out[...] = stage[...].astype(bf16)

    devices = stage.shape[0]
    halves = hidden // width
    inputs = 2 * SUBLANES
    small[...] = jnp.zeros(small.shape, f32)
    low, high = g_first[0:SUBLANES, :], g_first[SUBLANES:inputs, :]
    low, high = jnp.where(comp == 1, high, low), jnp.where(comp == 1, low, high)
    bias_sum = jnp.sum(g_bias[...], axis=1, keepdims=True)
    bias_row = jnp.sum(jnp.where(sub == lane, jnp.broadcast_to(bias_sum, shape), 0.0), axis=0,
                       keepdims=True)
    for h in range(halves):
        cols = slice(h * width, (h + 1) * width)
        top = h * 24
        small[top : top + 8, :] = low[:, cols]
        small[top + 8 : top + 16, :] = high[:, cols]
        small[top + 16 : top + 17, :] = g_first[inputs : inputs + 1, cols]
        small[top + 17 : top + 18, :] = g_second[hidden : hidden + 1, cols]
        if h == 0:
            small[top + 18 : top + 19, :] = bias_row
        small[top + 19 : top + 19 + fluxes, :] = g_third[0:fluxes, cols]
    for d in range(devices):
        done = 0
        while done < share:
            at = d * share + done
            h, row = divmod(at, hidden)
            step = min(share - done, hidden - row)
            if h < halves:
                grad_stage[d, done : done + step, :] = g_second[
                    row : row + step, h * width : (h + 1) * width
                ]
            done += step
        piece = small[d * small_share : (d + 1) * small_share, :]
        head = piece.astype(bf16).astype(f32)
        grad_stage[d, share : share + small_share, :] = head
        grad_stage[d, share + small_share : share + 2 * small_share, :] = piece - head
    grad_out[...] = grad_stage[...].astype(bf16)


def sum_kernel(scale, share, small_share, recv, out, stage):
    devices = recv.shape[0]
    total = recv[0].astype(f32)
    for d in range(1, devices):
        total = total + recv[d].astype(f32)
    stage[...] = total * scale
    low = slice(share + small_share, share + 2 * small_share)
    piece = stage[share : share + small_share, :] + stage[low, :]
    head = piece.astype(bf16).astype(f32)
    stage[share : share + small_share, :] = head
    stage[low, :] = piece - head
    total = stage[...].astype(bf16)
    for d in range(devices):
        out[d] = total


def back_kernel(
    rows, peers, slots, meta, source, count, recv, kernels, base, diffuse, rate_ref, out, total
):
    width = diffuse.shape[2]
    shape = (SUBLANES, width)
    lane = lax.broadcasted_iota(jnp.int32, shape, 1)
    west, east, south, north = get_edges(meta, recv)
    comp = meta[COMP]
    rate = jnp.broadcast_to(column_of(rate_ref, comp), shape)

    def lap_step(r, unused):
        here = diffuse[r]
        below = jnp.where(r > 0, diffuse[jnp.maximum(r - 1, 0)], south)
        above = jnp.where(r < rows - 1, diffuse[jnp.minimum(r + 1, rows - 1)], north)
        total[r] = base[r + BLOCK_ROWS] + rate * laplace_row(here, below, above, west, east, r, lane)
        return unused

    lax.fori_loop(0, rows, lap_step, 0, unroll=8)

    def peer_step(q, unused):
        block = recv[meta[OTHER] + q, 0:32, :].astype(f32)
        for s in range(slots):
            k = q * slots + s
            sent = block[s * SUBLANES : (s + 1) * SUBLANES].astype(bf16)
            live = (s < count[q]).astype(f32)
            row = source[s, q]
            total[row] = total[row] + dot_nt(sent, kernels[k]) * live
        return unused

    lax.fori_loop(0, peers, peer_step, 0, unroll=4)

    def out_step(r, unused):
        out[pl.ds(r, SUBLANES, stride=rows), :] = total[r]
        return unused

    lax.fori_loop(0, rows, out_step, 0, unroll=8)


def unpack_kernel(share, small_share, fluxes, recv, first, bias_one, second, bias_two, third,
                  bias_three, small):
    devices = recv.shape[0]
    width = recv.shape[2]
    hidden = second.shape[0]
    halves = hidden // width
    for d in range(devices):
        block = recv[d].astype(f32)
        done = 0
        while done < share:
            at = d * share + done
            h, row = divmod(at, hidden)
            step = min(share - done, hidden - row)
            if h < halves:
                second[row : row + step, h * width : (h + 1) * width] = block[done : done + step]
            done += step
        small[d * small_share : (d + 1) * small_share, :] = (
            block[share : share + small_share]
            + block[share + small_share : share + 2 * small_share]
        )
    for h in range(halves):
        cols = slice(h * width, (h + 1) * width)
        top = h * 24
        first[:, cols] = small[top : top + 16, :]
        bias_one[:, cols] = small[top + 16 : top + 17, :]
        bias_two[:, cols] = small[top + 17 : top + 18, :]
        third[:, cols] = small[top + 19 : top + 19 + fluxes, :]
    bias_three[...] = small[18:19, 0:fluxes]


def shards(
    state,
    target,
    land_mask,
    diffusivity,
    coupling,
    w_in,
    b_in,
    w_mid,
    b_mid,
    w_out,
    b_out,
    remap_weight,
    remap_source,
    remap_target,
    remap_count,
):
    n_gy, n_gx = lax.axis_size("gy"), lax.axis_size("gx")
    tiles = n_gy * n_gx
    devices = 2 * tiles
    comp, row, col = (lax.axis_index(axis) for axis in EVERYWHERE)
    own, other = comp * tiles, (1 - comp) * tiles
    is_top = row == n_gy - 1
    on_fold = jnp.logical_and(comp == 1, is_top)
    line = own + row * n_gx
    here = line + col
    meta = jnp.stack(
        [
            own,
            other,
            line + (col + n_gx - 1) % n_gx,
            line + (col + 1) % n_gx,
            jnp.where(row > 0, here - n_gx, here),
            jnp.where(on_fold, line + n_gx - 1 - col, jnp.where(is_top, here, here + n_gx)),
            comp,
            (row > 0).astype(jnp.int32),
            jnp.logical_or(on_fold, jnp.logical_not(is_top)).astype(jnp.int32),
            on_fold.astype(jnp.int32),
        ]
    ).astype(jnp.int32)
    channels, rows, width = state.shape[1:]
    hidden = w_mid.shape[0]
    inputs = w_in.shape[0]
    fluxes = w_out.shape[1]
    peers, slots = remap_source.shape[3:]
    surface = state.reshape(channels * rows, width)
    goal = target.reshape(channels * rows, width)
    mask = land_mask[0]
    source = remap_source.reshape(peers, slots).T
    landing = remap_target.reshape(peers, slots).T
    count = remap_count.reshape(peers)
    kernels = remap_weight.reshape(peers * slots, width, width)
    slot_rows = slots * channels

    smem = pl.BlockSpec(memory_space=pltpu.SMEM)
    vmem = pl.BlockSpec(memory_space=pltpu.VMEM)

    anywhere = pl.BlockSpec(memory_space=pl.ANY)
    parts = math.gcd(peers, 4)
    outgoing, by_row = pl.pallas_call(
        functools.partial(send_kernel, rows, peers, slots),
        name="send",
        out_shape=(
            jax.ShapeDtypeStruct((devices, slot_rows, width), bf16),
            jax.ShapeDtypeStruct((rows, channels, width), f32),
        ),
        in_specs=[smem, smem, smem, vmem, anywhere],
        out_specs=(vmem, vmem),
        scratch_shapes=[
            pltpu.VMEM((devices, slot_rows, width), f32),
            pltpu.VMEM(kernels.shape, bf16),
            pltpu.SemaphoreType.DMA((parts,)),
        ],
    )(meta, source, count, surface, kernels)
    arrived = lax.all_to_all(outgoing, EVERYWHERE, 0, 0, tiled=True)

    def pieces(bias):
        high = bias.astype(bf16)
        rest = bias - high.astype(f32)
        middle = rest.astype(bf16)
        low = (rest - middle.astype(f32)).astype(bf16)
        return jnp.stack([high, middle, low], axis=0)

    local_in = jnp.where(comp == 1, jnp.roll(w_in, channels, axis=0), w_in)
    half = jnp.asarray(0.5, bf16)
    w_first = jnp.concatenate(
        [local_in, pieces(b_in), jnp.zeros((13, hidden), bf16)], axis=0
    ).T * half
    w_second = w_mid.T * half
    b_second = (b_mid * 0.5)[:, None]
    w_third = jnp.pad(w_out.T, ((0, 16 - fluxes), (0, 0)))
    w_third_back = jnp.pad(w_out * half, ((0, 0), (0, 16 - fluxes)))
    w_second_back = w_mid * half
    w_first_back = local_in

    share = -(-hidden * hidden // (width * devices))
    small_share = -(-24 * hidden // (width * devices))
    packed = -(-(share + 2 * small_share) // 8) * 8
    cells = BLOCK_ROWS * width

    def twice(*args):
        return (pltpu.VMEM(*args), pltpu.VMEM(*args))

    tall = (rows + BLOCK_ROWS, channels, width)
    new_state, base, diffuse, leaving, gradients = pl.pallas_call(
        functools.partial(main_kernel, rows, peers, slots, share, small_share),
        name="main",
        out_shape=(
            jax.ShapeDtypeStruct((channels * rows, width), f32),
            jax.ShapeDtypeStruct(tall, f32),
            jax.ShapeDtypeStruct((rows, channels, width), f32),
            jax.ShapeDtypeStruct((devices, slot_rows, width), bf16),
            jax.ShapeDtypeStruct((devices, packed, width), bf16),
        ),
        in_specs=[smem, smem, smem] + [vmem] * 13,
        out_specs=(vmem,) * 5,
        scratch_shapes=[
            pltpu.VMEM((devices, slot_rows, width), f32),
            pltpu.VMEM((devices, packed, width), f32),
            pltpu.VMEM(tall, f32),
            pltpu.VMEM(tall, f32),
            twice((32, cells), bf16),
            twice((hidden + 16, cells), bf16),
            twice((hidden, cells), bf16),
            twice((hidden, cells), f32),
            twice((hidden, cells), f32),
            twice((16, cells), bf16),
            pltpu.VMEM((hidden, cells), bf16),
            pltpu.VMEM((hidden, cells), bf16),
            pltpu.VMEM((8, cells), f32),
            pltpu.VMEM((16, cells), f32),
            pltpu.VMEM((32, hidden), f32),
            pltpu.VMEM((hidden + 16, hidden), f32),
            pltpu.VMEM((16, hidden), f32),
            pltpu.VMEM((8, width), f32),
            pltpu.VMEM((2, 8, width), f32),
            pltpu.VMEM((max(48, small_share * devices), width), f32),
        ],
    )(
        meta,
        landing,
        b_out,
        by_row,
        goal,
        mask,
        arrived,
        diffusivity,
        coupling,
        w_first,
        w_second,
        b_second,
        w_third,
        w_third_back,
        w_second_back,
        w_first_back,
    )
    gradients = lax.all_to_all(gradients, EVERYWHERE, 0, 0, tiled=True)
    returned = lax.all_to_all(leaving, EVERYWHERE, 0, 0, tiled=True)
    scale = 1.0 / (rows * width * tiles)
    summed = pl.pallas_call(
        functools.partial(sum_kernel, scale, share, small_share),
        name="sum",
        out_shape=jax.ShapeDtypeStruct((devices, packed, width), bf16),
        in_specs=[vmem],
        out_specs=vmem,
        scratch_shapes=[pltpu.VMEM((packed, width), f32)],
    )(gradients)
    gathered = lax.all_to_all(summed, EVERYWHERE, 0, 0, tiled=True)
    adjoint = pl.pallas_call(
        functools.partial(back_kernel, rows, peers, slots),
        name="back",
        out_shape=jax.ShapeDtypeStruct((channels * rows, width), f32),
        in_specs=[smem, smem, smem] + [vmem] * 5,
        out_specs=vmem,
        scratch_shapes=[pltpu.VMEM((rows, channels, width), f32)],
    )(meta, source, count, returned, kernels, base, diffuse, diffusivity)
    first, bias_one, second, bias_two, third, bias_three = pl.pallas_call(
        functools.partial(unpack_kernel, share, small_share, fluxes),
        name="unpack",
        out_shape=(
            jax.ShapeDtypeStruct((inputs, hidden), f32),
            jax.ShapeDtypeStruct((1, hidden), f32),
            jax.ShapeDtypeStruct((hidden, hidden), f32),
            jax.ShapeDtypeStruct((1, hidden), f32),
            jax.ShapeDtypeStruct((fluxes, hidden), f32),
            jax.ShapeDtypeStruct((1, fluxes), f32),
        ),
        in_specs=[vmem],
        out_specs=(vmem,) * 6,
        scratch_shapes=[pltpu.VMEM((max(48, small_share * devices), width), f32)],
    )(gathered)
    return (
        new_state.reshape(state.shape),
        adjoint.reshape(state.shape),
        first,
        bias_one[0],
        second,
        bias_two[0],
        third.T,
        bias_three[0],
    )


def solution(mesh):
    tiles = P("comp", None, "gy", "gx")
    placed = (
        tiles,
        tiles,
        P("comp", "gy", "gx"),
        *(P() for _ in range(8)),
        P("comp", "gy", "gx", None, None, None, None),
        P("comp", "gy", "gx", None, None),
        P("comp", "gy", "gx", None, None),
        P("comp", "gy", "gx", None),
    )
    return jax.shard_map(
        shards,
        mesh=mesh,
        in_specs=placed,
        out_specs=(tiles, tiles, *(P() for _ in range(6))),
        check_vma=False,
    )
```

time: 96 us -> 91.4 us (0.952)
  waiting for transfers between devices: 6.98 us -> 16.3 us
  Pallas kernels: 49.6 us -> 41.3 us
  blocking collectives: 16.3 us -> 12.6 us
  local copies, waits for them, and re-layouts: 9.75 us -> 6.57 us
  starting transfers between devices: 11.3 us -> 12.5 us
    all_to_all x0 -> x1, waiting for transfers between devices: none -> 8.6 us  [shards(): returned = lax.all_to_all(leaving, EVERYWHERE, 0, 0, tiled=True)]
    pallas_call x1, Pallas kernels: 34.4 us -> 26.9 us  [shards(): pl.pallas_call(functools.partial(main_kernel, rows, peers, slots, share,...]
    all_to_all x1, blocking collectives: 16.3 us -> 12.6 us  [shards(): gradients = lax.all_to_all(gradients, EVERYWHERE, 0, 0, tiled=True)]
    all_to_all x0 -> x1, starting transfers between devices: none -> 2.58 us  [shards(): returned = lax.all_to_all(leaving, EVERYWHERE, 0, 0, tiled=True)]
    all_to_all x1, starting transfers between devices: 4.01 us -> 2.59 us  [shards(): gathered = lax.all_to_all(summed, EVERYWHERE, 0, 0, tiled=True)]
    reshape x2 -> x0, local copies, waits for them, and re-layouts: 1.21 us -> none  [the longest x1 0.61 us: shards(): source = remap_source.reshape(peers * slots)]
    squeeze x1 -> x0, local copies, waits for them, and re-layouts: 1.15 us -> none  [shards(): bias_three[0, :fluxes]]
    unnamed x24 -> x22, local copies, waits for them, and re-layouts: 3.13 us -> 2.22 us
  transfers between devices with their start and end apart: 2 -> 3, of which waited for: 2 -> 3; matrix products, arithmetic and copies ran while one was open for 6% -> 6% of each run, Pallas kernels for 7% -> 9%
where the time goes in v3:
time: 91.4 us; the launch traced here: 90.9 us
  Pallas kernels  41.3 us (45%)
  waiting for transfers between devices  16.3 us (18%)
  blocking collectives  12.6 us (14%)
  starting transfers between devices  12.5 us (14%)
  local copies, waits for them, and re-layouts  6.57 us (7%)
    pallas_call x1, Pallas kernels, shards(): pl.pallas_call(functools.partial(main_kernel, rows, peers, slots, share,...  26.9 us
    all_to_all x1, blocking collectives, shards(): gradients = lax.all_to_all(gradients, EVERYWHERE, 0, 0, tiled=True)  12.6 us
    all_to_all x1, waiting for transfers between devices, shards(): returned = lax.all_to_all(leaving, EVERYWHERE, 0, 0, tiled=True)  8.6 us
    all_to_all x1, starting transfers between devices, shards(): arrived = lax.all_to_all(outgoing, EVERYWHERE, 0, 0, tiled=True)  7.33 us
    pallas_call x1, Pallas kernels, shards(): pl.pallas_call(functools.partial(back_kernel, rows, peers, slots), name='...  6.5 us
    all_to_all x1, waiting for transfers between devices, shards(): arrived = lax.all_to_all(outgoing, EVERYWHERE, 0, 0, tiled=True)  4.94 us
    pallas_call x1, Pallas kernels, shards(): pl.pallas_call(functools.partial(send_kernel, rows, peers, slots), name='...  4.56 us
    all_to_all x1, waiting for transfers between devices, shards(): gathered = lax.all_to_all(summed, EVERYWHERE, 0, 0, tiled=True)  2.79 us
  transfers between devices with their start and end apart: 3, of which 3 were waited for; matrix products, arithmetic and copies ran while one was open for 6% of the time, Pallas kernels for 9%

profile of v3, /device:TPU:0, one launch (start us, length us, event | category | flops | bytes accessed | tf_op | source)
XLA Modules:
  0.0 90.9 jit_solution(4896708020122803453)
XLA Ops:
  0.6 0.0 copy-start.8
  0.6 0.0 copy-start.5
  0.7 0.0 copy-start.6
  0.7 0.0 copy-start.7
  0.7 0.0 copy-start.9
  0.7 0.0 copy-start.3
  0.7 0.7 stack.64.meta
  1.4 4.6 %send.1 = (bf16[32,32,128]{2,1,0:T(8,128)(2,1)}, f32[128,8,128]{2,1,0:T(8,128)}) custom-call(s32[10]{0:T(128)} %stack.64.meta, s32[4,16]{1,0:T(4,128)} %bitcast.40, s32[16]{0:T(128)} %bitcast.44, f32[1024,128]{1,0:T(8,128)} %bitcast.36, bf16[64,128,128]{2,1,0:T(8,128)(2,1)} %bitcast.33), custom_call_target="tpu_custom_call" | custom-call | tf_op jit(solution)/shard_map/send/pallas_call | solution.py:541
  6.0 7.3 %all-to-all-start = ((bf16[32,32,128]{2,1,0:T(8,128)(2,1)}), bf16[32,32,128]{2,1,0:T(8,128)(2,1)S(1)}, u32[]{:S(2)}, u32[]{:S(2)}) async-start(bf16[32,32,128]{2,1,0:T(8,128)(2,1)} %get-tuple-element.22), calls=%async_computation | async-start | bytes 524288 | tf_op jit(solution)/shard_map/all_to_all | solution.py:556
  13.3 0.0 copy-done.8
  13.4 0.0 copy-done.5
  13.4 0.0 copy-done.6
  13.4 0.1 copy.32
  13.6 0.0 copy-start.4
  13.6 0.1 concatenate.8
  13.8 0.0 copy-done.7
  13.8 0.7 copy.34.couple_ref
  14.5 0.6 pad.8.w_third
  15.1 0.7 copy.35.w_first
  15.8 0.6 pad.9.w_third_back
  16.4 0.0 copy-done.9
  16.4 0.8 copy.37.b_second
  17.2 0.0 copy-done.3
  17.2 0.7 broadcast_multiply_fusion
  17.9 0.8 copy.36.w_second
  18.6 4.9 %all-to-all-done.recv = bf16[32,32,128]{2,1,0:T(8,128)(2,1)S(1)} async-done(((bf16[32,32,128]{2,1,0:T(8,128)(2,1)}), bf16[32,32,128]{2,1,0:T(8,128)(2,1)S(1)}, u32[]{:S(2)}, u32[]{:S(2)}) %all-to-all-start) | async-done | bytes 262176 | tf_op jit(solution)/shard_map/all_to_all | solution.py:556
  23.6 0.0 copy-start.1
  23.6 0.0 copy-done.4
  23.6 0.7 copy-done.1
  24.3 26.9 %main.1 = (f32[1024,128]{1,0:T(8,128)}, f32[136,8,128]{2,1,0:T(8,128)}, f32[128,8,128]{2,1,0:T(8,128)}, bf16[32,32,128]{2,1,0:T(8,128)(2,1)}, bf16[32,24,128]{2,1,0:T(8,128)(2,1)}) custom-call(s32[10]{0:T(128)} %stack.64.meta, s32[4,16]{1,0:T(4,128)} %bitcast.43, f32[4]{0:T(128)} %b_out.1, f32[128,8,128]{2,1,0:T(8,128)} %get-tuple-element.21.state, ...), custom_call_target="tpu_custom_call" | custom-call | tf_op jit(solution)/shard_map/main/pallas_call | solution.py:586
  51.2 12.6 %all_to_all.20.recv = bf16[32,24,128]{2,1,0:T(8,128)(2,1)} all-to-all(bf16[32,24,128]{2,1,0:T(8,128)(2,1)} %get-tuple-element.27), channel_id=1, replica_groups=mesh['comp'=2,'gy'=4,'gx'=4] {'comp','gy','gx'}, dimensions={0} | all-to-all | bytes 393216 | tf_op jit(solution)/shard_map/all_to_all | solution.py:638
  63.8 2.6 %all-to-all-start.1 = ((bf16[32,32,128]{2,1,0:T(8,128)(2,1)}), bf16[32,32,128]{2,1,0:T(8,128)(2,1)S(1)}, u32[]{:S(2)}, u32[]{:S(2)}) async-start(bf16[32,32,128]{2,1,0:T(8,128)(2,1)} %get-tuple-element.24), calls=%async_computation.1 | async-start | bytes 524288 | tf_op jit(solution)/shard_map/all_to_all | solution.py:639
  66.4 1.7 %sum.1 = bf16[32,24,128]{2,1,0:T(8,128)(2,1)} custom-call(bf16[32,24,128]{2,1,0:T(8,128)(2,1)} %all_to_all.20.recv), custom_call_target="tpu_custom_call" | custom-call | tf_op jit(solution)/shard_map/sum/pallas_call | solution.py:641
  68.1 8.6 %all-to-all-done.1.recv = bf16[32,32,128]{2,1,0:T(8,128)(2,1)S(1)} async-done(((bf16[32,32,128]{2,1,0:T(8,128)(2,1)}), bf16[32,32,128]{2,1,0:T(8,128)(2,1)S(1)}, u32[]{:S(2)}, u32[]{:S(2)}) %all-to-all-start.1) | async-done | bytes 262176 | tf_op jit(solution)/shard_map/all_to_all | solution.py:639
  76.7 0.0 copy-start
  76.7 2.6 %all-to-all-start.3 = ((bf16[32,24,128]{2,1,0:T(8,128)(2,1)}), bf16[32,24,128]{2,1,0:T(8,128)(2,1)S(1)}, u32[]{:S(2)}, u32[]{:S(2)}) async-start(bf16[32,24,128]{2,1,0:T(8,128)(2,1)} %sum.1), calls=%async_computation.3 | async-start | bytes 393216 | tf_op jit(solution)/shard_map/all_to_all | solution.py:649
  79.3 0.0 copy-done
  79.3 6.5 %back.1 = f32[1024,128]{1,0:T(8,128)} custom-call(s32[10]{0:T(128)} %stack.64.meta, s32[4,16]{1,0:T(4,128)} %bitcast.41, s32[16]{0:T(128)} %bitcast.45, bf16[32,32,128]{2,1,0:T(8,128)(2,1)} %copy-done, bf16[64,128,128]{2,1,0:T(8,128)(2,1)} %bitcast.34, f32[136,8,128]{2,1,0:T(8,128)} %get-tuple-element.25.base, f32[128,8,128]{2,1,0:T(8,128)} %get-tuple-element.26.diffuse, ...), custom_call_target="tpu_custom_call" | custom-call | tf_op jit(solution)/shard_map/back/pallas_call | solution.py:650
  85.8 2.8 %all-to-all-done.3.recv = bf16[32,24,128]{2,1,0:T(8,128)(2,1)S(1)} async-done(((bf16[32,24,128]{2,1,0:T(8,128)(2,1)}), bf16[32,24,128]{2,1,0:T(8,128)(2,1)S(1)}, u32[]{:S(2)}, u32[]{:S(2)}) %all-to-all-start.3) | async-done | bytes 196640 | tf_op jit(solution)/shard_map/all_to_all | solution.py:649
  88.6 0.0 copy-start.2
  88.6 0.7 copy-done.2
  89.2 1.7 %unpack.1 = (f32[16,256]{1,0:T(8,128)}, f32[1,256]{1,0:T(1,128)}, f32[256,256]{1,0:T(8,128)}, f32[1,256]{1,0:T(1,128)}, f32[4,256]{1,0:T(4,128)}, /*index=5*/f32[1,4]{1,0:T(1,128)}) custom-call(bf16[32,24,128]{2,1,0:T(8,128)(2,1)} %copy-done.2), custom_call_target="tpu_custom_call" | custom-call | tf_op jit(solution)/shard_map/unpack/pallas_call | solution.py:658
  (10 shorter events, 0.1 us)
Async XLA Ops:
  0.6 12.7 %copy-start.8 = (f32[256]{0:T(256)S(1)}, f32[256]{0:T(256)}, u32[]{:S(2)}) copy-start(f32[256]{0:T(256)} %param.21) | copy-start | bytes 3076
  0.6 12.7 %copy-start.5 = (bf16[16,256]{1,0:T(8,128)(2,1)S(1)}, bf16[16,256]{1,0:T(8,128)(2,1)}, u32[]{:S(2)}) copy-start(bf16[16,256]{1,0:T(8,128)(2,1)} %param.20) | copy-start | bytes 24580
  0.7 12.7 %copy-start.6 = (bf16[256,4]{0,1:T(4,128)(2,1)S(1)}, bf16[256,4]{0,1:T(4,128)(2,1)}, u32[]{:S(2)}) copy-start(bf16[256,4]{0,1:T(4,128)(2,1)} %param.24) | copy-start | bytes 6148
  0.7 13.1 %copy-start.7 = (f32[2,8,4]{1,2,0:T(4,128)S(1)}, f32[2,8,4]{1,2,0:T(4,128)}, u32[]{:S(2)}) copy-start(f32[2,8,4]{1,2,0:T(4,128)} %param.19) | copy-start | bytes 772
  0.7 15.7 %copy-start.9 = (f32[256]{0:T(256)S(1)}, f32[256]{0:T(256)}, u32[]{:S(2)}) copy-start(f32[256]{0:T(256)} %param.23) | copy-start | bytes 3076
  0.7 16.5 %copy-start.3 = (bf16[256,256]{1,0:T(8,128)(2,1)S(1)}, bf16[256,256]{1,0:T(8,128)(2,1)}, u32[]{:S(2)}) copy-start(bf16[256,256]{1,0:T(8,128)(2,1)} %param.22) | copy-start | bytes 393220
  6.0 17.6 %all-to-all-start = ((bf16[32,32,128]{2,1,0:T(8,128)(2,1)}), bf16[32,32,128]{2,1,0:T(8,128)(2,1)S(1)}, u32[]{:S(2)}, u32[]{:S(2)}) async-start(bf16[32,32,128]{2,1,0:T(8,128)(2,1)} %get-tuple-element.22), calls=%async_computation | async-start | bytes 524288 | tf_op jit(solution)/shard_map/all_to_all | solution.py:556
  13.6 10.0 %copy-start.4 = (bf16[16,256]{1,0:T(8,128)(2,1)}, bf16[16,256]{1,0:T(8,128)(2,1)S(1)}, u32[]{:S(2)}) copy-start(bf16[16,256]{1,0:T(8,128)(2,1)S(1)} %maximum_select_fusion.w_first_back) | copy-start | bytes 24580
  23.6 0.7 copy-start.1
  63.8 12.9 %all-to-all-start.1 = ((bf16[32,32,128]{2,1,0:T(8,128)(2,1)}), bf16[32,32,128]{2,1,0:T(8,128)(2,1)S(1)}, u32[]{:S(2)}, u32[]{:S(2)}) async-start(bf16[32,32,128]{2,1,0:T(8,128)(2,1)} %get-tuple-element.24), calls=%async_computation.1 | async-start | bytes 524288 | tf_op jit(solution)/shard_map/all_to_all | solution.py:639
  76.7 2.6 %copy-start = (bf16[32,32,128]{2,1,0:T(8,128)(2,1)}, bf16[32,32,128]{2,1,0:T(8,128)(2,1)S(1)}, u32[]{:S(2)}) copy-start(bf16[32,32,128]{2,1,0:T(8,128)(2,1)S(1)} %all-to-all-done.1.recv) | copy-start | bytes 786436
  76.7 11.9 %all-to-all-start.3 = ((bf16[32,24,128]{2,1,0:T(8,128)(2,1)}), bf16[32,24,128]{2,1,0:T(8,128)(2,1)S(1)}, u32[]{:S(2)}, u32[]{:S(2)}) async-start(bf16[32,24,128]{2,1,0:T(8,128)(2,1)} %sum.1), calls=%async_computation.3 | async-start | bytes 393216 | tf_op jit(solution)/shard_map/all_to_all | solution.py:649
  88.6 0.7 copy-start.2

commit v4 on v3

--- a/solution.py
+++ b/solution.py
@@ -13,10 +13,49 @@
 CHUNK = 256
 SUBLANES = 8
 
+KEYS = {
+    "take": (0.0, 0.05),
+    "first": (0.05, 0.3),
+    "second": (0.3, 0.6),
+    "third": (0.6, 0.65),
+    "fields": (0.65, 1.0),
+    "cot_second": (0.05, 0.3),
+    "cot_first": (0.3, 0.6),
+    "cot_inputs": (0.62, 0.7),
+    "leave": (0.9, 1.0),
+    "grad_second": 0.61,
+    "grad_third": 0.605,
+    "grad_first": 0.71,
+}
+
 OWN, OTHER, WEST, EAST, SOUTH, NORTH, COMP, HAS_SOUTH, HAS_NORTH, ON_FOLD = range(10)
 
 f32 = jnp.float32
 bf16 = jnp.bfloat16
+
+
+def place():
+    n_gy, n_gx = lax.axis_size("gy"), lax.axis_size("gx")
+    comp, row, col = (lax.axis_index(axis) for axis in EVERYWHERE)
+    tiles = n_gy * n_gx
+    own = comp * tiles
+    line = own + row * n_gx
+    here = line + col
+    is_top = row == n_gy - 1
+    on_fold = jnp.logical_and(comp == 1, is_top)
+    up = jnp.where(is_top, here, here + n_gx)
+    return (
+        own,
+        (1 - comp) * tiles,
+        line + lax.rem(col + (n_gx - 1), n_gx),
+        line + lax.rem(col + 1, n_gx),
+        jnp.where(row > 0, here - n_gx, here),
+        jnp.where(on_fold, line + (n_gx - 1) - col, up),
+        comp,
+        (row > 0).astype(jnp.int32),
+        jnp.logical_or(on_fold, jnp.logical_not(is_top)).astype(jnp.int32),
+        on_fold.astype(jnp.int32),
+    )
 
 
 def dot(a, b):
@@ -53,10 +92,10 @@
 
 
 def get_edges(meta, recv):
-    west = recv[meta[WEST], 0:32, :].astype(f32)[0:SUBLANES]
-    east = recv[meta[EAST], 0:32, :].astype(f32)[SUBLANES : 2 * SUBLANES]
-    south = recv[meta[SOUTH], 0:32, :].astype(f32)[2 * SUBLANES : 3 * SUBLANES]
-    above = recv[meta[NORTH], 0:32, :].astype(f32)
+    west = recv[meta[WEST]].astype(f32)[0:SUBLANES]
+    east = recv[meta[EAST]].astype(f32)[SUBLANES : 2 * SUBLANES]
+    south = recv[meta[SOUTH]].astype(f32)[2 * SUBLANES : 3 * SUBLANES]
+    above = recv[meta[NORTH]].astype(f32)
     north = jnp.where(
         meta[ON_FOLD] == 1,
         above[2 * SUBLANES : 3 * SUBLANES],
@@ -91,8 +130,9 @@
 
 
 def send_kernel(
-    rows, peers, slots, meta, source, count, state, kernels, out, by_row, stage, blocks, sems
+    rows, peers, slots, source, count, state, kernels, out, by_row, stage, blocks, sems
 ):
+    meta = place()
     width = state.shape[1]
     shape = (SUBLANES, width)
     lane = lax.broadcasted_iota(jnp.int32, shape, 1)
@@ -116,7 +156,7 @@
         return take_edges(tile, r, lane, sides)
 
     zero = jnp.zeros(shape, f32)
-    first, last = lax.fori_loop(0, rows, row_step, (zero, zero), unroll=8)
+    first, last = lax.fori_loop(0, rows, row_step, (zero, zero), unroll=32)
     put_edges(meta, first, last, by_row[0], by_row[rows - 1], stage)
 
     def peer_step(q, unused):
@@ -135,13 +175,15 @@
     out[...] = stage[...].astype(bf16)
 
 
+def spread(low, high, step, count):
+    return [
+        (low + (high - low) * (i + 0.5) / count, functools.partial(step, i)) for i in range(count)
+    ]
+
+
 def weave(*lists):
-    keyed = []
-    for order, steps in enumerate(lists):
-        for i, step in enumerate(steps):
-            keyed.append(((i + 0.5) / len(steps), order, i, step))
-    for entry in sorted(keyed, key=lambda e: e[:3]):
-        entry[3]()
+    for entry in sorted((e for steps in lists for e in steps), key=lambda e: e[0]):
+        entry[1]()
 
 
 def main_kernel(
@@ -150,13 +192,12 @@
     slots,
     share,
     small_share,
-    meta,
     landing,
     b_out,
-    state,
-    goal,
+    state_in,
+    goal_in,
     mask,
-    recv,
+    recv_in,
     rate_ref,
     couple_ref,
     w_first,
@@ -166,13 +207,18 @@
     w_third_back,
     w_second_back,
     w_first_back,
+    new_hbm,
+    base_hbm,
+    diffuse_hbm,
+    send_out,
+    state,
+    goal,
+    recv,
     new_out,
     base_out,
     diffuse_out,
-    send_out,
-    grad_out,
+    sems,
     stage,
-    grad_stage,
     other,
     misfits,
     feats,
@@ -200,14 +246,24 @@
     lane = lax.broadcasted_iota(jnp.int32, shape, 1)
     sub = lax.broadcasted_iota(jnp.int32, shape, 0)
     fluxes = couple_ref.shape[2]
-    pad = BLOCK_ROWS
+    meta = place()
+    slot_rows = recv.shape[1]
+    fetches = [
+        pltpu.make_async_copy(recv_in, recv, sems.at[0]),
+        pltpu.make_async_copy(state_in, state, sems.at[1]),
+        pltpu.make_async_copy(goal_in, goal, sems.at[2]),
+    ]
+    for fetch in fetches:
+        fetch.start()
 
     other[...] = jnp.zeros(other.shape, f32)
 
+    fetches[0].wait()
+
     def land(p, unused):
-        block = recv[meta[OTHER] + p, 0:32, :].astype(f32)
+        block = recv[meta[OTHER] + p].astype(f32)
         for s in range(slots):
-            row = landing[s, p] + pad
+            row = landing[s, p]
             other[row] = other[row] + block[s * SUBLANES : (s + 1) * SUBLANES]
         return unused
 
@@ -218,10 +274,8 @@
     pairs = couple_ref[comp]
     couple = [jnp.broadcast_to(pairs[:, f : f + 1], shape) for f in range(fluxes)]
     ones = (lax.broadcasted_iota(jnp.int32, (16, cells), 0) < 3).astype(f32).astype(bf16)
-    for ref in (*hid_firsts, *hid_seconds, *flux_cots, *feats):
+    for ref in flux_cots:
         ref[...] = jnp.zeros(ref.shape, bf16)
-    for ref in (*slope_firsts, *slope_seconds):
-        ref[...] = jnp.zeros(ref.shape, f32)
     for ref in feats:
         ref[16:32, :] = ones
     for ref in hid_firsts:
@@ -229,6 +283,8 @@
     for ref in (g_first, g_second, g_third, g_bias, edges):
         ref[...] = jnp.zeros(ref.shape, f32)
     bias = jnp.broadcast_to(b_second[...], (hidden, CHUNK))
+    fetches[1].wait()
+    fetches[2].wait()
     b_third = jnp.zeros(shape, f32)
     for f in range(fluxes):
         b_third = jnp.where(sub == f, b_out[f], b_third)
@@ -239,7 +295,7 @@
         def take(i):
             at = pl.ds(i * width, width)
             r = start + i
-            feat[0:16, at] = jnp.concatenate([state[r], other[r + pad]], axis=0).astype(bf16)
+            feat[0:16, at] = jnp.concatenate([state[r], other[r]], axis=0).astype(bf16)
 
         def layer(net, hid_ref, slope_ref, at):
             turn = jnp.tanh(net)
@@ -279,7 +335,7 @@
             diffuse = spread_mask * misfit
             diffuse_out[r] = diffuse
             edges[0], edges[1] = take_edges(diffuse, r, lane, (edges[0], edges[1]))
-            misfits[r + pad] = misfit
+            misfits[r] = misfit
             pulled = jnp.zeros(shape, f32)
             for f in range(fluxes):
                 total = jnp.sum(couple[f] * misfit, axis=0, keepdims=True)
@@ -288,10 +344,13 @@
             flux_cot[0:SUBLANES, at] = pulled
             g_bias[...] = g_bias[...] + pulled.astype(f32)
 
-        steps = [functools.partial(take, i) for i in range(BLOCK_ROWS)]
-        for stage_step in (first, second, third):
-            steps += [functools.partial(stage_step, j) for j in range(chunks)]
-        return steps + [functools.partial(fields, i) for i in range(BLOCK_ROWS)]
+        return (
+            spread(*KEYS["take"], take, BLOCK_ROWS)
+            + spread(*KEYS["first"], first, chunks)
+            + spread(*KEYS["second"], second, chunks)
+            + spread(*KEYS["third"], third, chunks)
+            + spread(*KEYS["fields"], fields, BLOCK_ROWS)
+        )
 
     def backward(block, feat, hid_first, hid_second, slope_first, slope_second, flux_cot):
         start = block * BLOCK_ROWS
@@ -312,7 +371,7 @@
 
         def leave(i):
             at = pl.ds(i * width, width)
-            r = start + i + pad
+            r = start + i
             base_out[r] = misfits[r] + feat_cot[0:SUBLANES, at]
             other[r] = feat_cot[SUBLANES : 2 * SUBLANES, at]
 
@@ -325,39 +384,59 @@
         def grad_first():
             g_first[...] += dot_nt(feat[...], cot_first[...])
 
-        steps = [functools.partial(second, j) for j in range(chunks)]
-        steps += [functools.partial(first, j) for j in range(chunks)]
-        steps += [grad_third, grad_second]
-        steps += [functools.partial(inputs, j) for j in range(chunks)]
-        steps += [grad_first]
-        return steps + [functools.partial(leave, i) for i in range(BLOCK_ROWS)]
+        return (
+            spread(*KEYS["cot_second"], second, chunks)
+            + spread(*KEYS["cot_first"], first, chunks)
+            + spread(*KEYS["cot_inputs"], inputs, chunks)
+            + spread(*KEYS["leave"], leave, BLOCK_ROWS)
+            + [
+                (KEYS["grad_second"], grad_second),
+                (KEYS["grad_third"], grad_third),
+                (KEYS["grad_first"], grad_first),
+            ]
+        )
 
     sets = list(
         zip(feats, hid_firsts, hid_seconds, slope_firsts, slope_seconds, flux_cots, strict=True)
     )
     blocks = rows // BLOCK_ROWS
 
+    def beside(block, this, that):
+        weave(backward(block, *this), forward(block + 1, *that))
+
     def pair_step(pair, unused):
-        even = pair * 2
-        weave(backward(even - 1, *sets[1]), forward(even, *sets[0]))
-        weave(backward(even, *sets[0]), forward(even + 1, *sets[1]))
+        beside(2 * pair, *sets)
+        beside(2 * pair + 1, *sets[::-1])
         return unused
 
-    lax.fori_loop(0, blocks // 2, pair_step, 0)
+    weave(forward(0, *sets[0]))
+    lax.fori_loop(0, blocks // 2 - 1, pair_step, 0)
+    beside(blocks - 2, *sets)
+    ready = rows - BLOCK_ROWS
+    stores = [
+        pltpu.make_async_copy(new_out, new_hbm, sems.at[3]),
+        pltpu.make_async_copy(diffuse_out, diffuse_hbm, sems.at[4]),
+        pltpu.make_async_copy(
+            base_out.at[pl.ds(0, ready)], base_hbm.at[pl.ds(0, ready)], sems.at[5]
+        ),
+    ]
+    for store in stores:
+        store.start()
     weave(backward(blocks - 1, *sets[1]))
-
-    stage[pl.ds(meta[OWN], peers)] = jnp.zeros((peers,) + stage.shape[1:], f32)
+    rest = pltpu.make_async_copy(
+        base_out.at[pl.ds(ready, BLOCK_ROWS)], base_hbm.at[pl.ds(ready, BLOCK_ROWS)], sems.at[6]
+    )
+    rest.start()
+    stage[pl.ds(meta[OWN], peers), 0:slot_rows, :] = jnp.zeros((peers, slot_rows, width), f32)
 
     def leave(p, unused):
         for s in range(slots):
-            row = landing[s, p] + pad
+            row = landing[s, p]
             stage[meta[OTHER] + p, s * SUBLANES : (s + 1) * SUBLANES, :] = other[row]
         return unused
 
     lax.fori_loop(0, peers, leave, 0, unroll=2)
     put_edges(meta, edges[0], edges[1], diffuse_out[0], diffuse_out[rows - 1], stage)
-    send_out[...] = stage[...].astype(bf16)
-
     devices = stage.shape[0]
     halves = hidden // width
     inputs = 2 * SUBLANES
@@ -384,19 +463,28 @@
             h, row = divmod(at, hidden)
             step = min(share - done, hidden - row)
             if h < halves:
-                grad_stage[d, done : done + step, :] = g_second[
+                stage[d, slot_rows + done : slot_rows + done + step, :] = g_second[
                     row : row + step, h * width : (h + 1) * width
                 ]
             done += step
         piece = small[d * small_share : (d + 1) * small_share, :]
         head = piece.astype(bf16).astype(f32)
-        grad_stage[d, share : share + small_share, :] = head
-        grad_stage[d, share + small_share : share + 2 * small_share, :] = piece - head
-    grad_out[...] = grad_stage[...].astype(bf16)
-
-
-def sum_kernel(scale, share, small_share, recv, out, stage):
-    devices = recv.shape[0]
+        top = slot_rows + share
+        stage[d, top : top + small_share, :] = head
+        stage[d, top + small_share : top + 2 * small_share, :] = piece - head
+    send_out[...] = stage[...].astype(bf16)
+    for store in stores:
+        store.wait()
+    rest.wait()
+
+
+def sum_kernel(scale, share, small_share, recv_in, out, recv, stage, sem):
+    devices, packed = recv.shape[:2]
+    fetch = pltpu.make_async_copy(
+        recv_in.at[:, pl.ds(recv_in.shape[1] - packed, packed), :], recv, sem
+    )
+    fetch.start()
+    fetch.wait()
     total = recv[0].astype(f32)
     for d in range(1, devices):
         total = total + recv[d].astype(f32)
@@ -412,8 +500,13 @@
 
 
 def back_kernel(
-    rows, peers, slots, meta, source, count, recv, kernels, base, diffuse, rate_ref, out, total
+    rows, peers, slots, source, count, recv_in, kernels, base, diffuse, rate_ref, out, total, recv,
+    sem,
 ):
+    meta = place()
+    fetch = pltpu.make_async_copy(recv_in.at[:, pl.ds(0, recv.shape[1]), :], recv, sem)
+    fetch.start()
+    fetch.wait()
     width = diffuse.shape[2]
     shape = (SUBLANES, width)
     lane = lax.broadcasted_iota(jnp.int32, shape, 1)
@@ -425,13 +518,13 @@
         here = diffuse[r]
         below = jnp.where(r > 0, diffuse[jnp.maximum(r - 1, 0)], south)
         above = jnp.where(r < rows - 1, diffuse[jnp.minimum(r + 1, rows - 1)], north)
-        total[r] = base[r + BLOCK_ROWS] + rate * laplace_row(here, below, above, west, east, r, lane)
+        total[r] = base[r] + rate * laplace_row(here, below, above, west, east, r, lane)
         return unused
 
     lax.fori_loop(0, rows, lap_step, 0, unroll=8)
 
     def peer_step(q, unused):
-        block = recv[meta[OTHER] + q, 0:32, :].astype(f32)
+        block = recv[meta[OTHER] + q].astype(f32)
         for s in range(slots):
             k = q * slots + s
             sent = block[s * SUBLANES : (s + 1) * SUBLANES].astype(bf16)
@@ -449,8 +542,11 @@
     lax.fori_loop(0, rows, out_step, 0, unroll=8)
 
 
-def unpack_kernel(share, small_share, fluxes, recv, first, bias_one, second, bias_two, third,
-                  bias_three, small):
+def unpack_kernel(share, small_share, fluxes, recv_in, first, bias_one, second, bias_two, third,
+                  bias_three, recv, small, sem):
+    fetch = pltpu.make_async_copy(recv_in, recv, sem)
+    fetch.start()
+    fetch.wait()
     devices = recv.shape[0]
     width = recv.shape[2]
     hidden = second.shape[0]
@@ -499,26 +595,7 @@
     n_gy, n_gx = lax.axis_size("gy"), lax.axis_size("gx")
     tiles = n_gy * n_gx
     devices = 2 * tiles
-    comp, row, col = (lax.axis_index(axis) for axis in EVERYWHERE)
-    own, other = comp * tiles, (1 - comp) * tiles
-    is_top = row == n_gy - 1
-    on_fold = jnp.logical_and(comp == 1, is_top)
-    line = own + row * n_gx
-    here = line + col
-    meta = jnp.stack(
-        [
-            own,
-            other,
-            line + (col + n_gx - 1) % n_gx,
-            line + (col + 1) % n_gx,
-            jnp.where(row > 0, here - n_gx, here),
-            jnp.where(on_fold, line + n_gx - 1 - col, jnp.where(is_top, here, here + n_gx)),
-            comp,
-            (row > 0).astype(jnp.int32),
-            jnp.logical_or(on_fold, jnp.logical_not(is_top)).astype(jnp.int32),
-            on_fold.astype(jnp.int32),
-        ]
-    ).astype(jnp.int32)
+    comp = lax.axis_index("comp")
     channels, rows, width = state.shape[1:]
     hidden = w_mid.shape[0]
     inputs = w_in.shape[0]
@@ -545,14 +622,14 @@
             jax.ShapeDtypeStruct((devices, slot_rows, width), bf16),
             jax.ShapeDtypeStruct((rows, channels, width), f32),
         ),
-        in_specs=[smem, smem, smem, vmem, anywhere],
+        in_specs=[smem, smem, vmem, anywhere],
         out_specs=(vmem, vmem),
         scratch_shapes=[
             pltpu.VMEM((devices, slot_rows, width), f32),
             pltpu.VMEM(kernels.shape, bf16),
             pltpu.SemaphoreType.DMA((parts,)),
         ],
-    )(meta, source, count, surface, kernels)
+    )(source, count, surface, kernels)
     arrived = lax.all_to_all(outgoing, EVERYWHERE, 0, 0, tiled=True)
 
     def pieces(bias):
@@ -582,22 +659,27 @@
     def twice(*args):
         return (pltpu.VMEM(*args), pltpu.VMEM(*args))
 
-    tall = (rows + BLOCK_ROWS, channels, width)
-    new_state, base, diffuse, leaving, gradients = pl.pallas_call(
+    tall = (rows, channels, width)
+    new_state, base, diffuse, leaving = pl.pallas_call(
         functools.partial(main_kernel, rows, peers, slots, share, small_share),
         name="main",
         out_shape=(
             jax.ShapeDtypeStruct((channels * rows, width), f32),
             jax.ShapeDtypeStruct(tall, f32),
             jax.ShapeDtypeStruct((rows, channels, width), f32),
-            jax.ShapeDtypeStruct((devices, slot_rows, width), bf16),
-            jax.ShapeDtypeStruct((devices, packed, width), bf16),
+            jax.ShapeDtypeStruct((devices, slot_rows + packed, width), bf16),
         ),
-        in_specs=[smem, smem, smem] + [vmem] * 13,
-        out_specs=(vmem,) * 5,
+        in_specs=[smem, smem, anywhere, anywhere, vmem, anywhere] + [vmem] * 9,
+        out_specs=(anywhere,) * 3 + (vmem,),
         scratch_shapes=[
-            pltpu.VMEM((devices, slot_rows, width), f32),
-            pltpu.VMEM((devices, packed, width), f32),
+            pltpu.VMEM((rows, channels, width), f32),
+            pltpu.VMEM((channels * rows, width), f32),
+            pltpu.VMEM((devices, slot_rows, width), bf16),
+            pltpu.VMEM((channels * rows, width), f32),
+            pltpu.VMEM(tall, f32),
+            pltpu.VMEM((rows, channels, width), f32),
+            pltpu.SemaphoreType.DMA((7,)),
+            pltpu.VMEM((devices, slot_rows + packed, width), f32),
             pltpu.VMEM(tall, f32),
             pltpu.VMEM(tall, f32),
             twice((32, cells), bf16),
@@ -618,7 +700,6 @@
             pltpu.VMEM((max(48, small_share * devices), width), f32),
         ],
     )(
-        meta,
         landing,
         b_out,
         by_row,
@@ -635,26 +716,33 @@
         w_second_back,
         w_first_back,
     )
-    gradients = lax.all_to_all(gradients, EVERYWHERE, 0, 0, tiled=True)
     returned = lax.all_to_all(leaving, EVERYWHERE, 0, 0, tiled=True)
     scale = 1.0 / (rows * width * tiles)
     summed = pl.pallas_call(
         functools.partial(sum_kernel, scale, share, small_share),
         name="sum",
         out_shape=jax.ShapeDtypeStruct((devices, packed, width), bf16),
-        in_specs=[vmem],
+        in_specs=[anywhere],
         out_specs=vmem,
-        scratch_shapes=[pltpu.VMEM((packed, width), f32)],
-    )(gradients)
+        scratch_shapes=[
+            pltpu.VMEM((devices, packed, width), bf16),
+            pltpu.VMEM((packed, width), f32),
+            pltpu.SemaphoreType.DMA,
+        ],
+    )(returned)
     gathered = lax.all_to_all(summed, EVERYWHERE, 0, 0, tiled=True)
     adjoint = pl.pallas_call(
         functools.partial(back_kernel, rows, peers, slots),
         name="back",
         out_shape=jax.ShapeDtypeStruct((channels * rows, width), f32),
-        in_specs=[smem, smem, smem] + [vmem] * 5,
+        in_specs=[smem, smem, anywhere] + [vmem] * 4,
         out_specs=vmem,
-        scratch_shapes=[pltpu.VMEM((rows, channels, width), f32)],
-    )(meta, source, count, returned, kernels, base, diffuse, diffusivity)
+        scratch_shapes=[
+            pltpu.VMEM((rows, channels, width), f32),
+            pltpu.VMEM((devices, slot_rows, width), bf16),
+            pltpu.SemaphoreType.DMA,
+        ],
+    )(source, count, returned, kernels, base, diffuse, diffusivity)
     first, bias_one, second, bias_two, third, bias_three = pl.pallas_call(
         functools.partial(unpack_kernel, share, small_share, fluxes),
         name="unpack",
@@ -666,9 +754,13 @@
             jax.ShapeDtypeStruct((fluxes, hidden), f32),
             jax.ShapeDtypeStruct((1, fluxes), f32),
         ),
-        in_specs=[vmem],
+        in_specs=[anywhere],
         out_specs=(vmem,) * 6,
-        scratch_shapes=[pltpu.VMEM((max(48, small_share * devices), width), f32)],
+        scratch_shapes=[
+            pltpu.VMEM((devices, packed, width), bf16),
+            pltpu.VMEM((max(48, small_share * devices), width), f32),
+            pltpu.SemaphoreType.DMA,
+        ],
     )(gathered)
     return (
         new_state.reshape(state.shape),

time: 91.4 us -> 83 us (0.908)
  waiting for transfers between devices: 16.3 us -> 6.82 us
  blocking collectives: 12.6 us -> 16.3 us
  starting transfers between devices: 12.5 us -> 11.4 us
    all_to_all x1 -> x0, waiting for transfers between devices: 8.6 us -> none  [shards(): returned = lax.all_to_all(leaving, EVERYWHERE, 0, 0, tiled=True)]
    all_to_all x1, blocking collectives: 12.6 us -> 16.3 us  [shards(): returned = lax.all_to_all(leaving, EVERYWHERE, 0, 0, tiled=True)]
    all_to_all x1 -> x0, starting transfers between devices: 2.58 us -> none  [shards(): returned = lax.all_to_all(leaving, EVERYWHERE, 0, 0, tiled=True)]
    all_to_all x1, starting transfers between devices: 2.59 us -> 4.02 us  [shards(): gathered = lax.all_to_all(summed, EVERYWHERE, 0, 0, tiled=True)]
    pallas_call x1, Pallas kernels: 26.9 us -> 25.9 us  [shards(): pl.pallas_call(functools.partial(main_kernel, rows, peers, slots, share,...]
    unnamed x22 -> x20, local copies, waits for them, and re-layouts: 2.22 us -> 2.25 us
  transfers between devices with their start and end apart: 3 -> 2, of which waited for: 3 -> 2; matrix products, arithmetic and copies ran while one was open for 6% -> 6% of each run, Pallas kernels for 9% -> 9%
where the time goes in v4:
time: 83 us; the launch traced here: 82.5 us
  Pallas kernels  40.5 us (49%)
  blocking collectives  16.3 us (20%)
  starting transfers between devices  11.4 us (14%)
  waiting for transfers between devices  6.82 us (8%)
  local copies, waits for them, and re-layouts  5.98 us (7%)
  between operations  0.85 us (1%)
    pallas_call x1, Pallas kernels, shards(): pl.pallas_call(functools.partial(main_kernel, rows, peers, slots, share,...  25.9 us
    all_to_all x1, blocking collectives, shards(): returned = lax.all_to_all(leaving, EVERYWHERE, 0, 0, tiled=True)  16.3 us
    pallas_call x1, Pallas kernels, shards(): pl.pallas_call(functools.partial(back_kernel, rows, peers, slots), name='...  7.36 us
    all_to_all x1, starting transfers between devices, shards(): arrived = lax.all_to_all(outgoing, EVERYWHERE, 0, 0, tiled=True)  7.33 us
    all_to_all x1, waiting for transfers between devices, shards(): arrived = lax.all_to_all(outgoing, EVERYWHERE, 0, 0, tiled=True)  4.88 us
    all_to_all x1, starting transfers between devices, shards(): gathered = lax.all_to_all(summed, EVERYWHERE, 0, 0, tiled=True)  4.02 us
    pallas_call x1, Pallas kernels, shards(): pl.pallas_call(functools.partial(send_kernel, rows, peers, slots), name='...  3.91 us
    unnamed x20, local copies, waits for them, and re-layouts  2.25 us
  transfers between devices with their start and end apart: 2, of which 2 were waited for; matrix products, arithmetic and copies ran while one was open for 6% of the time, Pallas kernels for 9%

profile of v4, /device:TPU:0, one launch (start us, length us, event | category | flops | bytes accessed | tf_op | source)
XLA Modules:
  0.0 82.5 jit_solution(991742462443803170)
XLA Ops:
  0.6 0.0 copy-start.7
  0.6 0.0 copy-start.4
  0.7 0.0 copy-start.5
  0.7 0.0 copy-start.6
  0.7 0.0 copy-start.8
  0.7 0.0 copy-start.2
  0.7 3.9 %send.1 = (bf16[32,32,128]{2,1,0:T(8,128)(2,1)}, f32[128,8,128]{2,1,0:T(8,128)}) custom-call(s32[4,16]{1,0:T(4,128)} %bitcast.29, s32[16]{0:T(128)} %bitcast.34, f32[1024,128]{1,0:T(8,128)} %bitcast.25, bf16[64,128,128]{2,1,0:T(8,128)(2,1)} %bitcast.23), custom_call_target="tpu_custom_call" | custom-call | tf_op jit(solution)/shard_map/send/pallas_call | solution.py:618
  4.6 7.3 %all-to-all-start = ((bf16[32,32,128]{2,1,0:T(8,128)(2,1)}), bf16[32,32,128]{2,1,0:T(8,128)(2,1)S(1)}, u32[]{:S(2)}, u32[]{:S(2)}) async-start(bf16[32,32,128]{2,1,0:T(8,128)(2,1)} %get-tuple-element.21), calls=%async_computation | async-start | bytes 524288 | tf_op jit(solution)/shard_map/all_to_all | solution.py:633
  12.0 0.0 copy-done.7
  12.0 0.0 copy-done.4
  12.0 0.0 copy-done.5
  12.1 0.1 copy.32
  12.2 0.0 copy-start.3
  12.2 0.1 concatenate.8
  12.4 0.0 copy-done.6
  12.4 0.7 copy.34.couple_ref
  13.1 0.6 pad.8.w_third
  13.7 0.7 copy.35.w_first
  14.4 0.6 pad.9.w_third_back
  15.1 0.0 copy-done.8
  15.1 0.8 copy.37.b_second
  15.9 0.0 copy-done.2
  15.9 0.7 broadcast_multiply_fusion
  16.6 0.8 copy.36.w_second
  17.4 4.9 %all-to-all-done.recv_in = bf16[32,32,128]{2,1,0:T(8,128)(2,1)S(1)} async-done(((bf16[32,32,128]{2,1,0:T(8,128)(2,1)}), bf16[32,32,128]{2,1,0:T(8,128)(2,1)S(1)}, u32[]{:S(2)}, u32[]{:S(2)}) %all-to-all-start) | async-done | bytes 262176 | tf_op jit(solution)/shard_map/all_to_all | solution.py:633
  22.2 0.0 copy-start
  22.2 0.0 copy-done.3
  22.2 0.7 copy-done
  22.9 25.9 %main.1 = (f32[1024,128]{1,0:T(8,128)}, f32[128,8,128]{2,1,0:T(8,128)}, f32[128,8,128]{2,1,0:T(8,128)}, bf16[32,56,128]{2,1,0:T(8,128)(2,1)}) custom-call(s32[4,16]{1,0:T(4,128)} %bitcast.33, f32[4]{0:T(128)} %b_out.1, f32[128,8,128]{2,1,0:T(8,128)} %get-tuple-element.20.state_in, f32[1024,128]{1,0:T(8,128)} %bitcast.26, s32[128,128]{1,0:T(8,128)} %bitcast.28, ...), custom_call_target="tpu_custom_call" | custom-call | tf_op jit(solution)/shard_map/main/pallas_call | solution.py:663
  48.8 16.3 %all_to_all.15.recv_in = bf16[32,56,128]{2,1,0:T(8,128)(2,1)} all-to-all(bf16[32,56,128]{2,1,0:T(8,128)(2,1)} %get-tuple-element.23), channel_id=1, replica_groups=mesh['comp'=2,'gy'=4,'gx'=4] {'comp','gy','gx'}, dimensions={0} | all-to-all | bytes 917504 | tf_op jit(solution)/shard_map/all_to_all | solution.py:719
  65.1 1.7 %sum.1 = bf16[32,24,128]{2,1,0:T(8,128)(2,1)} custom-call(bf16[32,56,128]{2,1,0:T(8,128)(2,1)} %all_to_all.15.recv_in), custom_call_target="tpu_custom_call" | custom-call | tf_op jit(solution)/shard_map/sum/pallas_call | solution.py:721
  66.8 4.0 %all-to-all-start.2 = ((bf16[32,24,128]{2,1,0:T(8,128)(2,1)}), bf16[32,24,128]{2,1,0:T(8,128)(2,1)S(1)}, u32[]{:S(2)}, u32[]{:S(2)}) async-start(bf16[32,24,128]{2,1,0:T(8,128)(2,1)} %sum.1), calls=%async_computation.2 | async-start | bytes 393216 | tf_op jit(solution)/shard_map/all_to_all | solution.py:733
  70.8 7.4 %back.1 = f32[1024,128]{1,0:T(8,128)} custom-call(s32[4,16]{1,0:T(4,128)} %bitcast.30, s32[16]{0:T(128)} %bitcast.35, bf16[32,56,128]{2,1,0:T(8,128)(2,1)} %all_to_all.15.recv_in, bf16[64,128,128]{2,1,0:T(8,128)(2,1)} %bitcast.24, f32[128,8,128]{2,1,0:T(8,128)} %get-tuple-element.24.base, f32[128,8,128]{2,1,0:T(8,128)} %get-tuple-element.25.diffuse, ...), custom_call_target="tpu_custom_call" | custom-call | tf_op jit(solution)/shard_map/back/pallas_call | solution.py:734
  78.2 1.9 %all-to-all-done.2.recv_in = bf16[32,24,128]{2,1,0:T(8,128)(2,1)S(1)} async-done(((bf16[32,24,128]{2,1,0:T(8,128)(2,1)}), bf16[32,24,128]{2,1,0:T(8,128)(2,1)S(1)}, u32[]{:S(2)}, u32[]{:S(2)}) %all-to-all-start.2) | async-done | bytes 196640 | tf_op jit(solution)/shard_map/all_to_all | solution.py:733
  80.1 0.0 copy-start.1
  80.1 0.7 copy-done.1
  80.8 1.7 %unpack.1 = (f32[16,256]{1,0:T(8,128)}, f32[1,256]{1,0:T(1,128)}, f32[256,256]{1,0:T(8,128)}, f32[1,256]{1,0:T(1,128)}, f32[4,256]{1,0:T(4,128)}, /*index=5*/f32[1,4]{1,0:T(1,128)}) custom-call(bf16[32,24,128]{2,1,0:T(8,128)(2,1)} %copy-done.1), custom_call_target="tpu_custom_call" | custom-call | tf_op jit(solution)/shard_map/unpack/pallas_call | solution.py:746
  (10 shorter events, 0.1 us)
Async XLA Ops:
  0.6 11.3 %copy-start.7 = (f32[256]{0:T(256)S(1)}, f32[256]{0:T(256)}, u32[]{:S(2)}) copy-start(f32[256]{0:T(256)} %param.21) | copy-start | bytes 3076
  0.6 11.4 %copy-start.4 = (bf16[16,256]{1,0:T(8,128)(2,1)S(1)}, bf16[16,256]{1,0:T(8,128)(2,1)}, u32[]{:S(2)}) copy-start(bf16[16,256]{1,0:T(8,128)(2,1)} %param.20) | copy-start | bytes 24580
  0.7 11.4 %copy-start.5 = (bf16[256,4]{0,1:T(4,128)(2,1)S(1)}, bf16[256,4]{0,1:T(4,128)(2,1)}, u32[]{:S(2)}) copy-start(bf16[256,4]{0,1:T(4,128)(2,1)} %param.24) | copy-start | bytes 6148
  0.7 11.8 %copy-start.6 = (f32[2,8,4]{1,2,0:T(4,128)S(1)}, f32[2,8,4]{1,2,0:T(4,128)}, u32[]{:S(2)}) copy-start(f32[2,8,4]{1,2,0:T(4,128)} %param.19) | copy-start | bytes 772
  0.7 14.4 %copy-start.8 = (f32[256]{0:T(256)S(1)}, f32[256]{0:T(256)}, u32[]{:S(2)}) copy-start(f32[256]{0:T(256)} %param.23) | copy-start | bytes 3076
  0.7 15.2 %copy-start.2 = (bf16[256,256]{1,0:T(8,128)(2,1)S(1)}, bf16[256,256]{1,0:T(8,128)(2,1)}, u32[]{:S(2)}) copy-start(bf16[256,256]{1,0:T(8,128)(2,1)} %param.22) | copy-start | bytes 393220
  4.6 17.6 %all-to-all-start = ((bf16[32,32,128]{2,1,0:T(8,128)(2,1)}), bf16[32,32,128]{2,1,0:T(8,128)(2,1)S(1)}, u32[]{:S(2)}, u32[]{:S(2)}) async-start(bf16[32,32,128]{2,1,0:T(8,128)(2,1)} %get-tuple-element.21), calls=%async_computation | async-start | bytes 524288 | tf_op jit(solution)/shard_map/all_to_all | solution.py:633
  12.2 10.0 %copy-start.3 = (bf16[16,256]{1,0:T(8,128)(2,1)}, bf16[16,256]{1,0:T(8,128)(2,1)S(1)}, u32[]{:S(2)}) copy-start(bf16[16,256]{1,0:T(8,128)(2,1)S(1)} %maximum_select_fusion.w_first_back) | copy-start | bytes 24580
  22.2 0.7 copy-start
  66.8 13.3 %all-to-all-start.2 = ((bf16[32,24,128]{2,1,0:T(8,128)(2,1)}), bf16[32,24,128]{2,1,0:T(8,128)(2,1)S(1)}, u32[]{:S(2)}, u32[]{:S(2)}) async-start(bf16[32,24,128]{2,1,0:T(8,128)(2,1)} %sum.1), calls=%async_computation.2 | async-start | bytes 393216 | tf_op jit(solution)/shard_map/all_to_all | solution.py:733
  80.1 0.7 copy-start.1

commit v5 on v4

--- a/solution.py
+++ b/solution.py
@@ -32,6 +32,10 @@
 
 f32 = jnp.float32
 bf16 = jnp.bfloat16
+
+
+def side_by_side(ref, first, count, low, high):
+    return jnp.concatenate([ref[first + i, low:high, :] for i in range(count)], axis=1)
 
 
 def place():
@@ -273,13 +277,16 @@
     rate = jnp.broadcast_to(column_of(rate_ref, comp), shape)
     pairs = couple_ref[comp]
     couple = [jnp.broadcast_to(pairs[:, f : f + 1], shape) for f in range(fluxes)]
-    ones = (lax.broadcasted_iota(jnp.int32, (16, cells), 0) < 3).astype(f32).astype(bf16)
+    ones = (lax.broadcasted_iota(jnp.int32, (16, width), 0) < 3).astype(f32).astype(bf16)
+    lanes = CHUNK // width
     for ref in flux_cots:
         ref[...] = jnp.zeros(ref.shape, bf16)
     for ref in feats:
-        ref[16:32, :] = ones
+        for i in range(BLOCK_ROWS):
+            ref[i, 16:32, :] = ones
     for ref in hid_firsts:
-        ref[hidden : hidden + 16, :] = ones
+        for i in range(BLOCK_ROWS):
+            ref[i, hidden : hidden + 16, :] = ones
     for ref in (g_first, g_second, g_third, g_bias, edges):
         ref[...] = jnp.zeros(ref.shape, f32)
     bias = jnp.broadcast_to(b_second[...], (hidden, CHUNK))
@@ -293,29 +300,32 @@
         start = block * BLOCK_ROWS
 
         def take(i):
-            at = pl.ds(i * width, width)
             r = start + i
-            feat[0:16, at] = jnp.concatenate([state[r], other[r]], axis=0).astype(bf16)
-
-        def layer(net, hid_ref, slope_ref, at):
+            feat[i, 0:16, :] = jnp.concatenate([state[r], other[r]], axis=0).astype(bf16)
+
+        def layer(net, hid_ref, slope_ref, j):
             turn = jnp.tanh(net)
             up = 1.0 + turn
             hid = net * up
-            hid_ref[0:hidden, at] = hid.astype(bf16)
-            slope_ref[:, at] = (up + hid) - hid * turn
+            slope = (up + hid) - hid * turn
+            hid = hid.astype(bf16)
+            for i in range(lanes):
+                cols = slice(i * width, (i + 1) * width)
+                hid_ref[j * lanes + i, 0:hidden, :] = hid[:, cols]
+                slope_ref[j * lanes + i] = slope[:, cols]
 
         def first(j):
-            at = pl.ds(j * CHUNK, CHUNK)
-            layer(dot(w_first[...], feat[:, at]), hid_first, slope_first, at)
+            net = dot(w_first[...], side_by_side(feat, j * lanes, lanes, 0, 32))
+            layer(net, hid_first, slope_first, j)
 
         def second(j):
-            at = pl.ds(j * CHUNK, CHUNK)
-            net = dot(w_second[...], hid_first[0:hidden, at]) + bias
-            layer(net, hid_second, slope_second, at)
+            net = dot(w_second[...], side_by_side(hid_first, j * lanes, lanes, 0, hidden)) + bias
+            layer(net, hid_second, slope_second, j)
 
         def third(j):
             at = pl.ds(j * CHUNK, CHUNK)
-            flux[:, at] = dot(w_third[...], hid_second[:, at])[0:SUBLANES]
+            hid = side_by_side(hid_second, j * lanes, lanes, 0, hidden)
+            flux[:, at] = dot(w_third[...], hid)[0:SUBLANES]
 
         def fields(i):
             at = pl.ds(i * width, width)
@@ -341,7 +351,7 @@
                 total = jnp.sum(couple[f] * misfit, axis=0, keepdims=True)
                 pulled = jnp.where(sub == f, jnp.broadcast_to(total, shape), pulled)
             pulled = (pulled * wet).astype(bf16)
-            flux_cot[0:SUBLANES, at] = pulled
+            flux_cot[i, 0:SUBLANES, :] = pulled
             g_bias[...] = g_bias[...] + pulled.astype(f32)
 
         return (
@@ -355,19 +365,26 @@
     def backward(block, feat, hid_first, hid_second, slope_first, slope_second, flux_cot):
         start = block * BLOCK_ROWS
 
+        def pull(net, slope_ref, cot_ref, j):
+            for i in range(lanes):
+                cols = slice(i * width, (i + 1) * width)
+                cot_ref[j * lanes + i] = (net[:, cols] * slope_ref[j * lanes + i]).astype(bf16)
+
         def second(j):
-            at = pl.ds(j * CHUNK, CHUNK)
-            net = dot(w_third_back[...], flux_cot[:, at])
-            cot_second[:, at] = (net * slope_second[:, at]).astype(bf16)
+            net = dot(w_third_back[...], side_by_side(flux_cot, j * lanes, lanes, 0, 16))
+            pull(net, slope_second, cot_second, j)
 
         def first(j):
-            at = pl.ds(j * CHUNK, CHUNK)
-            net = dot(w_second_back[...], cot_second[:, at])
-            cot_first[:, at] = (net * slope_first[:, at]).astype(bf16)
+            net = dot(w_second_back[...], side_by_side(cot_second, j * lanes, lanes, 0, hidden))
+            pull(net, slope_first, cot_first, j)
 
         def inputs(j):
             at = pl.ds(j * CHUNK, CHUNK)
-            feat_cot[:, at] = dot(w_first_back[...], cot_first[:, at])
+            cot = side_by_side(cot_first, j * lanes, lanes, 0, hidden)
+            feat_cot[:, at] = dot(w_first_back[...], cot)
+
+        def whole(ref):
+            return side_by_side(ref, 0, BLOCK_ROWS, 0, ref.shape[1])
 
         def leave(i):
             at = pl.ds(i * width, width)
@@ -376,13 +393,13 @@
             other[r] = feat_cot[SUBLANES : 2 * SUBLANES, at]
 
         def grad_second():
-            g_second[...] += dot_nt(hid_first[...], cot_second[...])
+            g_second[...] += dot_nt(whole(hid_first), whole(cot_second))
 
         def grad_third():
-            g_third[...] += dot_nt(flux_cot[...], hid_second[...])
+            g_third[...] += dot_nt(whole(flux_cot), whole(hid_second))
 
         def grad_first():
-            g_first[...] += dot_nt(feat[...], cot_first[...])
+            g_first[...] += dot_nt(whole(feat), whole(cot_first))
 
         return (
             spread(*KEYS["cot_second"], second, chunks)
@@ -682,14 +699,14 @@
             pltpu.VMEM((devices, slot_rows + packed, width), f32),
             pltpu.VMEM(tall, f32),
             pltpu.VMEM(tall, f32),
-            twice((32, cells), bf16),
-            twice((hidden + 16, cells), bf16),
-            twice((hidden, cells), bf16),
-            twice((hidden, cells), f32),
-            twice((hidden, cells), f32),
-            twice((16, cells), bf16),
-            pltpu.VMEM((hidden, cells), bf16),
-            pltpu.VMEM((hidden, cells), bf16),
+            twice((BLOCK_ROWS, 32, width), bf16),
+            twice((BLOCK_ROWS, hidden + 16, width), bf16),
+            twice((BLOCK_ROWS, hidden, width), bf16),
+            twice((BLOCK_ROWS, hidden, width), f32),
+            twice((BLOCK_ROWS, hidden, width), f32),
+            twice((BLOCK_ROWS, 16, width), bf16),
+            pltpu.VMEM((BLOCK_ROWS, hidden, width), bf16),
+            pltpu.VMEM((BLOCK_ROWS, hidden, width), bf16),
             pltpu.VMEM((8, cells), f32),
             pltpu.VMEM((16, cells), f32),
             pltpu.VMEM((32, hidden), f32),

time: 83 us -> 82.1 us (0.989)
    pallas_call x1, Pallas kernels: 25.9 us -> 25 us  [shards(): pl.pallas_call(functools.partial(main_kernel, rows, peers, slots, share,...]
where the time goes in v5:
time: 82.1 us; the launch traced here: 81.7 us
  Pallas kernels  39.7 us (48%)
  blocking collectives  16.3 us (20%)
  starting transfers between devices  11.4 us (14%)
  waiting for transfers between devices  6.81 us (8%)
  local copies, waits for them, and re-layouts  5.98 us (7%)
  between operations  0.85 us (1%)
    pallas_call x1, Pallas kernels, shards(): pl.pallas_call(functools.partial(main_kernel, rows, peers, slots, share,...  25 us
    all_to_all x1, blocking collectives, shards(): returned = lax.all_to_all(leaving, EVERYWHERE, 0, 0, tiled=True)  16.3 us
    pallas_call x1, Pallas kernels, shards(): pl.pallas_call(functools.partial(back_kernel, rows, peers, slots), name='...  7.36 us
    all_to_all x1, starting transfers between devices, shards(): arrived = lax.all_to_all(outgoing, EVERYWHERE, 0, 0, tiled=True)  7.33 us
    all_to_all x1, waiting for transfers between devices, shards(): arrived = lax.all_to_all(outgoing, EVERYWHERE, 0, 0, tiled=True)  4.88 us
    all_to_all x1, starting transfers between devices, shards(): gathered = lax.all_to_all(summed, EVERYWHERE, 0, 0, tiled=True)  4.02 us
    pallas_call x1, Pallas kernels, shards(): pl.pallas_call(functools.partial(send_kernel, rows, peers, slots), name='...  3.91 us
    unnamed x20, local copies, waits for them, and re-layouts  2.25 us
  transfers between devices with their start and end apart: 2, of which 2 were waited for; matrix products, arithmetic and copies ran while one was open for 6% of the time, Pallas kernels for 9%

profile of v5, /device:TPU:0, one launch (start us, length us, event | category | flops | bytes accessed | tf_op | source)
XLA Modules:
  0.0 81.7 jit_solution(7097447092121153565)
XLA Ops:
  0.6 0.0 copy-start.7
  0.6 0.0 copy-start.4
  0.7 0.0 copy-start.5
  0.7 0.0 copy-start.6
  0.7 0.0 copy-start.8
  0.7 0.0 copy-start.2
  0.7 3.9 %send.1 = (bf16[32,32,128]{2,1,0:T(8,128)(2,1)}, f32[128,8,128]{2,1,0:T(8,128)}) custom-call(s32[4,16]{1,0:T(4,128)} %bitcast.29, s32[16]{0:T(128)} %bitcast.34, f32[1024,128]{1,0:T(8,128)} %bitcast.25, bf16[64,128,128]{2,1,0:T(8,128)(2,1)} %bitcast.23), custom_call_target="tpu_custom_call" | custom-call | tf_op jit(solution)/shard_map/send/pallas_call | solution.py:635
  4.6 7.3 %all-to-all-start = ((bf16[32,32,128]{2,1,0:T(8,128)(2,1)}), bf16[32,32,128]{2,1,0:T(8,128)(2,1)S(1)}, u32[]{:S(2)}, u32[]{:S(2)}) async-start(bf16[32,32,128]{2,1,0:T(8,128)(2,1)} %get-tuple-element.21), calls=%async_computation | async-start | bytes 524288 | tf_op jit(solution)/shard_map/all_to_all | solution.py:650
  12.0 0.0 copy-done.7
  12.0 0.0 copy-done.4
  12.0 0.0 copy-done.5
  12.1 0.1 copy.32
  12.2 0.0 copy-start.3
  12.2 0.1 concatenate.8
  12.4 0.0 copy-done.6
  12.4 0.7 copy.34.couple_ref
  13.1 0.6 pad.8.w_third
  13.7 0.7 copy.35.w_first
  14.4 0.6 pad.9.w_third_back
  15.1 0.0 copy-done.8
  15.1 0.8 %copy.37.b_second = f32[256,1]{1,0:T(8,128)} copy(f32[256,1]{0,1:T(1,128)S(1)} %bitcast.32) | data formatting | bytes 2048 | tf_op jit(solution)/shard_map/broadcast_in_dim | solution.py:665
  15.9 0.0 copy-done.2
  15.9 0.7 broadcast_multiply_fusion
  16.6 0.8 copy.36.w_second
  17.4 4.9 %all-to-all-done.recv_in = bf16[32,32,128]{2,1,0:T(8,128)(2,1)S(1)} async-done(((bf16[32,32,128]{2,1,0:T(8,128)(2,1)}), bf16[32,32,128]{2,1,0:T(8,128)(2,1)S(1)}, u32[]{:S(2)}, u32[]{:S(2)}) %all-to-all-start) | async-done | bytes 262176 | tf_op jit(solution)/shard_map/all_to_all | solution.py:650
  22.2 0.0 copy-start
  22.2 0.0 copy-done.3
  22.2 0.7 copy-done
  22.9 25.0 %main.1 = (f32[1024,128]{1,0:T(8,128)}, f32[128,8,128]{2,1,0:T(8,128)}, f32[128,8,128]{2,1,0:T(8,128)}, bf16[32,56,128]{2,1,0:T(8,128)(2,1)}) custom-call(s32[4,16]{1,0:T(4,128)} %bitcast.33, f32[4]{0:T(128)} %b_out.1, f32[128,8,128]{2,1,0:T(8,128)} %get-tuple-element.20.state_in, f32[1024,128]{1,0:T(8,128)} %bitcast.26, s32[128,128]{1,0:T(8,128)} %bitcast.28, ...), custom_call_target="tpu_custom_call" | custom-call | tf_op jit(solution)/shard_map/main/pallas_call | solution.py:680
  48.0 16.3 %all_to_all.15.recv_in = bf16[32,56,128]{2,1,0:T(8,128)(2,1)} all-to-all(bf16[32,56,128]{2,1,0:T(8,128)(2,1)} %get-tuple-element.23), channel_id=1, replica_groups=mesh['comp'=2,'gy'=4,'gx'=4] {'comp','gy','gx'}, dimensions={0} | all-to-all | bytes 917504 | tf_op jit(solution)/shard_map/all_to_all | solution.py:736
  64.3 1.7 %sum.1 = bf16[32,24,128]{2,1,0:T(8,128)(2,1)} custom-call(bf16[32,56,128]{2,1,0:T(8,128)(2,1)} %all_to_all.15.recv_in), custom_call_target="tpu_custom_call" | custom-call | tf_op jit(solution)/shard_map/sum/pallas_call | solution.py:738
  66.0 4.0 %all-to-all-start.2 = ((bf16[32,24,128]{2,1,0:T(8,128)(2,1)}), bf16[32,24,128]{2,1,0:T(8,128)(2,1)S(1)}, u32[]{:S(2)}, u32[]{:S(2)}) async-start(bf16[32,24,128]{2,1,0:T(8,128)(2,1)} %sum.1), calls=%async_computation.2 | async-start | bytes 393216 | tf_op jit(solution)/shard_map/all_to_all | solution.py:750
  70.0 7.4 %back.1 = f32[1024,128]{1,0:T(8,128)} custom-call(s32[4,16]{1,0:T(4,128)} %bitcast.30, s32[16]{0:T(128)} %bitcast.35, bf16[32,56,128]{2,1,0:T(8,128)(2,1)} %all_to_all.15.recv_in, bf16[64,128,128]{2,1,0:T(8,128)(2,1)} %bitcast.24, f32[128,8,128]{2,1,0:T(8,128)} %get-tuple-element.24.base, f32[128,8,128]{2,1,0:T(8,128)} %get-tuple-element.25.diffuse, ...), custom_call_target="tpu_custom_call" | custom-call | tf_op jit(solution)/shard_map/back/pallas_call | solution.py:751
  77.4 1.9 %all-to-all-done.2.recv_in = bf16[32,24,128]{2,1,0:T(8,128)(2,1)S(1)} async-done(((bf16[32,24,128]{2,1,0:T(8,128)(2,1)}), bf16[32,24,128]{2,1,0:T(8,128)(2,1)S(1)}, u32[]{:S(2)}, u32[]{:S(2)}) %all-to-all-start.2) | async-done | bytes 196640 | tf_op jit(solution)/shard_map/all_to_all | solution.py:750
  79.3 0.0 copy-start.1
  79.3 0.7 copy-done.1
  80.0 1.7 %unpack.1 = (f32[16,256]{1,0:T(8,128)}, f32[1,256]{1,0:T(1,128)}, f32[256,256]{1,0:T(8,128)}, f32[1,256]{1,0:T(1,128)}, f32[4,256]{1,0:T(4,128)}, /*index=5*/f32[1,4]{1,0:T(1,128)}) custom-call(bf16[32,24,128]{2,1,0:T(8,128)(2,1)} %copy-done.1), custom_call_target="tpu_custom_call" | custom-call | tf_op jit(solution)/shard_map/unpack/pallas_call | solution.py:763
  (10 shorter events, 0.1 us)
Async XLA Ops:
  0.6 11.3 %copy-start.7 = (f32[256]{0:T(256)S(1)}, f32[256]{0:T(256)}, u32[]{:S(2)}) copy-start(f32[256]{0:T(256)} %param.21) | copy-start | bytes 3076
  0.6 11.4 %copy-start.4 = (bf16[16,256]{1,0:T(8,128)(2,1)S(1)}, bf16[16,256]{1,0:T(8,128)(2,1)}, u32[]{:S(2)}) copy-start(bf16[16,256]{1,0:T(8,128)(2,1)} %param.20) | copy-start | bytes 24580
  0.7 11.4 %copy-start.5 = (bf16[256,4]{0,1:T(4,128)(2,1)S(1)}, bf16[256,4]{0,1:T(4,128)(2,1)}, u32[]{:S(2)}) copy-start(bf16[256,4]{0,1:T(4,128)(2,1)} %param.24) | copy-start | bytes 6148
  0.7 11.8 %copy-start.6 = (f32[2,8,4]{1,2,0:T(4,128)S(1)}, f32[2,8,4]{1,2,0:T(4,128)}, u32[]{:S(2)}) copy-start(f32[2,8,4]{1,2,0:T(4,128)} %param.19) | copy-start | bytes 772
  0.7 14.4 %copy-start.8 = (f32[256]{0:T(256)S(1)}, f32[256]{0:T(256)}, u32[]{:S(2)}) copy-start(f32[256]{0:T(256)} %param.23) | copy-start | bytes 3076
  0.7 15.2 %copy-start.2 = (bf16[256,256]{1,0:T(8,128)(2,1)S(1)}, bf16[256,256]{1,0:T(8,128)(2,1)}, u32[]{:S(2)}) copy-start(bf16[256,256]{1,0:T(8,128)(2,1)} %param.22) | copy-start | bytes 393220
  4.6 17.6 %all-to-all-start = ((bf16[32,32,128]{2,1,0:T(8,128)(2,1)}), bf16[32,32,128]{2,1,0:T(8,128)(2,1)S(1)}, u32[]{:S(2)}, u32[]{:S(2)}) async-start(bf16[32,32,128]{2,1,0:T(8,128)(2,1)} %get-tuple-element.21), calls=%async_computation | async-start | bytes 524288 | tf_op jit(solution)/shard_map/all_to_all | solution.py:650
  12.2 10.0 %copy-start.3 = (bf16[16,256]{1,0:T(8,128)(2,1)}, bf16[16,256]{1,0:T(8,128)(2,1)S(1)}, u32[]{:S(2)}) copy-start(bf16[16,256]{1,0:T(8,128)(2,1)S(1)} %maximum_select_fusion.w_first_back) | copy-start | bytes 24580
  22.2 0.7 copy-start
  66.0 13.3 %all-to-all-start.2 = ((bf16[32,24,128]{2,1,0:T(8,128)(2,1)}), bf16[32,24,128]{2,1,0:T(8,128)(2,1)S(1)}, u32[]{:S(2)}, u32[]{:S(2)}) async-start(bf16[32,24,128]{2,1,0:T(8,128)(2,1)} %sum.1), calls=%async_computation.2 | async-start | bytes 393216 | tf_op jit(solution)/shard_map/all_to_all | solution.py:750
  79.3 0.7 copy-start.1

commit v6 on v5

--- a/solution.py
+++ b/solution.py
@@ -11,6 +11,7 @@
 EVERYWHERE = ("comp", "gy", "gx")
 BLOCK_ROWS = 8
 CHUNK = 256
+FETCHED = 12
 SUBLANES = 8
 
 KEYS = {
@@ -32,6 +33,16 @@
 
 f32 = jnp.float32
 bf16 = jnp.bfloat16
+
+
+def fetch_all(pairs, sems):
+    copies = [
+        pltpu.make_async_copy(src, dst, sems.at[i])
+        for i, (src, dst) in enumerate(pairs)
+    ]
+    for copy in copies:
+        copy.start()
+    return copies
 
 
 def side_by_side(ref, first, count, low, high):
@@ -96,10 +107,10 @@
 
 
 def get_edges(meta, recv):
-    west = recv[meta[WEST]].astype(f32)[0:SUBLANES]
-    east = recv[meta[EAST]].astype(f32)[SUBLANES : 2 * SUBLANES]
-    south = recv[meta[SOUTH]].astype(f32)[2 * SUBLANES : 3 * SUBLANES]
-    above = recv[meta[NORTH]].astype(f32)
+    west = recv[meta[WEST], 0 : 4 * SUBLANES, :].astype(f32)[0:SUBLANES]
+    east = recv[meta[EAST], 0 : 4 * SUBLANES, :].astype(f32)[SUBLANES : 2 * SUBLANES]
+    south = recv[meta[SOUTH], 0 : 4 * SUBLANES, :].astype(f32)[2 * SUBLANES : 3 * SUBLANES]
+    above = recv[meta[NORTH], 0 : 4 * SUBLANES, :].astype(f32)
     north = jnp.where(
         meta[ON_FOLD] == 1,
         above[2 * SUBLANES : 3 * SUBLANES],
@@ -134,9 +145,11 @@
 
 
 def send_kernel(
-    rows, peers, slots, source, count, state, kernels, out, by_row, stage, blocks, sems
+    rows, peers, slots, source_in, count_in, state_in, kernels, out, by_row, stage, blocks, sems,
+    source, count, state, small_sems,
 ):
     meta = place()
+    small = fetch_all([(state_in, state), (source_in, source), (count_in, count)], small_sems)
     width = state.shape[1]
     shape = (SUBLANES, width)
     lane = lax.broadcasted_iota(jnp.int32, shape, 1)
@@ -154,6 +167,9 @@
         copy.start()
     stage[pl.ds(meta[OWN], peers)] = jnp.zeros((peers,) + stage.shape[1:], f32)
 
+    for copy in small:
+        copy.wait()
+
     def row_step(r, sides):
         tile = state[pl.ds(r, SUBLANES, stride=rows), :]
         by_row[r] = tile
@@ -196,12 +212,52 @@
     slots,
     share,
     small_share,
+    state,
+    goal,
+    recv,
+    *refs,
+):
+    fetched, refs = refs[:FETCHED], refs[FETCHED:]
+    (new_hbm, base_hbm, diffuse_hbm, send_out), refs = refs[:4], refs[4:]
+    kept, refs = refs[:FETCHED], refs[FETCHED:]
+    fetch_sems, store_sems, new_out, base_out, diffuse_out = refs[:5]
+    copies = fetch_all(list(zip(fetched, kept, strict=True)), fetch_sems)
+    main_steps(
+        rows,
+        peers,
+        slots,
+        share,
+        small_share,
+        copies,
+        state,
+        goal,
+        recv,
+        *kept,
+        new_hbm,
+        base_hbm,
+        diffuse_hbm,
+        send_out,
+        store_sems,
+        new_out,
+        base_out,
+        diffuse_out,
+        *refs[5:],
+    )
+
+
+def main_steps(
+    rows,
+    peers,
+    slots,
+    share,
+    small_share,
+    copies,
+    state,
+    goal,
+    recv,
     landing,
     b_out,
-    state_in,
-    goal_in,
     mask,
-    recv_in,
     rate_ref,
     couple_ref,
     w_first,
@@ -215,13 +271,10 @@
     base_hbm,
     diffuse_hbm,
     send_out,
-    state,
-    goal,
-    recv,
+    store_sems,
     new_out,
     base_out,
     diffuse_out,
-    sems,
     stage,
     other,
     misfits,
@@ -252,17 +305,9 @@
     fluxes = couple_ref.shape[2]
     meta = place()
     slot_rows = recv.shape[1]
-    fetches = [
-        pltpu.make_async_copy(recv_in, recv, sems.at[0]),
-        pltpu.make_async_copy(state_in, state, sems.at[1]),
-        pltpu.make_async_copy(goal_in, goal, sems.at[2]),
-    ]
-    for fetch in fetches:
-        fetch.start()
-
     other[...] = jnp.zeros(other.shape, f32)
-
-    fetches[0].wait()
+    for copy in copies:
+        copy.wait()
 
     def land(p, unused):
         block = recv[meta[OTHER] + p].astype(f32)
@@ -290,8 +335,6 @@
     for ref in (g_first, g_second, g_third, g_bias, edges):
         ref[...] = jnp.zeros(ref.shape, f32)
     bias = jnp.broadcast_to(b_second[...], (hidden, CHUNK))
-    fetches[1].wait()
-    fetches[2].wait()
     b_third = jnp.zeros(shape, f32)
     for f in range(fluxes):
         b_third = jnp.where(sub == f, b_out[f], b_third)
@@ -430,18 +473,19 @@
     lax.fori_loop(0, blocks // 2 - 1, pair_step, 0)
     beside(blocks - 2, *sets)
     ready = rows - BLOCK_ROWS
-    stores = [
-        pltpu.make_async_copy(new_out, new_hbm, sems.at[3]),
-        pltpu.make_async_copy(diffuse_out, diffuse_hbm, sems.at[4]),
-        pltpu.make_async_copy(
-            base_out.at[pl.ds(0, ready)], base_hbm.at[pl.ds(0, ready)], sems.at[5]
-        ),
-    ]
-    for store in stores:
-        store.start()
+    stores = fetch_all(
+        [
+            (new_out, new_hbm),
+            (diffuse_out, diffuse_hbm),
+            (base_out.at[pl.ds(0, ready)], base_hbm.at[pl.ds(0, ready)]),
+        ],
+        store_sems,
+    )
     weave(backward(blocks - 1, *sets[1]))
     rest = pltpu.make_async_copy(
-        base_out.at[pl.ds(ready, BLOCK_ROWS)], base_hbm.at[pl.ds(ready, BLOCK_ROWS)], sems.at[6]
+        base_out.at[pl.ds(ready, BLOCK_ROWS)],
+        base_hbm.at[pl.ds(ready, BLOCK_ROWS)],
+        store_sems.at[3],
     )
     rest.start()
     stage[pl.ds(meta[OWN], peers), 0:slot_rows, :] = jnp.zeros((peers, slot_rows, width), f32)
@@ -490,21 +534,17 @@
         stage[d, top : top + small_share, :] = head
         stage[d, top + small_share : top + 2 * small_share, :] = piece - head
     send_out[...] = stage[...].astype(bf16)
-    for store in stores:
-        store.wait()
-    rest.wait()
-
-
-def sum_kernel(scale, share, small_share, recv_in, out, recv, stage, sem):
-    devices, packed = recv.shape[:2]
-    fetch = pltpu.make_async_copy(
-        recv_in.at[:, pl.ds(recv_in.shape[1] - packed, packed), :], recv, sem
-    )
-    fetch.start()
-    fetch.wait()
-    total = recv[0].astype(f32)
+    for copy in (*stores, rest):
+        copy.wait()
+
+
+def sum_kernel(scale, share, small_share, recv, out, stage):
+    devices = recv.shape[0]
+    packed = stage.shape[0]
+    at = slice(recv.shape[1] - packed, recv.shape[1])
+    total = recv[0, at, :].astype(f32)
     for d in range(1, devices):
-        total = total + recv[d].astype(f32)
+        total = total + recv[d, at, :].astype(f32)
     stage[...] = total * scale
     low = slice(share + small_share, share + 2 * small_share)
     piece = stage[share : share + small_share, :] + stage[low, :]
@@ -517,13 +557,23 @@
 
 
 def back_kernel(
-    rows, peers, slots, source, count, recv_in, kernels, base, diffuse, rate_ref, out, total, recv,
-    sem,
+    rows, peers, slots, recv, kernels, source_in, count_in, rate_in, base_in, diffuse_in, out,
+    source, count, rate_ref, base, diffuse, total, sems,
 ):
     meta = place()
-    fetch = pltpu.make_async_copy(recv_in.at[:, pl.ds(0, recv.shape[1]), :], recv, sem)
-    fetch.start()
-    fetch.wait()
+    copies = fetch_all(
+        [
+            (diffuse_in, diffuse),
+            (base_in, base),
+            (source_in, source),
+            (count_in, count),
+            (rate_in, rate_ref),
+        ],
+        sems,
+    )
+    for copy in copies:
+        copy.wait()
+    width = kernels.shape[2]
     width = diffuse.shape[2]
     shape = (SUBLANES, width)
     lane = lax.broadcasted_iota(jnp.int32, shape, 1)
@@ -541,7 +591,7 @@
     lax.fori_loop(0, rows, lap_step, 0, unroll=8)
 
     def peer_step(q, unused):
-        block = recv[meta[OTHER] + q].astype(f32)
+        block = recv[meta[OTHER] + q, 0 : slots * SUBLANES, :].astype(f32)
         for s in range(slots):
             k = q * slots + s
             sent = block[s * SUBLANES : (s + 1) * SUBLANES].astype(bf16)
@@ -559,11 +609,8 @@
     lax.fori_loop(0, rows, out_step, 0, unroll=8)
 
 
-def unpack_kernel(share, small_share, fluxes, recv_in, first, bias_one, second, bias_two, third,
-                  bias_three, recv, small, sem):
-    fetch = pltpu.make_async_copy(recv_in, recv, sem)
-    fetch.start()
-    fetch.wait()
+def unpack_kernel(share, small_share, fluxes, recv, first, bias_one, second, bias_two, third,
+                  bias_three, small):
     devices = recv.shape[0]
     width = recv.shape[2]
     hidden = second.shape[0]
@@ -627,10 +674,9 @@
     kernels = remap_weight.reshape(peers * slots, width, width)
     slot_rows = slots * channels
 
-    smem = pl.BlockSpec(memory_space=pltpu.SMEM)
     vmem = pl.BlockSpec(memory_space=pltpu.VMEM)
 
-    anywhere = pl.BlockSpec(memory_space=pl.ANY)
+    far = pl.BlockSpec(memory_space=pltpu.HBM)
     parts = math.gcd(peers, 4)
     outgoing, by_row = pl.pallas_call(
         functools.partial(send_kernel, rows, peers, slots),
@@ -639,12 +685,16 @@
             jax.ShapeDtypeStruct((devices, slot_rows, width), bf16),
             jax.ShapeDtypeStruct((rows, channels, width), f32),
         ),
-        in_specs=[smem, smem, vmem, anywhere],
+        in_specs=[far] * 4,
         out_specs=(vmem, vmem),
         scratch_shapes=[
             pltpu.VMEM((devices, slot_rows, width), f32),
             pltpu.VMEM(kernels.shape, bf16),
             pltpu.SemaphoreType.DMA((parts,)),
+            pltpu.SMEM(source.shape, jnp.int32),
+            pltpu.SMEM(count.shape, jnp.int32),
+            pltpu.VMEM(surface.shape, f32),
+            pltpu.SemaphoreType.DMA((3,)),
         ],
     )(source, count, surface, kernels)
     arrived = lax.all_to_all(outgoing, EVERYWHERE, 0, 0, tiled=True)
@@ -677,6 +727,18 @@
         return (pltpu.VMEM(*args), pltpu.VMEM(*args))
 
     tall = (rows, channels, width)
+    tables = (
+        mask,
+        diffusivity,
+        coupling,
+        w_first,
+        w_second,
+        b_second,
+        w_third,
+        w_third_back,
+        w_second_back,
+        w_first_back,
+    )
     new_state, base, diffuse, leaving = pl.pallas_call(
         functools.partial(main_kernel, rows, peers, slots, share, small_share),
         name="main",
@@ -686,16 +748,17 @@
             jax.ShapeDtypeStruct((rows, channels, width), f32),
             jax.ShapeDtypeStruct((devices, slot_rows + packed, width), bf16),
         ),
-        in_specs=[smem, smem, anywhere, anywhere, vmem, anywhere] + [vmem] * 9,
-        out_specs=(anywhere,) * 3 + (vmem,),
+        in_specs=[vmem] * 3 + [far] * FETCHED,
+        out_specs=(far,) * 3 + (vmem,),
         scratch_shapes=[
-            pltpu.VMEM((rows, channels, width), f32),
-            pltpu.VMEM((channels * rows, width), f32),
-            pltpu.VMEM((devices, slot_rows, width), bf16),
+            pltpu.SMEM(landing.shape, jnp.int32),
+            pltpu.SMEM(b_out.shape, f32),
+            *(pltpu.VMEM(array.shape, array.dtype) for array in tables),
+            pltpu.SemaphoreType.DMA((FETCHED,)),
+            pltpu.SemaphoreType.DMA((4,)),
             pltpu.VMEM((channels * rows, width), f32),
             pltpu.VMEM(tall, f32),
             pltpu.VMEM((rows, channels, width), f32),
-            pltpu.SemaphoreType.DMA((7,)),
             pltpu.VMEM((devices, slot_rows + packed, width), f32),
             pltpu.VMEM(tall, f32),
             pltpu.VMEM(tall, f32),
@@ -717,21 +780,12 @@
             pltpu.VMEM((max(48, small_share * devices), width), f32),
         ],
     )(
+        near(by_row),
+        near(goal),
+        near(arrived),
         landing,
         b_out,
-        by_row,
-        goal,
-        mask,
-        arrived,
-        diffusivity,
-        coupling,
-        w_first,
-        w_second,
-        b_second,
-        w_third,
-        w_third_back,
-        w_second_back,
-        w_first_back,
+        *tables,
     )
     returned = lax.all_to_all(leaving, EVERYWHERE, 0, 0, tiled=True)
     scale = 1.0 / (rows * width * tiles)
@@ -739,27 +793,27 @@
         functools.partial(sum_kernel, scale, share, small_share),
         name="sum",
         out_shape=jax.ShapeDtypeStruct((devices, packed, width), bf16),
-        in_specs=[anywhere],
+        in_specs=[vmem],
         out_specs=vmem,
-        scratch_shapes=[
-            pltpu.VMEM((devices, packed, width), bf16),
-            pltpu.VMEM((packed, width), f32),
-            pltpu.SemaphoreType.DMA,
-        ],
-    )(returned)
+        scratch_shapes=[pltpu.VMEM((packed, width), f32)],
+    )(near(returned))
     gathered = lax.all_to_all(summed, EVERYWHERE, 0, 0, tiled=True)
     adjoint = pl.pallas_call(
         functools.partial(back_kernel, rows, peers, slots),
         name="back",
         out_shape=jax.ShapeDtypeStruct((channels * rows, width), f32),
-        in_specs=[smem, smem, anywhere] + [vmem] * 4,
+        in_specs=[vmem] * 2 + [far] * 5,
         out_specs=vmem,
         scratch_shapes=[
-            pltpu.VMEM((rows, channels, width), f32),
-            pltpu.VMEM((devices, slot_rows, width), bf16),
-            pltpu.SemaphoreType.DMA,
+            pltpu.SMEM(source.shape, jnp.int32),
+            pltpu.SMEM(count.shape, jnp.int32),
+            pltpu.VMEM(diffusivity.shape, f32),
+            pltpu.VMEM(tall, f32),
+            pltpu.VMEM(tall, f32),
+            pltpu.VMEM(tall, f32),
+            pltpu.SemaphoreType.DMA((5,)),
         ],
-    )(source, count, returned, kernels, base, diffuse, diffusivity)
+    )(near(returned), kernels, source, count, diffusivity, base, diffuse)
     first, bias_one, second, bias_two, third, bias_three = pl.pallas_call(
         functools.partial(unpack_kernel, share, small_share, fluxes),
         name="unpack",
@@ -771,14 +825,10 @@
             jax.ShapeDtypeStruct((fluxes, hidden), f32),
             jax.ShapeDtypeStruct((1, fluxes), f32),
         ),
-        in_specs=[anywhere],
+        in_specs=[vmem],
         out_specs=(vmem,) * 6,
-        scratch_shapes=[
-            pltpu.VMEM((devices, packed, width), bf16),
-            pltpu.VMEM((max(48, small_share * devices), width), f32),
-            pltpu.SemaphoreType.DMA,
-        ],
-    )(gathered)
+        scratch_shapes=[pltpu.VMEM((max(48, small_share * devices), width), f32)],
+    )(near(gathered))
     return (
         new_state.reshape(state.shape),
         adjoint.reshape(state.shape),
@@ -789,6 +839,10 @@
         third.T,
         bias_three[0],
     )
+
+
+def near(array):
+    return pltpu.with_memory_space_constraint(array, pltpu.VMEM)
 
 
 def solution(mesh):

time: 82.1 us -> 77.2 us (0.940)
  Pallas kernels: 39.7 us -> 36.9 us
  local copies, waits for them, and re-layouts: 5.98 us -> 4.56 us
    unnamed x20, local copies, waits for them, and re-layouts: 2.25 us -> 0.87 us
    pallas_call x1, Pallas kernels: 25 us -> 24.1 us  [shards(): pl.pallas_call(functools.partial(main_kernel, rows, peers, slots, share,...]
    pallas_call x1, Pallas kernels: 1.67 us -> 0.74 us  [shards(): pl.pallas_call(functools.partial(unpack_kernel, share, small_share, fluxe...]
    pallas_call x1, Pallas kernels: 1.67 us -> 0.74 us  [shards(): pl.pallas_call(functools.partial(sum_kernel, scale, share, small_share),...]
  transfers between devices with their start and end apart: 2 -> 2, of which waited for: 2 -> 2; matrix products, arithmetic and copies ran while one was open for 6% -> 7% of each run, Pallas kernels for 9% -> 10%
where the time goes in v6:
time: 77.2 us; the launch traced here: 76.8 us
  Pallas kernels  36.9 us (48%)
  blocking collectives  15.6 us (20%)
  starting transfers between devices  11.4 us (15%)
  waiting for transfers between devices  6.78 us (9%)
  local copies, waits for them, and re-layouts  4.56 us (6%)
  between operations  0.86 us (1%)
    pallas_call x1, Pallas kernels, shards(): pl.pallas_call(functools.partial(main_kernel, rows, peers, slots, share,...  24.1 us
    all_to_all x1, blocking collectives, shards(): returned = lax.all_to_all(leaving, EVERYWHERE, 0, 0, tiled=True)  15.6 us
    pallas_call x1, Pallas kernels, shards(): pl.pallas_call(functools.partial(back_kernel, rows, peers, slots), name='...  7.42 us
    all_to_all x1, starting transfers between devices, shards(): arrived = lax.all_to_all(outgoing, EVERYWHERE, 0, 0, tiled=True)  7.33 us
    all_to_all x1, waiting for transfers between devices, shards(): arrived = lax.all_to_all(outgoing, EVERYWHERE, 0, 0, tiled=True)  4.9 us
    all_to_all x1, starting transfers between devices, shards(): gathered = lax.all_to_all(summed, EVERYWHERE, 0, 0, tiled=True)  4.04 us
    pallas_call x1, Pallas kernels, shards(): pl.pallas_call(functools.partial(send_kernel, rows, peers, slots), name='...  3.91 us
    all_to_all x1, waiting for transfers between devices, shards(): gathered = lax.all_to_all(summed, EVERYWHERE, 0, 0, tiled=True)  1.88 us
  transfers between devices with their start and end apart: 2, of which 2 were waited for; matrix products, arithmetic and copies ran while one was open for 7% of the time, Pallas kernels for 10%

profile of v6, /device:TPU:0, one launch (start us, length us, event | category | flops | bytes accessed | tf_op | source)
XLA Modules:
  0.0 76.8 jit_solution(10829522406587115593)
XLA Ops:
  0.6 0.0 copy-start.7
  0.6 0.0 copy-start.4
  0.7 0.0 copy-start.5
  0.7 0.0 copy-start.6
  0.7 0.0 copy-start.8
  0.7 0.0 copy-start.2
  0.7 0.0 copy-start
  0.7 3.9 %send.1 = (bf16[32,32,128]{2,1,0:T(8,128)(2,1)}, f32[128,8,128]{2,1,0:T(8,128)}) custom-call(s32[4,16]{1,0:T(4,128)} %bitcast.29, s32[16]{0:T(128)} %bitcast.34, f32[1024,128]{1,0:T(8,128)} %bitcast.26, bf16[64,128,128]{2,1,0:T(8,128)(2,1)} %bitcast.24), custom_call_target="tpu_custom_call" | custom-call | tf_op jit(solution)/shard_map/send/pallas_call | solution.py:681
  4.6 0.0 copy-start.1
  4.6 7.3 %all-to-all-start = ((bf16[32,32,128]{2,1,0:T(8,128)(2,1)}), bf16[32,32,128]{2,1,0:T(8,128)(2,1)S(1)}, u32[]{:S(2)}, u32[]{:S(2)}) async-start(bf16[32,32,128]{2,1,0:T(8,128)(2,1)} %get-tuple-element.21), calls=%async_computation | async-start | bytes 524288 | tf_op jit(solution)/shard_map/all_to_all | solution.py:700
  12.0 0.0 copy-done.7
  12.0 0.0 copy-done.4
  12.1 0.0 copy-done.5
  12.1 0.1 copy.32
  12.2 0.0 copy-start.3
  12.3 0.1 concatenate.8
  12.4 0.0 copy-done.6
  12.4 0.7 copy.34.refs_4_
  13.1 0.6 pad.8.refs_8_
  13.7 0.7 copy.35.refs_5_
  14.5 0.6 pad.9.refs_9_
  15.1 0.0 copy-done.8
  15.1 0.8 %copy.37.refs_7_ = f32[256,1]{1,0:T(8,128)} copy(f32[256,1]{0,1:T(1,128)S(1)} %bitcast.32) | data formatting | bytes 2048 | tf_op jit(solution)/shard_map/broadcast_in_dim | solution.py:715
  15.9 0.0 copy-done.2
  15.9 0.7 broadcast_multiply_fusion
  16.6 0.7 copy.36.refs_6_
  17.3 4.9 %all-to-all-done.recv = bf16[32,32,128]{2,1,0:T(8,128)(2,1)S(1)} async-done(((bf16[32,32,128]{2,1,0:T(8,128)(2,1)}), bf16[32,32,128]{2,1,0:T(8,128)(2,1)S(1)}, u32[]{:S(2)}, u32[]{:S(2)}) %all-to-all-start) | async-done | bytes 262176 | tf_op jit(solution)/shard_map/all_to_all | solution.py:700
  22.2 0.0 copy-done.3
  22.3 0.0 copy-done
  22.3 0.0 copy-done.1
  22.3 24.1 %main.1 = (f32[1024,128]{1,0:T(8,128)}, f32[128,8,128]{2,1,0:T(8,128)}, f32[128,8,128]{2,1,0:T(8,128)}, bf16[32,56,128]{2,1,0:T(8,128)(2,1)}) custom-call(f32[128,8,128]{2,1,0:T(8,128)S(1)} %copy-done.1, f32[1024,128]{1,0:T(8,128)S(1)} %bitcast.23, bf16[32,32,128]{2,1,0:T(8,128)(2,1)S(1)} %all-to-all-done.recv, s32[4,16]{1,0:T(4,128)} %bitcast.33, ...), custom_call_target="tpu_custom_call" | custom-call | tf_op jit(solution)/shard_map/main/pallas_call | solution.py:742
  46.3 15.6 %all_to_all.15.recv = bf16[32,56,128]{2,1,0:T(8,128)(2,1)S(1)} all-to-all(bf16[32,56,128]{2,1,0:T(8,128)(2,1)} %get-tuple-element.23), channel_id=1, replica_groups=mesh['comp'=2,'gy'=4,'gx'=4] {'comp','gy','gx'}, dimensions={0} | all-to-all | bytes 917504 | tf_op jit(solution)/shard_map/all_to_all | solution.py:790
  62.0 0.7 sum.1
  62.7 4.0 %all-to-all-start.2 = ((bf16[32,24,128]{2,1,0:T(8,128)(2,1)}), bf16[32,24,128]{2,1,0:T(8,128)(2,1)S(1)}, u32[]{:S(2)}, u32[]{:S(2)}) async-start(bf16[32,24,128]{2,1,0:T(8,128)(2,1)} %sum.1), calls=%async_computation.2 | async-start | bytes 393216 | tf_op jit(solution)/shard_map/all_to_all | solution.py:800
  66.8 7.4 %back.1 = f32[1024,128]{1,0:T(8,128)} custom-call(bf16[32,56,128]{2,1,0:T(8,128)(2,1)S(1)} %all_to_all.15.recv, bf16[64,128,128]{2,1,0:T(8,128)(2,1)} %bitcast.25, s32[4,16]{1,0:T(4,128)} %bitcast.30, s32[16]{0:T(128)} %bitcast.35, f32[2,8]{1,0:T(2,128)} %rate_in.1, f32[128,8,128]{2,1,0:T(8,128)} %get-tuple-element.24.base_in, ...), custom_call_target="tpu_custom_call" | custom-call | tf_op jit(solution)/shard_map/back/pallas_call | solution.py:801
  74.2 1.9 %all-to-all-done.2.recv = bf16[32,24,128]{2,1,0:T(8,128)(2,1)S(1)} async-done(((bf16[32,24,128]{2,1,0:T(8,128)(2,1)}), bf16[32,24,128]{2,1,0:T(8,128)(2,1)S(1)}, u32[]{:S(2)}, u32[]{:S(2)}) %all-to-all-start.2) | async-done | bytes 196640 | tf_op jit(solution)/shard_map/all_to_all | solution.py:800
  76.1 0.7 unpack.1
  (10 shorter events, 0.1 us)
Async XLA Ops:
  0.6 11.3 %copy-start.7 = (f32[256]{0:T(256)S(1)}, f32[256]{0:T(256)}, u32[]{:S(2)}) copy-start(f32[256]{0:T(256)} %param.21) | copy-start | bytes 3076
  0.6 11.4 %copy-start.4 = (bf16[16,256]{1,0:T(8,128)(2,1)S(1)}, bf16[16,256]{1,0:T(8,128)(2,1)}, u32[]{:S(2)}) copy-start(bf16[16,256]{1,0:T(8,128)(2,1)} %param.20) | copy-start | bytes 24580
  0.7 11.4 %copy-start.5 = (bf16[256,4]{0,1:T(4,128)(2,1)S(1)}, bf16[256,4]{0,1:T(4,128)(2,1)}, u32[]{:S(2)}) copy-start(bf16[256,4]{0,1:T(4,128)(2,1)} %param.24) | copy-start | bytes 6148
  0.7 11.8 %copy-start.6 = (f32[2,8,4]{1,2,0:T(4,128)S(1)}, f32[2,8,4]{1,2,0:T(4,128)}, u32[]{:S(2)}) copy-start(f32[2,8,4]{1,2,0:T(4,128)} %param.19) | copy-start | bytes 772
  0.7 14.4 %copy-start.8 = (f32[256]{0:T(256)S(1)}, f32[256]{0:T(256)}, u32[]{:S(2)}) copy-start(f32[256]{0:T(256)} %param.23) | copy-start | bytes 3076
  0.7 15.2 %copy-start.2 = (bf16[256,256]{1,0:T(8,128)(2,1)S(1)}, bf16[256,256]{1,0:T(8,128)(2,1)}, u32[]{:S(2)}) copy-start(bf16[256,256]{1,0:T(8,128)(2,1)} %param.22) | copy-start | bytes 393220
  0.7 21.6 %copy-start = (f32[1,8,128,128]{3,2,1,0:T(8,128)S(1)}, f32[1,8,128,128]{3,2,1,0:T(8,128)}, u32[]{:S(2)}) copy-start(f32[1,8,128,128]{3,2,1,0:T(8,128)} %param.16) | copy-start | bytes 1572868
  4.6 17.6 %copy-start.1 = (f32[128,8,128]{2,1,0:T(8,128)S(1)}, f32[128,8,128]{2,1,0:T(8,128)}, u32[]{:S(2)}) copy-start(f32[128,8,128]{2,1,0:T(8,128)} %get-tuple-element.20.state) | copy-start | bytes 1572868
  4.6 17.6 %all-to-all-start = ((bf16[32,32,128]{2,1,0:T(8,128)(2,1)}), bf16[32,32,128]{2,1,0:T(8,128)(2,1)S(1)}, u32[]{:S(2)}, u32[]{:S(2)}) async-start(bf16[32,32,128]{2,1,0:T(8,128)(2,1)} %get-tuple-element.21), calls=%async_computation | async-start | bytes 524288 | tf_op jit(solution)/shard_map/all_to_all | solution.py:700
  12.2 10.0 %copy-start.3 = (bf16[16,256]{1,0:T(8,128)(2,1)}, bf16[16,256]{1,0:T(8,128)(2,1)S(1)}, u32[]{:S(2)}) copy-start(bf16[16,256]{1,0:T(8,128)(2,1)S(1)} %maximum_select_fusion.refs_11_) | copy-start | bytes 24580
  62.7 13.4 %all-to-all-start.2 = ((bf16[32,24,128]{2,1,0:T(8,128)(2,1)}), bf16[32,24,128]{2,1,0:T(8,128)(2,1)S(1)}, u32[]{:S(2)}, u32[]{:S(2)}) async-start(bf16[32,24,128]{2,1,0:T(8,128)(2,1)} %sum.1), calls=%async_computation.2 | async-start | bytes 393216 | tf_op jit(solution)/shard_map/all_to_all | solution.py:800

commit v7 on v6

--- a/solution.py
+++ b/solution.py
@@ -12,6 +12,7 @@
 BLOCK_ROWS = 8
 CHUNK = 256
 FETCHED = 12
+SMALL_PLANE = 3
 SUBLANES = 8
 
 KEYS = {
@@ -93,8 +94,11 @@
     stage[meta[EAST], 0:SUBLANES, :] = last
     stage[meta[WEST], SUBLANES : 2 * SUBLANES, :] = first
     top = jnp.where(meta[ON_FOLD] == 1, mirror(top), top)
-    stage[meta[NORTH], 2 * SUBLANES : 3 * SUBLANES, :] = top
-    stage[meta[SOUTH], 3 * SUBLANES : 4 * SUBLANES, :] = bottom
+    straight = jnp.logical_and(meta[HAS_NORTH] == 1, meta[ON_FOLD] == 0)
+    up = pl.multiple_of(jnp.where(straight, 0, 2 * SUBLANES), SUBLANES)
+    down = pl.multiple_of(jnp.where(meta[HAS_SOUTH] == 1, SUBLANES, 2 * SUBLANES), SUBLANES)
+    stage[meta[SOUTH], pl.ds(down, SUBLANES), :] = bottom
+    stage[meta[NORTH], pl.ds(up, SUBLANES), :] = top
 
 
 def take_edges(tile, r, lane, sides):
@@ -109,12 +113,12 @@
 def get_edges(meta, recv):
     west = recv[meta[WEST], 0 : 4 * SUBLANES, :].astype(f32)[0:SUBLANES]
     east = recv[meta[EAST], 0 : 4 * SUBLANES, :].astype(f32)[SUBLANES : 2 * SUBLANES]
-    south = recv[meta[SOUTH], 0 : 4 * SUBLANES, :].astype(f32)[2 * SUBLANES : 3 * SUBLANES]
+    south = recv[meta[SOUTH], 0 : 4 * SUBLANES, :].astype(f32)[0:SUBLANES]
     above = recv[meta[NORTH], 0 : 4 * SUBLANES, :].astype(f32)
     north = jnp.where(
         meta[ON_FOLD] == 1,
         above[2 * SUBLANES : 3 * SUBLANES],
-        above[3 * SUBLANES : 4 * SUBLANES],
+        above[SUBLANES : 2 * SUBLANES],
     )
     south = jnp.where(meta[HAS_SOUTH] == 1, south, 0.0)
     north = jnp.where(meta[HAS_NORTH] == 1, north, 0.0)
@@ -152,7 +156,7 @@
     small = fetch_all([(state_in, state), (source_in, source), (count_in, count)], small_sems)
     width = state.shape[1]
     shape = (SUBLANES, width)
-    lane = lax.broadcasted_iota(jnp.int32, shape, 1)
+    sub = lax.broadcasted_iota(jnp.int32, shape, 0)
     parts = sems.shape[0]
     part = peers // parts
     copies = [
@@ -170,13 +174,25 @@
     for copy in small:
         copy.wait()
 
-    def row_step(r, sides):
-        tile = state[pl.ds(r, SUBLANES, stride=rows), :]
-        by_row[r] = tile
-        return take_edges(tile, r, lane, sides)
-
-    zero = jnp.zeros(shape, f32)
-    first, last = lax.fori_loop(0, rows, row_step, (zero, zero), unroll=32)
+    def row_step(r, unused):
+        by_row[r] = state[pl.ds(r, SUBLANES, stride=rows), :]
+        return unused
+
+    lax.fori_loop(0, rows, row_step, 0, unroll=32)
+    wide = (16, width)
+    which = lax.broadcasted_iota(jnp.int32, wide, 0)
+    place_of = lax.broadcasted_iota(jnp.int32, wide, 1)
+    unit = jnp.logical_or(
+        jnp.logical_and(which == 0, place_of == 0),
+        jnp.logical_and(which == 1, place_of == width - 1),
+    )
+    unit = unit.astype(f32).astype(bf16)
+    first = jnp.zeros(shape, f32)
+    last = jnp.zeros(shape, f32)
+    for ch in range(SUBLANES):
+        both = dot_nt(unit, state[ch * rows : (ch + 1) * rows, :].astype(bf16))
+        first = jnp.where(sub == ch, jnp.broadcast_to(both[0:1], shape), first)
+        last = jnp.where(sub == ch, jnp.broadcast_to(both[1:2], shape), last)
     put_edges(meta, first, last, by_row[0], by_row[rows - 1], stage)
 
     def peer_step(q, unused):
@@ -305,6 +321,7 @@
     fluxes = couple_ref.shape[2]
     meta = place()
     slot_rows = recv.shape[1]
+    assert 2 * small_share <= SUBLANES
     other[...] = jnp.zeros(other.shape, f32)
     for copy in copies:
         copy.wait()
@@ -528,29 +545,35 @@
                     row : row + step, h * width : (h + 1) * width
                 ]
             done += step
-        piece = small[d * small_share : (d + 1) * small_share, :]
+    top = SMALL_PLANE * SUBLANES
+    for p in range(peers):
+        piece = small[p * small_share : (p + 1) * small_share, :]
         head = piece.astype(bf16).astype(f32)
-        top = slot_rows + share
-        stage[d, top : top + small_share, :] = head
-        stage[d, top + small_share : top + 2 * small_share, :] = piece - head
+        stage[meta[OWN] + p, top : top + small_share, :] = head
+        stage[meta[OWN] + p, top + small_share : top + 2 * small_share, :] = piece - head
     send_out[...] = stage[...].astype(bf16)
     for copy in (*stores, rest):
         copy.wait()
 
 
-def sum_kernel(scale, share, small_share, recv, out, stage):
+def sum_kernel(scale, peers, share, small_share, recv, out, stage):
     devices = recv.shape[0]
-    packed = stage.shape[0]
-    at = slice(recv.shape[1] - packed, recv.shape[1])
+    own = lax.axis_index("comp") * peers
+    slot_rows = 4 * SUBLANES
+    planes = slice(SMALL_PLANE * SUBLANES, (SMALL_PLANE + 1) * SUBLANES)
+    at = slice(slot_rows, slot_rows + -(-share // SUBLANES) * SUBLANES)
     total = recv[0, at, :].astype(f32)
     for d in range(1, devices):
         total = total + recv[d, at, :].astype(f32)
-    stage[...] = total * scale
-    low = slice(share + small_share, share + 2 * small_share)
-    piece = stage[share : share + small_share, :] + stage[low, :]
+    part = recv[own, planes, :].astype(f32)
+    for p in range(1, peers):
+        part = part + recv[own + p, planes, :].astype(f32)
+    part = part * scale
+    piece = part[0:small_share] + part[small_share : 2 * small_share]
     head = piece.astype(bf16).astype(f32)
+    stage[0:share, :] = total[0:share] * scale
     stage[share : share + small_share, :] = head
-    stage[low, :] = piece - head
+    stage[share + small_share : share + 2 * small_share, :] = piece - head
     total = stage[...].astype(bf16)
     for d in range(devices):
         out[d] = total
@@ -558,7 +581,7 @@
 
 def back_kernel(
     rows, peers, slots, recv, kernels, source_in, count_in, rate_in, base_in, diffuse_in, out,
-    source, count, rate_ref, base, diffuse, total, sems,
+    source, count, rate_ref, base, diffuse, total, blocks, sems, block_sems,
 ):
     meta = place()
     copies = fetch_all(
@@ -571,9 +594,12 @@
         ],
         sems,
     )
+    parts = block_sems.shape[0]
+    part = peers // parts
+    steps = [pl.ds(i * part * slots, part * slots) for i in range(parts)]
+    block_copies = fetch_all([(kernels.at[at], blocks.at[at]) for at in steps], block_sems)
     for copy in copies:
         copy.wait()
-    width = kernels.shape[2]
     width = diffuse.shape[2]
     shape = (SUBLANES, width)
     lane = lax.broadcasted_iota(jnp.int32, shape, 1)
@@ -588,7 +614,7 @@
         total[r] = base[r] + rate * laplace_row(here, below, above, west, east, r, lane)
         return unused
 
-    lax.fori_loop(0, rows, lap_step, 0, unroll=8)
+    lax.fori_loop(0, rows, lap_step, 0, unroll=32)
 
     def peer_step(q, unused):
         block = recv[meta[OTHER] + q, 0 : slots * SUBLANES, :].astype(f32)
@@ -597,21 +623,24 @@
             sent = block[s * SUBLANES : (s + 1) * SUBLANES].astype(bf16)
             live = (s < count[q]).astype(f32)
             row = source[s, q]
-            total[row] = total[row] + dot_nt(sent, kernels[k]) * live
+            total[row] = total[row] + dot_nt(sent, blocks[k]) * live
         return unused
 
-    lax.fori_loop(0, peers, peer_step, 0, unroll=4)
+    for i in range(parts):
+        block_copies[i].wait()
+        lax.fori_loop(i * part, (i + 1) * part, peer_step, 0, unroll=math.gcd(part, 4))
 
     def out_step(r, unused):
         out[pl.ds(r, SUBLANES, stride=rows), :] = total[r]
         return unused
 
-    lax.fori_loop(0, rows, out_step, 0, unroll=8)
+    lax.fori_loop(0, rows, out_step, 0, unroll=32)
 
 
 def unpack_kernel(share, small_share, fluxes, recv, first, bias_one, second, bias_two, third,
                   bias_three, small):
     devices = recv.shape[0]
+    peers = devices // 2
     width = recv.shape[2]
     hidden = second.shape[0]
     halves = hidden // width
@@ -625,10 +654,14 @@
             if h < halves:
                 second[row : row + step, h * width : (h + 1) * width] = block[done : done + step]
             done += step
-        small[d * small_share : (d + 1) * small_share, :] = (
+        piece = (
             block[share : share + small_share]
             + block[share + small_share : share + 2 * small_share]
         )
+        at = d % peers * small_share
+        if d >= peers:
+            piece = piece + small[at : at + small_share, :]
+        small[at : at + small_share, :] = piece
     for h in range(halves):
         cols = slice(h * width, (h + 1) * width)
         top = h * 24
@@ -719,7 +752,8 @@
     w_first_back = local_in
 
     share = -(-hidden * hidden // (width * devices))
-    small_share = -(-24 * hidden // (width * devices))
+    small_share = -(-24 * hidden // (width * tiles))
+    sent = -(-share // 8) * 8
     packed = -(-(share + 2 * small_share) // 8) * 8
     cells = BLOCK_ROWS * width
 
@@ -746,7 +780,7 @@
             jax.ShapeDtypeStruct((channels * rows, width), f32),
             jax.ShapeDtypeStruct(tall, f32),
             jax.ShapeDtypeStruct((rows, channels, width), f32),
-            jax.ShapeDtypeStruct((devices, slot_rows + packed, width), bf16),
+            jax.ShapeDtypeStruct((devices, slot_rows + sent, width), bf16),
         ),
         in_specs=[vmem] * 3 + [far] * FETCHED,
         out_specs=(far,) * 3 + (vmem,),
@@ -759,7 +793,7 @@
             pltpu.VMEM((channels * rows, width), f32),
             pltpu.VMEM(tall, f32),
             pltpu.VMEM((rows, channels, width), f32),
-            pltpu.VMEM((devices, slot_rows + packed, width), f32),
+            pltpu.VMEM((devices, slot_rows + sent, width), f32),
             pltpu.VMEM(tall, f32),
             pltpu.VMEM(tall, f32),
             twice((BLOCK_ROWS, 32, width), bf16),
@@ -777,7 +811,7 @@
             pltpu.VMEM((16, hidden), f32),
             pltpu.VMEM((8, width), f32),
             pltpu.VMEM((2, 8, width), f32),
-            pltpu.VMEM((max(48, small_share * devices), width), f32),
+            pltpu.VMEM((max(48, small_share * tiles), width), f32),
         ],
     )(
         near(by_row),
@@ -790,7 +824,7 @@
     returned = lax.all_to_all(leaving, EVERYWHERE, 0, 0, tiled=True)
     scale = 1.0 / (rows * width * tiles)
     summed = pl.pallas_call(
-        functools.partial(sum_kernel, scale, share, small_share),
+        functools.partial(sum_kernel, scale, peers, share, small_share),
         name="sum",
         out_shape=jax.ShapeDtypeStruct((devices, packed, width), bf16),
         in_specs=[vmem],
@@ -802,7 +836,7 @@
         functools.partial(back_kernel, rows, peers, slots),
         name="back",
         out_shape=jax.ShapeDtypeStruct((channels * rows, width), f32),
-        in_specs=[vmem] * 2 + [far] * 5,
+        in_specs=[vmem] + [far] * 6,
         out_specs=vmem,
         scratch_shapes=[
             pltpu.SMEM(source.shape, jnp.int32),
@@ -811,7 +845,9 @@
             pltpu.VMEM(tall, f32),
             pltpu.VMEM(tall, f32),
             pltpu.VMEM(tall, f32),
+            pltpu.VMEM(kernels.shape, bf16),
             pltpu.SemaphoreType.DMA((5,)),
+            pltpu.SemaphoreType.DMA((parts,)),
         ],
     )(near(returned), kernels, source, count, diffusivity, base, diffuse)
     first, bias_one, second, bias_two, third, bias_three = pl.pallas_call(
@@ -827,7 +863,7 @@
         ),
         in_specs=[vmem],
         out_specs=(vmem,) * 6,
-        scratch_shapes=[pltpu.VMEM((max(48, small_share * devices), width), f32)],
+        scratch_shapes=[pltpu.VMEM((max(48, small_share * tiles), width), f32)],
     )(near(gathered))
     return (
         new_state.reshape(state.shape),

time: 77.2 us -> 75.6 us (0.979)
  Pallas kernels: 36.9 us -> 34.4 us
  waiting for transfers between devices: 6.78 us -> 8.93 us
  blocking collectives: 15.6 us -> 14.5 us
    all_to_all x1, waiting for transfers between devices: 1.88 us -> 4.03 us  [shards(): gathered = lax.all_to_all(summed, EVERYWHERE, 0, 0, tiled=True)]
    pallas_call x1, Pallas kernels: 7.42 us -> 5.27 us  [shards(): pl.pallas_call(functools.partial(back_kernel, rows, peers, slots), name='...]
    all_to_all x1, blocking collectives: 15.6 us -> 14.5 us  [shards(): returned = lax.all_to_all(leaving, EVERYWHERE, 0, 0, tiled=True)]
  transfers between devices with their start and end apart: 2 -> 2, of which waited for: 2 -> 2; matrix products, arithmetic and copies ran while one was open for 7% -> 7% of each run, Pallas kernels for 10% -> 7%
where the time goes in v7:
time: 75.6 us; the launch traced here: 75.1 us
  Pallas kernels  34.4 us (46%)
  blocking collectives  14.5 us (19%)
  starting transfers between devices  11.1 us (15%)
  waiting for transfers between devices  8.93 us (12%)
  local copies, waits for them, and re-layouts  4.56 us (6%)
  between operations  0.86 us (1%)
    pallas_call x1, Pallas kernels, shards(): pl.pallas_call(functools.partial(main_kernel, rows, peers, slots, share,...  24 us
    all_to_all x1, blocking collectives, shards(): returned = lax.all_to_all(leaving, EVERYWHERE, 0, 0, tiled=True)  14.5 us
    all_to_all x1, starting transfers between devices, shards(): arrived = lax.all_to_all(outgoing, EVERYWHERE, 0, 0, tiled=True)  7.33 us
    pallas_call x1, Pallas kernels, shards(): pl.pallas_call(functools.partial(back_kernel, rows, peers, slots), name='...  5.27 us
    all_to_all x1, waiting for transfers between devices, shards(): arrived = lax.all_to_all(outgoing, EVERYWHERE, 0, 0, tiled=True)  4.9 us
    all_to_all x1, waiting for transfers between devices, shards(): gathered = lax.all_to_all(summed, EVERYWHERE, 0, 0, tiled=True)  4.03 us
    all_to_all x1, starting transfers between devices, shards(): gathered = lax.all_to_all(summed, EVERYWHERE, 0, 0, tiled=True)  3.76 us
    pallas_call x1, Pallas kernels, shards(): pl.pallas_call(functools.partial(send_kernel, rows, peers, slots), name='...  3.66 us
  transfers between devices with their start and end apart: 2, of which 2 were waited for; matrix products, arithmetic and copies ran while one was open for 7% of the time, Pallas kernels for 7%

profile of v7, /device:TPU:0, one launch (start us, length us, event | category | flops | bytes accessed | tf_op | source)
XLA Modules:
  0.0 75.1 jit_solution(1157947866219111072)
XLA Ops:
  0.6 0.0 copy-start.7
  0.6 0.0 copy-start.4
  0.7 0.0 copy-start.5
  0.7 0.0 copy-start.6
  0.7 0.0 copy-start.8
  0.7 0.0 copy-start.2
  0.7 0.0 copy-start
  0.7 3.7 %send.1 = (bf16[32,32,128]{2,1,0:T(8,128)(2,1)}, f32[128,8,128]{2,1,0:T(8,128)}) custom-call(s32[4,16]{1,0:T(4,128)} %bitcast.29, s32[16]{0:T(128)} %bitcast.34, f32[1024,128]{1,0:T(8,128)} %bitcast.26, bf16[64,128,128]{2,1,0:T(8,128)(2,1)} %bitcast.24), custom_call_target="tpu_custom_call" | custom-call | tf_op jit(solution)/shard_map/send/pallas_call | solution.py:714
  4.4 0.0 copy-start.1
  4.4 7.3 %all-to-all-start = ((bf16[32,32,128]{2,1,0:T(8,128)(2,1)}), bf16[32,32,128]{2,1,0:T(8,128)(2,1)S(1)}, u32[]{:S(2)}, u32[]{:S(2)}) async-start(bf16[32,32,128]{2,1,0:T(8,128)(2,1)} %get-tuple-element.21), calls=%async_computation | async-start | bytes 524288 | tf_op jit(solution)/shard_map/all_to_all | solution.py:733
  11.7 0.0 copy-done.7
  11.8 0.0 copy-done.4
  11.8 0.0 copy-done.5
  11.8 0.1 copy.32
  12.0 0.0 copy-start.3
  12.0 0.1 concatenate.8
  12.2 0.0 copy-done.6
  12.2 0.7 copy.34.refs_4_
  12.9 0.6 pad.8.refs_8_
  13.5 0.7 copy.35.refs_5_
  14.2 0.6 pad.9.refs_9_
  14.9 0.0 copy-done.8
  14.9 0.8 %copy.37.refs_7_ = f32[256,1]{1,0:T(8,128)} copy(f32[256,1]{0,1:T(1,128)S(1)} %bitcast.32) | data formatting | bytes 2048 | tf_op jit(solution)/shard_map/broadcast_in_dim | solution.py:748
  15.7 0.0 copy-done.2
  15.7 0.7 broadcast_multiply_fusion
  16.4 0.7 copy.36.refs_6_
  17.1 4.9 %all-to-all-done.recv = bf16[32,32,128]{2,1,0:T(8,128)(2,1)S(1)} async-done(((bf16[32,32,128]{2,1,0:T(8,128)(2,1)}), bf16[32,32,128]{2,1,0:T(8,128)(2,1)S(1)}, u32[]{:S(2)}, u32[]{:S(2)}) %all-to-all-start) | async-done | bytes 262176 | tf_op jit(solution)/shard_map/all_to_all | solution.py:733
  22.0 0.0 copy-done.3
  22.0 0.0 copy-done
  22.0 0.0 copy-done.1
  22.0 24.0 %main.1 = (f32[1024,128]{1,0:T(8,128)}, f32[128,8,128]{2,1,0:T(8,128)}, f32[128,8,128]{2,1,0:T(8,128)}, bf16[32,48,128]{2,1,0:T(8,128)(2,1)}) custom-call(f32[128,8,128]{2,1,0:T(8,128)S(1)} %copy-done.1, f32[1024,128]{1,0:T(8,128)S(1)} %bitcast.23, bf16[32,32,128]{2,1,0:T(8,128)(2,1)S(1)} %all-to-all-done.recv, s32[4,16]{1,0:T(4,128)} %bitcast.33, ...), custom_call_target="tpu_custom_call" | custom-call | tf_op jit(solution)/shard_map/main/pallas_call | solution.py:776
  46.1 14.5 %all_to_all.15.recv = bf16[32,48,128]{2,1,0:T(8,128)(2,1)S(1)} all-to-all(bf16[32,48,128]{2,1,0:T(8,128)(2,1)} %get-tuple-element.23), channel_id=1, replica_groups=mesh['comp'=2,'gy'=4,'gx'=4] {'comp','gy','gx'}, dimensions={0} | all-to-all | bytes 786432 | tf_op jit(solution)/shard_map/all_to_all | solution.py:824
  60.6 0.7 sum.1
  61.3 3.8 %all-to-all-start.2 = ((bf16[32,24,128]{2,1,0:T(8,128)(2,1)}), bf16[32,24,128]{2,1,0:T(8,128)(2,1)S(1)}, u32[]{:S(2)}, u32[]{:S(2)}) async-start(bf16[32,24,128]{2,1,0:T(8,128)(2,1)} %sum.1), calls=%async_computation.2 | async-start | bytes 393216 | tf_op jit(solution)/shard_map/all_to_all | solution.py:834
  65.1 5.3 %back.1 = f32[1024,128]{1,0:T(8,128)} custom-call(bf16[32,48,128]{2,1,0:T(8,128)(2,1)S(1)} %all_to_all.15.recv, bf16[64,128,128]{2,1,0:T(8,128)(2,1)} %bitcast.25, s32[4,16]{1,0:T(4,128)} %bitcast.30, s32[16]{0:T(128)} %bitcast.35, f32[2,8]{1,0:T(2,128)} %rate_in.1, f32[128,8,128]{2,1,0:T(8,128)} %get-tuple-element.24.base_in, ...), custom_call_target="tpu_custom_call" | custom-call | tf_op jit(solution)/shard_map/back/pallas_call | solution.py:835
  70.4 4.0 %all-to-all-done.2.recv = bf16[32,24,128]{2,1,0:T(8,128)(2,1)S(1)} async-done(((bf16[32,24,128]{2,1,0:T(8,128)(2,1)}), bf16[32,24,128]{2,1,0:T(8,128)(2,1)S(1)}, u32[]{:S(2)}, u32[]{:S(2)}) %all-to-all-start.2) | async-done | bytes 196640 | tf_op jit(solution)/shard_map/all_to_all | solution.py:834
  74.4 0.7 unpack.1
  (10 shorter events, 0.1 us)
Async XLA Ops:
  0.6 11.1 %copy-start.7 = (f32[256]{0:T(256)S(1)}, f32[256]{0:T(256)}, u32[]{:S(2)}) copy-start(f32[256]{0:T(256)} %param.21) | copy-start | bytes 3076
  0.6 11.1 %copy-start.4 = (bf16[16,256]{1,0:T(8,128)(2,1)S(1)}, bf16[16,256]{1,0:T(8,128)(2,1)}, u32[]{:S(2)}) copy-start(bf16[16,256]{1,0:T(8,128)(2,1)} %param.20) | copy-start | bytes 24580
  0.7 11.2 %copy-start.5 = (bf16[256,4]{0,1:T(4,128)(2,1)S(1)}, bf16[256,4]{0,1:T(4,128)(2,1)}, u32[]{:S(2)}) copy-start(bf16[256,4]{0,1:T(4,128)(2,1)} %param.24) | copy-start | bytes 6148
  0.7 11.5 %copy-start.6 = (f32[2,8,4]{1,2,0:T(4,128)S(1)}, f32[2,8,4]{1,2,0:T(4,128)}, u32[]{:S(2)}) copy-start(f32[2,8,4]{1,2,0:T(4,128)} %param.19) | copy-start | bytes 772
  0.7 14.2 %copy-start.8 = (f32[256]{0:T(256)S(1)}, f32[256]{0:T(256)}, u32[]{:S(2)}) copy-start(f32[256]{0:T(256)} %param.23) | copy-start | bytes 3076
  0.7 15.0 %copy-start.2 = (bf16[256,256]{1,0:T(8,128)(2,1)S(1)}, bf16[256,256]{1,0:T(8,128)(2,1)}, u32[]{:S(2)}) copy-start(bf16[256,256]{1,0:T(8,128)(2,1)} %param.22) | copy-start | bytes 393220
  0.7 21.3 %copy-start = (f32[1,8,128,128]{3,2,1,0:T(8,128)S(1)}, f32[1,8,128,128]{3,2,1,0:T(8,128)}, u32[]{:S(2)}) copy-start(f32[1,8,128,128]{3,2,1,0:T(8,128)} %param.16) | copy-start | bytes 1572868
  4.4 17.6 %copy-start.1 = (f32[128,8,128]{2,1,0:T(8,128)S(1)}, f32[128,8,128]{2,1,0:T(8,128)}, u32[]{:S(2)}) copy-start(f32[128,8,128]{2,1,0:T(8,128)} %get-tuple-element.20.state) | copy-start | bytes 1572868
  4.4 17.6 %all-to-all-start = ((bf16[32,32,128]{2,1,0:T(8,128)(2,1)}), bf16[32,32,128]{2,1,0:T(8,128)(2,1)S(1)}, u32[]{:S(2)}, u32[]{:S(2)}) async-start(bf16[32,32,128]{2,1,0:T(8,128)(2,1)} %get-tuple-element.21), calls=%async_computation | async-start | bytes 524288 | tf_op jit(solution)/shard_map/all_to_all | solution.py:733
  12.0 10.0 %copy-start.3 = (bf16[16,256]{1,0:T(8,128)(2,1)}, bf16[16,256]{1,0:T(8,128)(2,1)S(1)}, u32[]{:S(2)}) copy-start(bf16[16,256]{1,0:T(8,128)(2,1)S(1)} %maximum_select_fusion.refs_11_) | copy-start | bytes 24580
  61.3 13.1 %all-to-all-start.2 = ((bf16[32,24,128]{2,1,0:T(8,128)(2,1)}), bf16[32,24,128]{2,1,0:T(8,128)(2,1)S(1)}, u32[]{:S(2)}, u32[]{:S(2)}) async-start(bf16[32,24,128]{2,1,0:T(8,128)(2,1)} %sum.1), calls=%async_computation.2 | async-start | bytes 393216 | tf_op jit(solution)/shard_map/all_to_all | solution.py:834

commit v8 on v7

--- a/solution.py
+++ b/solution.py
@@ -9,7 +9,7 @@
 from jax.sharding import PartitionSpec as P
 
 EVERYWHERE = ("comp", "gy", "gx")
-BLOCK_ROWS = 8
+BLOCK_ROWS = 16
 CHUNK = 256
 FETCHED = 12
 SMALL_PLANE = 3
@@ -17,16 +17,16 @@
 
 KEYS = {
     "take": (0.0, 0.05),
-    "first": (0.05, 0.3),
+    "first": (0, 0.267),
     "second": (0.3, 0.6),
     "third": (0.6, 0.65),
     "fields": (0.65, 1.0),
     "cot_second": (0.05, 0.3),
     "cot_first": (0.3, 0.6),
     "cot_inputs": (0.62, 0.7),
-    "leave": (0.9, 1.0),
+    "leave": (0.837, 1.099),
     "grad_second": 0.61,
-    "grad_third": 0.605,
+    "grad_third": 0.749,
     "grad_first": 0.71,
 }
 
@@ -323,6 +323,7 @@
     slot_rows = recv.shape[1]
     assert 2 * small_share <= SUBLANES
     other[...] = jnp.zeros(other.shape, f32)
+    misfits[...] = jnp.zeros(misfits.shape, f32)
     for copy in copies:
         copy.wait()
 
@@ -330,10 +331,11 @@
         block = recv[meta[OTHER] + p].astype(f32)
         for s in range(slots):
             row = landing[s, p]
-            other[row] = other[row] + block[s * SUBLANES : (s + 1) * SUBLANES]
+            sums = (other, misfits)[s % 2]
+            sums[row] = sums[row] + block[s * SUBLANES : (s + 1) * SUBLANES]
         return unused
 
-    lax.fori_loop(0, peers, land, 0, unroll=2)
+    lax.fori_loop(0, peers, land, 0, unroll=4)
     west, east, south, north = get_edges(meta, recv)
     comp = meta[COMP]
     rate = jnp.broadcast_to(column_of(rate_ref, comp), shape)
@@ -361,7 +363,8 @@
 
         def take(i):
             r = start + i
-            feat[i, 0:16, :] = jnp.concatenate([state[r], other[r]], axis=0).astype(bf16)
+            landed = other[r] + misfits[r]
+            feat[i, 0:16, :] = jnp.concatenate([state[r], landed], axis=0).astype(bf16)
 
         def layer(net, hid_ref, slope_ref, j):
             turn = jnp.tanh(net)

time: 75.6 us -> 74.1 us (0.980)
  Pallas kernels: 34.4 us -> 33 us
    pallas_call x1, Pallas kernels: 24 us -> 22.6 us  [shards(): pl.pallas_call(functools.partial(main_kernel, rows, peers, slots, share,...]
where the time goes in v8:
time: 74.1 us; the launch traced here: 73.7 us
  Pallas kernels  33 us (45%)
  blocking collectives  14.5 us (20%)
  starting transfers between devices  11.1 us (15%)
  waiting for transfers between devices  8.93 us (12%)
  local copies, waits for them, and re-layouts  4.56 us (6%)
  between operations  0.86 us (1%)
    pallas_call x1, Pallas kernels, shards(): pl.pallas_call(functools.partial(main_kernel, rows, peers, slots, share,...  22.6 us
    all_to_all x1, blocking collectives, shards(): returned = lax.all_to_all(leaving, EVERYWHERE, 0, 0, tiled=True)  14.5 us
    all_to_all x1, starting transfers between devices, shards(): arrived = lax.all_to_all(outgoing, EVERYWHERE, 0, 0, tiled=True)  7.33 us
    pallas_call x1, Pallas kernels, shards(): pl.pallas_call(functools.partial(back_kernel, rows, peers, slots), name='...  5.27 us
    all_to_all x1, waiting for transfers between devices, shards(): arrived = lax.all_to_all(outgoing, EVERYWHERE, 0, 0, tiled=True)  4.9 us
    all_to_all x1, waiting for transfers between devices, shards(): gathered = lax.all_to_all(summed, EVERYWHERE, 0, 0, tiled=True)  4.03 us
    all_to_all x1, starting transfers between devices, shards(): gathered = lax.all_to_all(summed, EVERYWHERE, 0, 0, tiled=True)  3.76 us
    pallas_call x1, Pallas kernels, shards(): pl.pallas_call(functools.partial(send_kernel, rows, peers, slots), name='...  3.66 us
  transfers between devices with their start and end apart: 2, of which 2 were waited for; matrix products, arithmetic and copies ran while one was open for 7% of the time, Pallas kernels for 7%

profile of v8, /device:TPU:0, one launch (start us, length us, event | category | flops | bytes accessed | tf_op | source)
XLA Modules:
  0.0 73.7 jit_solution(11415921067205705852)
XLA Ops:
  0.6 0.0 copy-start.7
  0.6 0.0 copy-start.4
  0.7 0.0 copy-start.5
  0.7 0.0 copy-start.6
  0.7 0.0 copy-start.8
  0.7 0.0 copy-start.2
  0.7 0.0 copy-start
  0.7 3.7 %send.1 = (bf16[32,32,128]{2,1,0:T(8,128)(2,1)}, f32[128,8,128]{2,1,0:T(8,128)}) custom-call(s32[4,16]{1,0:T(4,128)} %bitcast.29, s32[16]{0:T(128)} %bitcast.34, f32[1024,128]{1,0:T(8,128)} %bitcast.26, bf16[64,128,128]{2,1,0:T(8,128)(2,1)} %bitcast.24), custom_call_target="tpu_custom_call" | custom-call | tf_op jit(solution)/shard_map/send/pallas_call | solution.py:717
  4.4 0.0 copy-start.1
  4.4 7.3 %all-to-all-start = ((bf16[32,32,128]{2,1,0:T(8,128)(2,1)}), bf16[32,32,128]{2,1,0:T(8,128)(2,1)S(1)}, u32[]{:S(2)}, u32[]{:S(2)}) async-start(bf16[32,32,128]{2,1,0:T(8,128)(2,1)} %get-tuple-element.21), calls=%async_computation | async-start | bytes 524288 | tf_op jit(solution)/shard_map/all_to_all | solution.py:736
  11.7 0.0 copy-done.7
  11.8 0.0 copy-done.4
  11.8 0.0 copy-done.5
  11.8 0.1 copy.32
  12.0 0.0 copy-start.3
  12.0 0.1 concatenate.8
  12.2 0.0 copy-done.6
  12.2 0.7 copy.34.refs_4_
  12.9 0.6 pad.8.refs_8_
  13.5 0.7 copy.35.refs_5_
  14.2 0.6 pad.9.refs_9_
  14.9 0.0 copy-done.8
  14.9 0.8 %copy.37.refs_7_ = f32[256,1]{1,0:T(8,128)} copy(f32[256,1]{0,1:T(1,128)S(1)} %bitcast.32) | data formatting | bytes 2048 | tf_op jit(solution)/shard_map/broadcast_in_dim | solution.py:751
  15.7 0.0 copy-done.2
  15.7 0.7 broadcast_multiply_fusion
  16.4 0.7 %copy.36.refs_6_ = bf16[256,256]{1,0:T(8,128)(2,1)} copy(bf16[256,256]{0,1:T(8,128)(2,1)S(1)} %get-tuple-element.33) | data formatting | bytes 262144 | tf_op jit(solution)/shard_map/mul | solution.py:750
  17.1 4.9 %all-to-all-done.recv = bf16[32,32,128]{2,1,0:T(8,128)(2,1)S(1)} async-done(((bf16[32,32,128]{2,1,0:T(8,128)(2,1)}), bf16[32,32,128]{2,1,0:T(8,128)(2,1)S(1)}, u32[]{:S(2)}, u32[]{:S(2)}) %all-to-all-start) | async-done | bytes 262176 | tf_op jit(solution)/shard_map/all_to_all | solution.py:736
  22.0 0.0 copy-done.3
  22.0 0.0 copy-done
  22.0 0.0 copy-done.1
  22.0 22.6 %main.1 = (f32[1024,128]{1,0:T(8,128)}, f32[128,8,128]{2,1,0:T(8,128)}, f32[128,8,128]{2,1,0:T(8,128)}, bf16[32,48,128]{2,1,0:T(8,128)(2,1)}) custom-call(f32[128,8,128]{2,1,0:T(8,128)S(1)} %copy-done.1, f32[1024,128]{1,0:T(8,128)S(1)} %bitcast.23, bf16[32,32,128]{2,1,0:T(8,128)(2,1)S(1)} %all-to-all-done.recv, s32[4,16]{1,0:T(4,128)} %bitcast.33, ...), custom_call_target="tpu_custom_call" | custom-call | tf_op jit(solution)/shard_map/main/pallas_call | solution.py:779
  44.6 14.5 %all_to_all.15.recv = bf16[32,48,128]{2,1,0:T(8,128)(2,1)S(1)} all-to-all(bf16[32,48,128]{2,1,0:T(8,128)(2,1)} %get-tuple-element.23), channel_id=1, replica_groups=mesh['comp'=2,'gy'=4,'gx'=4] {'comp','gy','gx'}, dimensions={0} | all-to-all | bytes 786432 | tf_op jit(solution)/shard_map/all_to_all | solution.py:827
  59.2 0.7 sum.1
  59.9 3.8 %all-to-all-start.2 = ((bf16[32,24,128]{2,1,0:T(8,128)(2,1)}), bf16[32,24,128]{2,1,0:T(8,128)(2,1)S(1)}, u32[]{:S(2)}, u32[]{:S(2)}) async-start(bf16[32,24,128]{2,1,0:T(8,128)(2,1)} %sum.1), calls=%async_computation.2 | async-start | bytes 393216 | tf_op jit(solution)/shard_map/all_to_all | solution.py:837
  63.7 5.3 %back.1 = f32[1024,128]{1,0:T(8,128)} custom-call(bf16[32,48,128]{2,1,0:T(8,128)(2,1)S(1)} %all_to_all.15.recv, bf16[64,128,128]{2,1,0:T(8,128)(2,1)} %bitcast.25, s32[4,16]{1,0:T(4,128)} %bitcast.30, s32[16]{0:T(128)} %bitcast.35, f32[2,8]{1,0:T(2,128)} %rate_in.1, f32[128,8,128]{2,1,0:T(8,128)} %get-tuple-element.24.base_in, ...), custom_call_target="tpu_custom_call" | custom-call | tf_op jit(solution)/shard_map/back/pallas_call | solution.py:838
  68.9 4.0 %all-to-all-done.2.recv = bf16[32,24,128]{2,1,0:T(8,128)(2,1)S(1)} async-done(((bf16[32,24,128]{2,1,0:T(8,128)(2,1)}), bf16[32,24,128]{2,1,0:T(8,128)(2,1)S(1)}, u32[]{:S(2)}, u32[]{:S(2)}) %all-to-all-start.2) | async-done | bytes 196640 | tf_op jit(solution)/shard_map/all_to_all | solution.py:837
  73.0 0.7 %unpack.1 = (f32[16,256]{1,0:T(8,128)}, f32[1,256]{1,0:T(1,128)}, f32[256,256]{1,0:T(8,128)}, f32[1,256]{1,0:T(1,128)}, f32[4,256]{1,0:T(4,128)}, /*index=5*/f32[1,4]{1,0:T(1,128)}) custom-call(bf16[32,24,128]{2,1,0:T(8,128)(2,1)S(1)} %all-to-all-done.2.recv), custom_call_target="tpu_custom_call" | custom-call | tf_op jit(solution)/shard_map/unpack/pallas_call | solution.py:856
  (10 shorter events, 0.1 us)
Async XLA Ops:
  0.6 11.1 %copy-start.7 = (f32[256]{0:T(256)S(1)}, f32[256]{0:T(256)}, u32[]{:S(2)}) copy-start(f32[256]{0:T(256)} %param.21) | copy-start | bytes 3076
  0.6 11.1 %copy-start.4 = (bf16[16,256]{1,0:T(8,128)(2,1)S(1)}, bf16[16,256]{1,0:T(8,128)(2,1)}, u32[]{:S(2)}) copy-start(bf16[16,256]{1,0:T(8,128)(2,1)} %param.20) | copy-start | bytes 24580
  0.7 11.2 %copy-start.5 = (bf16[256,4]{0,1:T(4,128)(2,1)S(1)}, bf16[256,4]{0,1:T(4,128)(2,1)}, u32[]{:S(2)}) copy-start(bf16[256,4]{0,1:T(4,128)(2,1)} %param.24) | copy-start | bytes 6148
  0.7 11.5 %copy-start.6 = (f32[2,8,4]{1,2,0:T(4,128)S(1)}, f32[2,8,4]{1,2,0:T(4,128)}, u32[]{:S(2)}) copy-start(f32[2,8,4]{1,2,0:T(4,128)} %param.19) | copy-start | bytes 772
  0.7 14.2 %copy-start.8 = (f32[256]{0:T(256)S(1)}, f32[256]{0:T(256)}, u32[]{:S(2)}) copy-start(f32[256]{0:T(256)} %param.23) | copy-start | bytes 3076
  0.7 15.0 %copy-start.2 = (bf16[256,256]{1,0:T(8,128)(2,1)S(1)}, bf16[256,256]{1,0:T(8,128)(2,1)}, u32[]{:S(2)}) copy-start(bf16[256,256]{1,0:T(8,128)(2,1)} %param.22) | copy-start | bytes 393220
  0.7 21.3 %copy-start = (f32[1,8,128,128]{3,2,1,0:T(8,128)S(1)}, f32[1,8,128,128]{3,2,1,0:T(8,128)}, u32[]{:S(2)}) copy-start(f32[1,8,128,128]{3,2,1,0:T(8,128)} %param.16) | copy-start | bytes 1572868
  4.4 17.6 %copy-start.1 = (f32[128,8,128]{2,1,0:T(8,128)S(1)}, f32[128,8,128]{2,1,0:T(8,128)}, u32[]{:S(2)}) copy-start(f32[128,8,128]{2,1,0:T(8,128)} %get-tuple-element.20.state) | copy-start | bytes 1572868
  4.4 17.6 %all-to-all-start = ((bf16[32,32,128]{2,1,0:T(8,128)(2,1)}), bf16[32,32,128]{2,1,0:T(8,128)(2,1)S(1)}, u32[]{:S(2)}, u32[]{:S(2)}) async-start(bf16[32,32,128]{2,1,0:T(8,128)(2,1)} %get-tuple-element.21), calls=%async_computation | async-start | bytes 524288 | tf_op jit(solution)/shard_map/all_to_all | solution.py:736
  12.0 10.0 %copy-start.3 = (bf16[16,256]{1,0:T(8,128)(2,1)}, bf16[16,256]{1,0:T(8,128)(2,1)S(1)}, u32[]{:S(2)}) copy-start(bf16[16,256]{1,0:T(8,128)(2,1)S(1)} %maximum_select_fusion.refs_11_) | copy-start | bytes 24580
  59.9 13.1 %all-to-all-start.2 = ((bf16[32,24,128]{2,1,0:T(8,128)(2,1)}), bf16[32,24,128]{2,1,0:T(8,128)(2,1)S(1)}, u32[]{:S(2)}, u32[]{:S(2)}) async-start(bf16[32,24,128]{2,1,0:T(8,128)(2,1)} %sum.1), calls=%async_computation.2 | async-start | bytes 393216 | tf_op jit(solution)/shard_map/all_to_all | solution.py:837

commit v9 on v8

--- a/solution.py
+++ b/solution.py
@@ -516,7 +516,7 @@
             stage[meta[OTHER] + p, s * SUBLANES : (s + 1) * SUBLANES, :] = other[row]
         return unused
 
-    lax.fori_loop(0, peers, leave, 0, unroll=2)
+    lax.fori_loop(0, peers, leave, 0, unroll=8)
     put_edges(meta, edges[0], edges[1], diffuse_out[0], diffuse_out[rows - 1], stage)
     devices = stage.shape[0]
     halves = hidden // width

time: 74.1 us -> 74.1 us (level)
  no operation moved by 1% of the time
where the time goes in v9:
time: 74.1 us; the launch traced here: 73.7 us
  Pallas kernels  33 us (45%)
  blocking collectives  14.5 us (20%)
  starting transfers between devices  11.1 us (15%)
  waiting for transfers between devices  8.93 us (12%)
  local copies, waits for them, and re-layouts  4.56 us (6%)
  between operations  0.86 us (1%)
    pallas_call x1, Pallas kernels, shards(): pl.pallas_call(functools.partial(main_kernel, rows, peers, slots, share,...  22.6 us
    all_to_all x1, blocking collectives, shards(): returned = lax.all_to_all(leaving, EVERYWHERE, 0, 0, tiled=True)  14.5 us
    all_to_all x1, starting transfers between devices, shards(): arrived = lax.all_to_all(outgoing, EVERYWHERE, 0, 0, tiled=True)  7.33 us
    pallas_call x1, Pallas kernels, shards(): pl.pallas_call(functools.partial(back_kernel, rows, peers, slots), name='...  5.27 us
    all_to_all x1, waiting for transfers between devices, shards(): arrived = lax.all_to_all(outgoing, EVERYWHERE, 0, 0, tiled=True)  4.9 us
    all_to_all x1, waiting for transfers between devices, shards(): gathered = lax.all_to_all(summed, EVERYWHERE, 0, 0, tiled=True)  4.03 us
    all_to_all x1, starting transfers between devices, shards(): gathered = lax.all_to_all(summed, EVERYWHERE, 0, 0, tiled=True)  3.76 us
    pallas_call x1, Pallas kernels, shards(): pl.pallas_call(functools.partial(send_kernel, rows, peers, slots), name='...  3.66 us
  transfers between devices with their start and end apart: 2, of which 2 were waited for; matrix products, arithmetic and copies ran while one was open for 7% of the time, Pallas kernels for 7%

profile of v9, /device:TPU:0, one launch (start us, length us, event | category | flops | bytes accessed | tf_op | source)
XLA Modules:
  0.0 73.7 jit_solution(7312232669250138619)
XLA Ops:
  0.6 0.0 copy-start.7
  0.6 0.0 copy-start.4
  0.7 0.0 copy-start.5
  0.7 0.0 copy-start.6
  0.7 0.0 copy-start.8
  0.7 0.0 copy-start.2
  0.7 0.0 copy-start
  0.7 3.7 %send.1 = (bf16[32,32,128]{2,1,0:T(8,128)(2,1)}, f32[128,8,128]{2,1,0:T(8,128)}) custom-call(s32[4,16]{1,0:T(4,128)} %bitcast.29, s32[16]{0:T(128)} %bitcast.34, f32[1024,128]{1,0:T(8,128)} %bitcast.26, bf16[64,128,128]{2,1,0:T(8,128)(2,1)} %bitcast.24), custom_call_target="tpu_custom_call" | custom-call | tf_op jit(solution)/shard_map/send/pallas_call | solution.py:717
  4.4 0.0 copy-start.1
  4.4 7.3 %all-to-all-start = ((bf16[32,32,128]{2,1,0:T(8,128)(2,1)}), bf16[32,32,128]{2,1,0:T(8,128)(2,1)S(1)}, u32[]{:S(2)}, u32[]{:S(2)}) async-start(bf16[32,32,128]{2,1,0:T(8,128)(2,1)} %get-tuple-element.21), calls=%async_computation | async-start | bytes 524288 | tf_op jit(solution)/shard_map/all_to_all | solution.py:736
  11.7 0.0 copy-done.7
  11.8 0.0 copy-done.4
  11.8 0.0 copy-done.5
  11.8 0.1 copy.32
  12.0 0.0 copy-start.3
  12.0 0.1 concatenate.8
  12.2 0.0 copy-done.6
  12.2 0.7 copy.34.refs_4_
  12.9 0.6 pad.8.refs_8_
  13.5 0.7 copy.35.refs_5_
  14.2 0.6 pad.9.refs_9_
  14.9 0.0 copy-done.8
  14.9 0.8 %copy.37.refs_7_ = f32[256,1]{1,0:T(8,128)} copy(f32[256,1]{0,1:T(1,128)S(1)} %bitcast.32) | data formatting | bytes 2048 | tf_op jit(solution)/shard_map/broadcast_in_dim | solution.py:751
  15.7 0.0 copy-done.2
  15.7 0.7 broadcast_multiply_fusion
  16.4 0.7 %copy.36.refs_6_ = bf16[256,256]{1,0:T(8,128)(2,1)} copy(bf16[256,256]{0,1:T(8,128)(2,1)S(1)} %get-tuple-element.33) | data formatting | bytes 262144 | tf_op jit(solution)/shard_map/mul | solution.py:750
  17.1 4.9 %all-to-all-done.recv = bf16[32,32,128]{2,1,0:T(8,128)(2,1)S(1)} async-done(((bf16[32,32,128]{2,1,0:T(8,128)(2,1)}), bf16[32,32,128]{2,1,0:T(8,128)(2,1)S(1)}, u32[]{:S(2)}, u32[]{:S(2)}) %all-to-all-start) | async-done | bytes 262176 | tf_op jit(solution)/shard_map/all_to_all | solution.py:736
  22.0 0.0 copy-done.3
  22.0 0.0 copy-done
  22.0 0.0 copy-done.1
  22.0 22.6 %main.1 = (f32[1024,128]{1,0:T(8,128)}, f32[128,8,128]{2,1,0:T(8,128)}, f32[128,8,128]{2,1,0:T(8,128)}, bf16[32,48,128]{2,1,0:T(8,128)(2,1)}) custom-call(f32[128,8,128]{2,1,0:T(8,128)S(1)} %copy-done.1, f32[1024,128]{1,0:T(8,128)S(1)} %bitcast.23, bf16[32,32,128]{2,1,0:T(8,128)(2,1)S(1)} %all-to-all-done.recv, s32[4,16]{1,0:T(4,128)} %bitcast.33, ...), custom_call_target="tpu_custom_call" | custom-call | tf_op jit(solution)/shard_map/main/pallas_call | solution.py:779
  44.6 14.5 %all_to_all.15.recv = bf16[32,48,128]{2,1,0:T(8,128)(2,1)S(1)} all-to-all(bf16[32,48,128]{2,1,0:T(8,128)(2,1)} %get-tuple-element.23), channel_id=1, replica_groups=mesh['comp'=2,'gy'=4,'gx'=4] {'comp','gy','gx'}, dimensions={0} | all-to-all | bytes 786432 | tf_op jit(solution)/shard_map/all_to_all | solution.py:827
  59.1 0.7 sum.1
  59.9 3.8 %all-to-all-start.2 = ((bf16[32,24,128]{2,1,0:T(8,128)(2,1)}), bf16[32,24,128]{2,1,0:T(8,128)(2,1)S(1)}, u32[]{:S(2)}, u32[]{:S(2)}) async-start(bf16[32,24,128]{2,1,0:T(8,128)(2,1)} %sum.1), calls=%async_computation.2 | async-start | bytes 393216 | tf_op jit(solution)/shard_map/all_to_all | solution.py:837
  63.6 5.3 %back.1 = f32[1024,128]{1,0:T(8,128)} custom-call(bf16[32,48,128]{2,1,0:T(8,128)(2,1)S(1)} %all_to_all.15.recv, bf16[64,128,128]{2,1,0:T(8,128)(2,1)} %bitcast.25, s32[4,16]{1,0:T(4,128)} %bitcast.30, s32[16]{0:T(128)} %bitcast.35, f32[2,8]{1,0:T(2,128)} %rate_in.1, f32[128,8,128]{2,1,0:T(8,128)} %get-tuple-element.24.base_in, ...), custom_call_target="tpu_custom_call" | custom-call | tf_op jit(solution)/shard_map/back/pallas_call | solution.py:838
  68.9 4.0 %all-to-all-done.2.recv = bf16[32,24,128]{2,1,0:T(8,128)(2,1)S(1)} async-done(((bf16[32,24,128]{2,1,0:T(8,128)(2,1)}), bf16[32,24,128]{2,1,0:T(8,128)(2,1)S(1)}, u32[]{:S(2)}, u32[]{:S(2)}) %all-to-all-start.2) | async-done | bytes 196640 | tf_op jit(solution)/shard_map/all_to_all | solution.py:837
  72.9 0.7 %unpack.1 = (f32[16,256]{1,0:T(8,128)}, f32[1,256]{1,0:T(1,128)}, f32[256,256]{1,0:T(8,128)}, f32[1,256]{1,0:T(1,128)}, f32[4,256]{1,0:T(4,128)}, /*index=5*/f32[1,4]{1,0:T(1,128)}) custom-call(bf16[32,24,128]{2,1,0:T(8,128)(2,1)S(1)} %all-to-all-done.2.recv), custom_call_target="tpu_custom_call" | custom-call | tf_op jit(solution)/shard_map/unpack/pallas_call | solution.py:856
  (10 shorter events, 0.1 us)
Async XLA Ops:
  0.6 11.1 %copy-start.7 = (f32[256]{0:T(256)S(1)}, f32[256]{0:T(256)}, u32[]{:S(2)}) copy-start(f32[256]{0:T(256)} %param.21) | copy-start | bytes 3076
  0.6 11.1 %copy-start.4 = (bf16[16,256]{1,0:T(8,128)(2,1)S(1)}, bf16[16,256]{1,0:T(8,128)(2,1)}, u32[]{:S(2)}) copy-start(bf16[16,256]{1,0:T(8,128)(2,1)} %param.20) | copy-start | bytes 24580
  0.7 11.2 %copy-start.5 = (bf16[256,4]{0,1:T(4,128)(2,1)S(1)}, bf16[256,4]{0,1:T(4,128)(2,1)}, u32[]{:S(2)}) copy-start(bf16[256,4]{0,1:T(4,128)(2,1)} %param.24) | copy-start | bytes 6148
  0.7 11.5 %copy-start.6 = (f32[2,8,4]{1,2,0:T(4,128)S(1)}, f32[2,8,4]{1,2,0:T(4,128)}, u32[]{:S(2)}) copy-start(f32[2,8,4]{1,2,0:T(4,128)} %param.19) | copy-start | bytes 772
  0.7 14.2 %copy-start.8 = (f32[256]{0:T(256)S(1)}, f32[256]{0:T(256)}, u32[]{:S(2)}) copy-start(f32[256]{0:T(256)} %param.23) | copy-start | bytes 3076
  0.7 15.0 %copy-start.2 = (bf16[256,256]{1,0:T(8,128)(2,1)S(1)}, bf16[256,256]{1,0:T(8,128)(2,1)}, u32[]{:S(2)}) copy-start(bf16[256,256]{1,0:T(8,128)(2,1)} %param.22) | copy-start | bytes 393220
  0.7 21.3 %copy-start = (f32[1,8,128,128]{3,2,1,0:T(8,128)S(1)}, f32[1,8,128,128]{3,2,1,0:T(8,128)}, u32[]{:S(2)}) copy-start(f32[1,8,128,128]{3,2,1,0:T(8,128)} %param.16) | copy-start | bytes 1572868
  4.4 17.6 %copy-start.1 = (f32[128,8,128]{2,1,0:T(8,128)S(1)}, f32[128,8,128]{2,1,0:T(8,128)}, u32[]{:S(2)}) copy-start(f32[128,8,128]{2,1,0:T(8,128)} %get-tuple-element.20.state) | copy-start | bytes 1572868
  4.4 17.6 %all-to-all-start = ((bf16[32,32,128]{2,1,0:T(8,128)(2,1)}), bf16[32,32,128]{2,1,0:T(8,128)(2,1)S(1)}, u32[]{:S(2)}, u32[]{:S(2)}) async-start(bf16[32,32,128]{2,1,0:T(8,128)(2,1)} %get-tuple-element.21), calls=%async_computation | async-start | bytes 524288 | tf_op jit(solution)/shard_map/all_to_all | solution.py:736
  12.0 10.0 %copy-start.3 = (bf16[16,256]{1,0:T(8,128)(2,1)}, bf16[16,256]{1,0:T(8,128)(2,1)S(1)}, u32[]{:S(2)}) copy-start(bf16[16,256]{1,0:T(8,128)(2,1)S(1)} %maximum_select_fusion.refs_11_) | copy-start | bytes 24580
  59.9 13.1 %all-to-all-start.2 = ((bf16[32,24,128]{2,1,0:T(8,128)(2,1)}), bf16[32,24,128]{2,1,0:T(8,128)(2,1)S(1)}, u32[]{:S(2)}, u32[]{:S(2)}) async-start(bf16[32,24,128]{2,1,0:T(8,128)(2,1)} %sum.1), calls=%async_computation.2 | async-start | bytes 393216 | tf_op jit(solution)/shard_map/all_to_all | solution.py:837
